TPU v7x, 256 devices: a whole 4x4x8 slice. The times are simulated.
256 devices in a mesh: batch: 32 (over z_lo, x, y), strip: 8 (over z_hi, core).
Axes of the slice: x: 4, y: 4, z: 8 (z_hi: 4, z_lo: 2; z = z_hi * 2 + z_lo), core: 2. Of those that a mesh axis runs over, the one named last changes fastest.
Arguments:
- state_maps: bfloat16 [32, 128, 64, 256], P('batch', 'strip'), may hold values from -6 to 6
- goal_maps: bfloat16 [32, 128, 64, 256], P('batch', 'strip'), may hold values from -6 to 6
- conv_one: bfloat16 [3, 3, 256, 256], replicated, may hold values from -0.125 to 0.125
- conv_two: bfloat16 [3, 3, 256, 256], replicated, may hold values from -0.125 to 0.125
- state_proj: bfloat16 [256, 1024], replicated, may hold values from -0.375 to 0.375
- goal_proj: bfloat16 [256, 1024], replicated, may hold values from -0.375 to 0.375
- inv_temp: float32 [1], replicated, may hold values from 4 to 16
- pair_index: int32 [32], P('batch'), may hold values from 0 to 31, each once
Outputs:
- pair_loss: float32 [32], P('batch')
- grad_state_proj: float32 [256, 1024], replicated
- grad_goal_proj: float32 [256, 1024], replicated
- block_maps: float32 [2, 32, 128, 64, 256], P(None, 'batch', 'strip')
Inputs may be any that keep to these rules, and one draw needn't show every extreme that they name: pair_index names each goal of 0 to 31 exactly once.
All inputs are finite; a program needn't handle non-finite values.
Results may differ from a plain program's by a relative error of at most 0.017.
Values may be sent and summed in bfloat16 or wider, within the bound.
No kernel may reach another device: no remote copies, remote signals or barrier semaphores. Data moves between devices by JAX's collectives and lax.ppermute only.
A program may use at most 64 MiB of HBM per device.

v0:
```python
import jax
import jax.numpy as jnp
from jax import lax
from jax.sharding import PartitionSpec as P


def extended(cells, sides, width):
    for axis, dim in sides:
        count = lax.axis_size(axis)
        ends = count - 1
        head = lax.slice_in_dim(cells, 0, width, axis=dim)
        tail = lax.slice_in_dim(cells, cells.shape[dim] - width, cells.shape[dim], axis=dim)
        cells = jnp.concatenate(
            [
                lax.ppermute(tail, axis, [(i, (i + 1) % count) for i in range(ends)]),
                cells,
                lax.ppermute(head, axis, [((i + 1) % count, i) for i in range(ends)]),
            ],
            axis=dim,
        )
    return cells


def from_everyone(x, axis):
    copies = jnp.broadcast_to(x, (lax.axis_size(axis), *x.shape))
    return lax.all_to_all(copies, axis, split_axis=0, concat_axis=0, tiled=True)


def of_everyone(x, axis):
    return from_everyone(x, axis).sum(axis=0)


def laid_out(blocks, dim):
    lengths = list(blocks.shape[1:])
    lengths[dim] *= blocks.shape[0]
    return jnp.moveaxis(blocks, 0, dim).reshape(lengths)


def gathered_copies(x, axis, dim):
    blocks = from_everyone(x, axis)
    return laid_out(blocks, dim)


def split_up(x, dim, size):
    before, after = (x.shape[:dim], x.shape[dim + 1 :])
    return jnp.moveaxis(x.reshape(*before, size, -1, *after), dim, 0)


def summed_on_arrival(x, axis, dim):
    size = lax.axis_size(axis)
    blocks = lax.all_to_all(split_up(x, dim, size), axis, 0, 0, tiled=True)
    return jnp.sum(blocks, axis=0)


def conv_rows(padded, kernel):
    return lax.conv_general_dilated(
        padded,
        kernel,
        (1, 1),
        ((0, 0), (1, 1)),
        dimension_numbers=("NHWC", "HWIO", "NHWC"),
        preferred_element_type=jnp.float32,
    )


def normalize(embedding):
    inverse_norm = lax.rsqrt(jnp.sum(embedding * embedding, axis=-1, keepdims=True) + 1e-06)
    return (embedding * inverse_norm, inverse_norm)


def shards(state_maps, goal_maps, conv_one, conv_two, state_proj, goal_proj, inv_temp, pair_index):
    local_pairs = state_maps.shape[0]
    strip_rows = state_maps.shape[1]
    columns = state_maps.shape[2]
    channels = state_maps.shape[3]
    frames = jnp.concatenate([state_maps, goal_maps], axis=0)
    active = jnp.maximum(frames, 0)
    padded = extended(active, (("strip", 1),), 1)
    first_out = jnp.maximum(conv_rows(padded, conv_one), 0.0).astype(jnp.bfloat16)
    padded_two = extended(first_out, (("strip", 1),), 1)
    block_out = jnp.maximum(frames.astype(jnp.float32) + conv_rows(padded_two, conv_two), 0.0)
    block_maps = block_out.reshape((2, local_pairs, strip_rows, columns, channels))
    total_cells = strip_rows * lax.axis_size("strip") * columns
    partial_value = jnp.sum(block_out, axis=(1, 2)) / total_cells
    pooled = of_everyone(partial_value, "strip")
    pooled_bf = pooled.astype(jnp.bfloat16)
    state_pool = pooled_bf[0:1]
    goal_pool = pooled_bf[1:2]
    state_emb = jnp.dot(state_pool, state_proj, preferred_element_type=jnp.float32)
    goal_emb = jnp.dot(goal_pool, goal_proj, preferred_element_type=jnp.float32)
    state_unit, state_inverse = normalize(state_emb)
    goal_unit, goal_inverse = normalize(goal_emb)
    state_bf = state_unit.astype(jnp.bfloat16)
    goal_bf = goal_unit.astype(jnp.bfloat16)
    goals_all = gathered_copies(goal_bf, "batch", 0)
    sharpness = inv_temp[0]
    logits = sharpness * jnp.einsum(
        "ie,je->ij", state_bf, goals_all, preferred_element_type=jnp.float32
    )
    exp_logits = jnp.exp(logits)
    row_total = jnp.sum(exp_logits, axis=1)
    matched = jnp.arange(goals_all.shape[0], dtype=jnp.int32)[None, :] == pair_index[:, None]
    positive = jnp.sum(jnp.where(matched, logits, 0.0), axis=1)
    pair_loss = jnp.log(row_total) - positive
    logit_grad = (exp_logits / row_total[:, None] - matched.astype(jnp.float32)).astype(
        jnp.bfloat16
    )
    state_unit_grad = sharpness * jnp.dot(logit_grad, goals_all, preferred_element_type=jnp.float32)
    picked = lax.slice_in_dim(logit_grad, 0, 1 * lax.axis_size("batch"), axis=1)
    goal_unit_grad = summed_on_arrival(
        sharpness * jnp.einsum("ij,ie->je", picked, state_bf, preferred_element_type=jnp.float32),
        "batch",
        0,
    )
    state_emb_grad = (
        state_unit_grad - state_unit * jnp.sum(state_unit * state_unit_grad, axis=-1, keepdims=True)
    ) * state_inverse
    goal_emb_grad = (
        goal_unit_grad - goal_unit * jnp.sum(goal_unit * goal_unit_grad, axis=-1, keepdims=True)
    ) * goal_inverse
    emb_grad_bf = jnp.stack([state_emb_grad, goal_emb_grad], axis=0).astype(jnp.bfloat16)
    pool_pair = jnp.stack([state_pool, goal_pool], axis=0)
    empty = jnp.zeros((channels, state_proj.shape[1]), jnp.float32)
    pool_piece = gathered_copies(pool_pair, "batch", 1)
    grad_piece = gathered_copies(emb_grad_bf, "batch", 1)
    state_sum = empty + jnp.einsum(
        "ic,ie->ce", pool_piece[0], grad_piece[0], preferred_element_type=jnp.float32
    )
    goal_sum = empty + jnp.einsum(
        "ic,ie->ce", pool_piece[1], grad_piece[1], preferred_element_type=jnp.float32
    )
    return (pair_loss, state_sum, goal_sum, block_maps)


def solution(mesh):
    placed = (
        P("batch", "strip", None, None),
        P("batch", "strip", None, None),
        P(),
        P(),
        P(),
        P(),
        P(),
        P("batch"),
    )
    return jax.shard_map(
        shards,
        mesh=mesh,
        in_specs=placed,
        out_specs=(P("batch"), P(), P(), P(None, "batch", "strip", None, None)),
        check_vma=False,
    )
```

profile of v0, /device:TPU:2, one launch (start us, length us, event | category | flops | bytes accessed | tf_op | source)
XLA Modules:
  0.0 130.4 jit_solution(2339476350111107983)
XLA Ops:
  0.6 1.4 %copy_dynamic-update-slice_fusion.1 = bf16[2,16,64,256]{3,1,2,0:T(8,128)(2,1)S(1)} fusion(bf16[1,16,64,256]{3,2,1,0:T(8,128)(2,1)} %param.8), kind=kLoop, calls=%fused_computation.24 | loop fusion | bytes 1048576
  2.1 1.3 %copy_dynamic-update-slice_fusion = bf16[2,16,64,256]{3,1,2,0:T(8,128)(2,1)S(1)} fusion(bf16[2,16,64,256]{3,1,2,0:T(8,128)(2,1)S(1)} %copy_dynamic-update-slice_fusion.1, bf16[1,16,64,256]{3,2,1,0:T(8,128)(2,1)} %param.9), kind=kLoop, calls=%fused_computation.23 | loop fusion | bytes 1048576 | tf_op jit(solution)/shard_map/concatenate | solution.py:76
  4.7 1.7 %collective-permute-start = (bf16[2,1,64,256]{3,1,2,0:T(2,128)(2,1)S(1)}, bf16[2,1,64,256]{3,1,2,0:T(2,128)(2,1)S(1)}, u32[]{:S(2)}, u32[]{:S(2)}) collective-permute-start(bf16[2,1,64,256]{3,1,2,0:T(2,128)(2,1)S(1)} %get-tuple-element.38), channel_id=1, source_target_pairs={{0,1},{1,2},{2,3},{3,4},{4,5},{5,6},{6,7},{8,9},{9,10},{10,11},{11... | collective-permute-start | bytes 196616 | tf_op jit(solution)/shard_map/ppermute | solution.py:15
  6.4 1.3 collective-permute-start.1
  7.7 5.0 %collective-permute-done.1 = bf16[2,1,64,256]{3,1,2,0:T(2,128)(2,1)S(1)} collective-permute-done((bf16[2,1,64,256]{3,1,2,0:T(2,128)(2,1)S(1)}, bf16[2,1,64,256]{3,1,2,0:T(2,128)(2,1)S(1)}, u32[]{:S(2)}, u32[]{:S(2)}) %collective-permute-start.1) | collective-permute-done | bytes 65568 | tf_op jit(solution)/shard_map/ppermute | solution.py:17
  12.7 1.0 maximum_bitcast_fusion
  13.8 1.2 copy.102
  16.2 1.5 %fusion.4 = bf16[18,2,8,11,256]{4,1,3,2,0:T(2,128)(2,1)S(1)} fusion(bf16[18,2,7,2,256]{4,1,3,2,0:T(2,128)(2,1)S(1)} %slice.54, bf16[18,2,8,9,256]{4,1,3,2,0:T(2,128)(2,1)S(1)} %bitcast.101), kind=kLoop, calls=%fused_computation.7 | loop fusion | flops 4866048 | bytes 3207168 | tf_op jit(solution)/shard_map/conv_general_dilated | solution.py:56
  17.7 2.9 %maximum_convert_fusion = bf16[16,16,9,256]{3,1,2,0:T(8,128)(2,1)S(1)} fusion(bf16[3,3,256,256]{3,2,1,0:T(8,128)(2,1)S(1)} %copy-done, bf16[18,2,8,11,256]{4,1,3,2,0:T(2,128)(2,1)S(1)} %fusion.4, pred[16,9]{0,1:T(8,128)(4,1)S(1)} %copy-done.4), kind=kOutput, calls=%fused_computation.3 | convolution fusion | flops 2719678464 | bytes 3981456 | tf_op jit(solution)/shard_map/conv_general_dilated | solution.py:56
  21.2 6.4 %collective-permute-start.2 = (bf16[2,1,64,256]{3,2,0,1:T(8,128)(2,1)S(1)}, bf16[2,1,64,256]{3,2,0,1:T(8,128)(2,1)S(1)}, u32[]{:S(2)}, u32[]{:S(2)}) collective-permute-start(bf16[2,1,64,256]{3,2,0,1:T(8,128)(2,1)S(1)} %slice_bitcast_fusion.7), channel_id=1, source_target_pairs={{0,1},{1,2},{2,3},{3,4},{4,5},{5,6},{6,7},{8,9},{9,10},{10,11},{11... | collective-permute-start | bytes 196616 | tf_op jit(solution)/shard_map/ppermute | solution.py:15
  27.8 1.5 %collective-permute-start.3 = (bf16[2,1,64,256]{3,1,2,0:T(2,128)(2,1)S(1)}, bf16[2,1,64,256]{3,1,2,0:T(2,128)(2,1)S(1)}, u32[]{:S(2)}, u32[]{:S(2)}) collective-permute-start(bf16[2,1,64,256]{3,1,2,0:T(2,128)(2,1)S(1)} %copy.91), channel_id=1, source_target_pairs={{1,0},{2,1},{3,2},{4,3},{5,4},{6,5},{7,6},{9,8},{10,9},{11,10},{12... | collective-permute-start | bytes 196616 | tf_op jit(solution)/shard_map/ppermute | solution.py:17
  29.4 1.6 %collective-permute-done.3 = bf16[2,1,64,256]{3,1,2,0:T(2,128)(2,1)S(1)} collective-permute-done((bf16[2,1,64,256]{3,1,2,0:T(2,128)(2,1)S(1)}, bf16[2,1,64,256]{3,1,2,0:T(2,128)(2,1)S(1)}, u32[]{:S(2)}, u32[]{:S(2)}) %collective-permute-start.3) | collective-permute-done | bytes 65568 | tf_op jit(solution)/shard_map/ppermute | solution.py:17
  31.0 1.0 maximum_bitcast_fusion.1
  32.0 1.2 copy.103
  34.5 1.5 %fusion.5 = bf16[18,2,8,11,256]{4,1,3,2,0:T(2,128)(2,1)S(1)} fusion(bf16[18,2,7,2,256]{4,1,3,2,0:T(2,128)(2,1)S(1)} %slice.60, bf16[18,2,8,9,256]{4,1,3,2,0:T(2,128)(2,1)S(1)} %bitcast.99), kind=kLoop, calls=%fused_computation.8 | loop fusion | flops 4866048 | bytes 3207168 | tf_op jit(solution)/shard_map/conv_general_dilated | solution.py:56
  36.0 3.1 %fusion.12 = f32[16,16,9,256]{3,1,2,0:T(8,128)S(1)} fusion(bf16[3,3,256,256]{3,2,1,0:T(8,128)(2,1)S(1)} %copy-done.3, bf16[18,2,8,11,256]{4,1,3,2,0:T(2,128)(2,1)S(1)} %fusion.5, pred[16,9]{0,1:T(8,128)(4,1)S(1)} %copy-done.4), kind=kOutput, calls=%fused_computation.17 | convolution fusion | flops 2718498816 | bytes 5161104 | tf_op jit(solution)/shard_map/conv_general_dilated | solution.py:56
  39.1 1.4 %copy.95 = f32[16,16,9,256]{3,0,2,1:T(8,128)S(1)} copy(f32[16,16,9,256]{3,1,2,0:T(8,128)S(1)} %fusion.12) | data formatting | bytes 4718592 | tf_op jit(solution)/shard_map/conv_general_dilated | solution.py:56
  41.5 14.5 %all-to-all-start = ((f32[8,2,256]{2,1,0:T(2,128)}), f32[8,2,256]{2,1,0:T(2,128)S(1)}, u32[]{:S(2)}, u32[]{:S(2)}) async-start(f32[8,2,256]{2,1,0:T(2,128)} %broadcast_in_dim.12), calls=%async_computation | async-start | bytes 32768 | tf_op jit(solution)/shard_map/all_to_all | solution.py:26
  57.3 6.5 %all-to-all-done = f32[8,2,256]{2,1,0:T(2,128)S(1)} async-done(((f32[8,2,256]{2,1,0:T(2,128)}), f32[8,2,256]{2,1,0:T(2,128)S(1)}, u32[]{:S(2)}, u32[]{:S(2)}) %all-to-all-start) | async-done | bytes 16416 | tf_op jit(solution)/shard_map/all_to_all | solution.py:26
  63.8 1.2 fusion.27
  66.3 1.2 fusion.29
  71.1 7.6 %all-to-all-start.1 = ((bf16[32,2,512]{2,1,0:T(2,128)(2,1)}), bf16[32,2,512]{2,1,0:T(2,128)(2,1)S(1)}, u32[]{:S(2)}, u32[]{:S(2)}) async-start(bf16[32,2,512]{2,1,0:T(2,128)(2,1)} %reshape.175), calls=%async_computation.1 | async-start | bytes 131072 | tf_op jit(solution)/shard_map/all_to_all | solution.py:26
  78.8 7.1 %all-to-all-done.1 = bf16[32,2,512]{2,1,0:T(2,128)(2,1)S(1)} async-done(((bf16[32,2,512]{2,1,0:T(2,128)(2,1)}), bf16[32,2,512]{2,1,0:T(2,128)(2,1)S(1)}, u32[]{:S(2)}, u32[]{:S(2)}) %all-to-all-start.1) | async-done | bytes 65568 | tf_op jit(solution)/shard_map/all_to_all | solution.py:26
  88.3 5.0 %all-to-all-start.3 = ((f32[32,1,1024]{2,1,0:T(1,128)}), f32[32,1,1024]{2,1,0:T(1,128)S(1)}, u32[]{:S(2)}, u32[]{:S(2)}) async-start(f32[32,1,1024]{2,1,0:T(1,128)} %reshape.135), calls=%async_computation.3 | async-start | bytes 262144 | tf_op jit(solution)/shard_map/all_to_all | solution.py:51
  94.6 6.1 %all-to-all-done.3 = f32[32,1,1024]{2,1,0:T(1,128)S(1)} async-done(((f32[32,1,1024]{2,1,0:T(1,128)}), f32[32,1,1024]{2,1,0:T(1,128)S(1)}, u32[]{:S(2)}, u32[]{:S(2)}) %all-to-all-start.3) | async-done | bytes 131104 | tf_op jit(solution)/shard_map/all_to_all | solution.py:51
  101.3 5.0 %all-to-all-start.2 = ((bf16[32,2,1,256]{3,1,2,0:T(2,128)(2,1)}), bf16[32,2,1,256]{3,1,2,0:T(2,128)(2,1)S(1)}, u32[]{:S(2)}, u32[]{:S(2)}) async-start(bf16[32,2,1,256]{3,1,2,0:T(2,128)(2,1)} %broadcast_in_dim.26), calls=%async_computation.2 | async-start | bytes 65536 | tf_op jit(solution)/shard_map/all_to_all | solution.py:26
  107.7 5.8 %all-to-all-done.2 = bf16[32,2,1,256]{3,1,2,0:T(2,128)(2,1)S(1)} async-done(((bf16[32,2,1,256]{3,1,2,0:T(2,128)(2,1)}), bf16[32,2,1,256]{3,1,2,0:T(2,128)(2,1)S(1)}, u32[]{:S(2)}, u32[]{:S(2)}) %all-to-all-start.2) | async-done | bytes 32800 | tf_op jit(solution)/shard_map/all_to_all | solution.py:26
  114.2 5.0 %all-to-all-start.4 = ((bf16[32,2,1,1024]{3,1,2,0:T(2,128)(2,1)}), bf16[32,2,1,1024]{3,1,2,0:T(2,128)(2,1)S(1)}, u32[]{:S(2)}, u32[]{:S(2)}) async-start(bf16[32,2,1,1024]{3,1,2,0:T(2,128)(2,1)} %broadcast_in_dim.27), calls=%async_computation.4 | async-start | bytes 262144 | tf_op jit(solution)/shard_map/all_to_all | solution.py:26
  119.2 2.5 %copy.99 = f32[2,1,16,64,256]{4,3,2,1,0:T(8,128)} copy(f32[2,1,16,64,256]{4,2,3,0,1:T(8,128)S(1)} %get-tuple-element.34) | data formatting | bytes 4194304
  123.0 3.6 %all-to-all-done.4 = bf16[32,2,1,1024]{3,1,2,0:T(2,128)(2,1)S(1)} async-done(((bf16[32,2,1,1024]{3,1,2,0:T(2,128)(2,1)}), bf16[32,2,1,1024]{3,1,2,0:T(2,128)(2,1)S(1)}, u32[]{:S(2)}, u32[]{:S(2)}) %all-to-all-start.4) | async-done | bytes 131104 | tf_op jit(solution)/shard_map/all_to_all | solution.py:26
  126.7 1.3 fusion.20
  127.9 1.3 fusion.21
  (62 shorter events, 15.4 us)
Async XLA Ops:
  0.6 17.1 %copy-start = (bf16[3,3,256,256]{3,2,1,0:T(8,128)(2,1)S(1)}, bf16[3,3,256,256]{3,2,1,0:T(8,128)(2,1)}, u32[]{:S(2)}) copy-start(bf16[3,3,256,256]{3,2,1,0:T(8,128)(2,1)} %param.10) | copy-start | bytes 3538948
  3.4 1.0 copy-start.1
  4.7 3.1 %collective-permute-start = (bf16[2,1,64,256]{3,1,2,0:T(2,128)(2,1)S(1)}, bf16[2,1,64,256]{3,1,2,0:T(2,128)(2,1)S(1)}, u32[]{:S(2)}, u32[]{:S(2)}) collective-permute-start(bf16[2,1,64,256]{3,1,2,0:T(2,128)(2,1)S(1)} %get-tuple-element.38), channel_id=1, source_target_pairs={{0,1},{1,2},{2,3},{3,4},{4,5},{5,6},{6,7},{8,9},{9,10},{10,11},{11... | collective-permute-start | bytes 196616 | tf_op jit(solution)/shard_map/ppermute | solution.py:15
  6.4 6.3 %collective-permute-start.1 = (bf16[2,1,64,256]{3,1,2,0:T(2,128)(2,1)S(1)}, bf16[2,1,64,256]{3,1,2,0:T(2,128)(2,1)S(1)}, u32[]{:S(2)}, u32[]{:S(2)}) collective-permute-start(bf16[2,1,64,256]{3,1,2,0:T(2,128)(2,1)S(1)} %get-tuple-element.39), channel_id=1, source_target_pairs={{1,0},{2,1},{3,2},{4,3},{5,4},{6,5},{7,6},{9,8},{10,9},{11,10},{12... | collective-permute-start | bytes 196616 | tf_op jit(solution)/shard_map/ppermute | solution.py:17
  16.2 1.5 %copy-start.4 = (pred[16,9]{0,1:T(8,128)(4,1)S(1)}, pred[16,9]{0,1:T(8,128)(4,1)}, u32[]{:S(2)}) copy-start(pred[16,9]{0,1:T(8,128)(4,1)} %constant.23) | copy-start | bytes 436
  21.2 8.1 %collective-permute-start.2 = (bf16[2,1,64,256]{3,2,0,1:T(8,128)(2,1)S(1)}, bf16[2,1,64,256]{3,2,0,1:T(8,128)(2,1)S(1)}, u32[]{:S(2)}, u32[]{:S(2)}) collective-permute-start(bf16[2,1,64,256]{3,2,0,1:T(8,128)(2,1)S(1)} %slice_bitcast_fusion.7), channel_id=1, source_target_pairs={{0,1},{1,2},{2,3},{3,4},{4,5},{5,6},{6,7},{8,9},{9,10},{10,11},{11... | collective-permute-start | bytes 196616 | tf_op jit(solution)/shard_map/ppermute | solution.py:15
  27.8 3.2 %collective-permute-start.3 = (bf16[2,1,64,256]{3,1,2,0:T(2,128)(2,1)S(1)}, bf16[2,1,64,256]{3,1,2,0:T(2,128)(2,1)S(1)}, u32[]{:S(2)}, u32[]{:S(2)}) collective-permute-start(bf16[2,1,64,256]{3,1,2,0:T(2,128)(2,1)S(1)} %copy.91), channel_id=1, source_target_pairs={{1,0},{2,1},{3,2},{4,3},{5,4},{6,5},{7,6},{9,8},{10,9},{11,10},{12... | collective-permute-start | bytes 196616 | tf_op jit(solution)/shard_map/ppermute | solution.py:17
  34.4 1.5 %copy-start.3 = (bf16[3,3,256,256]{3,2,1,0:T(8,128)(2,1)S(1)}, bf16[3,3,256,256]{3,2,1,0:T(8,128)(2,1)}, u32[]{:S(2)}) copy-start(bf16[3,3,256,256]{3,2,1,0:T(8,128)(2,1)} %param.11) | copy-start | bytes 3538948
  39.1 1.4 %copy-start.2 = (bf16[2,16,64,256]{3,1,2,0:T(8,128)(2,1)S(1)}, bf16[2,16,64,256]{3,1,2,0:T(8,128)(2,1)}, u32[]{:S(2)}) copy-start(bf16[2,16,64,256]{3,1,2,0:T(8,128)(2,1)} %copy-done.1) | copy-start | bytes 3145732
  41.5 22.3 %all-to-all-start = ((f32[8,2,256]{2,1,0:T(2,128)}), f32[8,2,256]{2,1,0:T(2,128)S(1)}, u32[]{:S(2)}, u32[]{:S(2)}) async-start(f32[8,2,256]{2,1,0:T(2,128)} %broadcast_in_dim.12), calls=%async_computation | async-start | bytes 32768 | tf_op jit(solution)/shard_map/all_to_all | solution.py:26
  71.1 14.8 %all-to-all-start.1 = ((bf16[32,2,512]{2,1,0:T(2,128)(2,1)}), bf16[32,2,512]{2,1,0:T(2,128)(2,1)S(1)}, u32[]{:S(2)}, u32[]{:S(2)}) async-start(bf16[32,2,512]{2,1,0:T(2,128)(2,1)} %reshape.175), calls=%async_computation.1 | async-start | bytes 131072 | tf_op jit(solution)/shard_map/all_to_all | solution.py:26
  88.3 12.4 %all-to-all-start.3 = ((f32[32,1,1024]{2,1,0:T(1,128)}), f32[32,1,1024]{2,1,0:T(1,128)S(1)}, u32[]{:S(2)}, u32[]{:S(2)}) async-start(f32[32,1,1024]{2,1,0:T(1,128)} %reshape.135), calls=%async_computation.3 | async-start | bytes 262144 | tf_op jit(solution)/shard_map/all_to_all | solution.py:51
  101.3 12.2 %all-to-all-start.2 = ((bf16[32,2,1,256]{3,1,2,0:T(2,128)(2,1)}), bf16[32,2,1,256]{3,1,2,0:T(2,128)(2,1)S(1)}, u32[]{:S(2)}, u32[]{:S(2)}) async-start(bf16[32,2,1,256]{3,1,2,0:T(2,128)(2,1)} %broadcast_in_dim.26), calls=%async_computation.2 | async-start | bytes 65536 | tf_op jit(solution)/shard_map/all_to_all | solution.py:26
  114.2 12.4 %all-to-all-start.4 = ((bf16[32,2,1,1024]{3,1,2,0:T(2,128)(2,1)}), bf16[32,2,1,1024]{3,1,2,0:T(2,128)(2,1)S(1)}, u32[]{:S(2)}, u32[]{:S(2)}) async-start(bf16[32,2,1,1024]{3,1,2,0:T(2,128)(2,1)} %broadcast_in_dim.27), calls=%async_computation.4 | async-start | bytes 262144 | tf_op jit(solution)/shard_map/all_to_all | solution.py:26
where the time goes:
time: 131 us; the launch traced here: 130 us
  starting transfers between devices  48 us (37%)
  waiting for transfers between devices  35.6 us (27%)
  local copies, waits for them, and re-layouts  17.5 us (13%)
  matrix products  12 us (9%)
  other arithmetic  11 us (8%)
  between operations  6.2 us (5%)
    all_to_all x4, starting transfers between devices, from_everyone(): return lax.all_to_all(copies, axis, split_axis=0, concat_axis=0, tiled=True)  32.1 us
    all_to_all x4, waiting for transfers between devices, from_everyone(): return lax.all_to_all(copies, axis, split_axis=0, concat_axis=0, tiled=True)  22.9 us
    ppermute x2, starting transfers between devices, extended(): lax.ppermute(tail, axis, [(i, (i + 1) % count) for i in range(ends)])  8.11 us
    unnamed x16, local copies, waits for them, and re-layouts  8.1 us
    ppermute x2, waiting for transfers between devices, extended(): lax.ppermute(head, axis, [((i + 1) % count, i) for i in range(ends)])  6.55 us
    all_to_all x1, waiting for transfers between devices, summed_on_arrival(): blocks = lax.all_to_all(split_up(x, dim, size), axis, 0, 0, tiled=True)  6.15 us
    conv_general_dilated x2, matrix products, conv_rows(): lax.conv_general_dilated(padded, kernel, (1, 1), ((0, 0), (1, 1)), dimens...  6.02 us
    all_to_all x1, starting transfers between devices, summed_on_arrival(): blocks = lax.all_to_all(split_up(x, dim, size), axis, 0, 0, tiled=True)  4.97 us
  transfers between devices with their start and end apart: 9, of which 7 were waited for; matrix products, arithmetic and copies ran while one was open for 4% of the time, Pallas kernels for 0%

commit v1 on v0

v1 whole, which is shorter than its diff:
```python
import functools
import jax
import jax.numpy as jnp
from jax import lax
from jax.experimental import pallas as pl
from jax.experimental.pallas import tpu as pltpu
from jax.sharding import PartitionSpec as P

ROWS, COLS, C, E = 16, 64, 256, 1024
BF, F32 = jnp.bfloat16, jnp.float32
MIB = 1 << 20


def widen(row):
    col = lax.broadcasted_iota(jnp.int32, row.shape, 0)
    left = jnp.where(col == 0, 0.0, pltpu.roll(row, 1, 0))
    right = jnp.where(col == COLS - 1, 0.0, pltpu.roll(row, COLS - 1, 0))
    return jnp.concatenate([left.astype(BF), row.astype(BF), right.astype(BF)], axis=-1)


def conv(wide, first, rows, weights):
    total = None
    for dy in range(3):
        lhs = wide[pl.ds(first + dy, rows)].reshape(rows * COLS, 3 * C)
        part = jnp.dot(lhs, weights[dy], preferred_element_type=F32)
        total = part if total is None else total + part
    return total


def interior_kernel(step1, step2, s_hbm, g_hbm, w1_hbm, w2_hbm, out_hbm, edge_ref, sum_ref,
                    x, w1, w2, xw, hw, o, sems, osem):
    cx = [pltpu.make_async_copy(ref.at[0], x.at[f], sems.at[f]) for f, ref in enumerate((s_hbm, g_hbm))]
    cw1 = pltpu.make_async_copy(w1_hbm, w1, sems.at[2])
    cw2 = pltpu.make_async_copy(w2_hbm, w2, sems.at[3])
    cx[0].start(); cw1.start(); cx[1].start(); cw2.start()
    outs = []
    for f in range(2):
        cx[f].wait()
        for r in range(ROWS):
            xw[f, r] = widen(jnp.maximum(x[f, r].astype(F32), 0.0))
        if f == 0:
            cw1.wait()
        for r in range(0, 14, step1):
            h = jnp.maximum(conv(xw.at[f], r, step1, w1), 0.0)
            for k in range(step1):
                hw[f, r + k] = widen(h[k * COLS:(k + 1) * COLS])
        if f == 0:
            cw2.wait()
        acc = None
        for r in range(0, 12, step2):
            y = conv(hw.at[f], r, step2, w2)
            y = jnp.maximum(y + x[f, r + 2:r + 2 + step2].reshape(step2 * COLS, C).astype(F32), 0.0)
            o[f, r:r + step2] = y.reshape(step2, COLS, C)
            part = jnp.sum(y.reshape(step2 * COLS // 8, 8, C), axis=0)
            acc = part if acc is None else acc + part
        sum_ref[f] = acc
        for k, r in enumerate((0, 1, 12, 13)):
            edge_ref[2 * f + k // 2, k % 2] = hw[f, r, :, C:2 * C]
        cp = pltpu.make_async_copy(o.at[f], out_hbm.at[f, 0, pl.ds(2, 12)], osem.at[f])
        cp.start()
        outs.append(cp)
    for cp in outs:
        cp.wait()


def interior(s, g, w1, w2, step1=7, step2=6):
    anyspec = pl.BlockSpec(memory_space=pl.ANY)
    vm = pl.BlockSpec(memory_space=pltpu.VMEM)
    return pl.pallas_call(
        functools.partial(interior_kernel, step1, step2),
        name="interior_rows",
        out_shape=(jax.ShapeDtypeStruct((2, 1, ROWS, COLS, C), F32),
                   jax.ShapeDtypeStruct((4, 2, COLS, C), BF),
                   jax.ShapeDtypeStruct((2, 8, C), F32)),
        in_specs=[anyspec] * 4,
        out_specs=(anyspec, vm, vm),
        scratch_shapes=[
            pltpu.VMEM((2, ROWS, COLS, C), BF),
            pltpu.VMEM((3, 3 * C, C), BF),
            pltpu.VMEM((3, 3 * C, C), BF),
            pltpu.VMEM((2, ROWS, COLS, 3 * C), BF),
            pltpu.VMEM((2, 14, COLS, 3 * C), BF),
            pltpu.VMEM((2, 12, COLS, C), F32),
            pltpu.SemaphoreType.DMA((4,)),
            pltpu.SemaphoreType.DMA((2,)),
        ],
        compiler_params=pltpu.CompilerParams(vmem_limit_bytes=40 * MIB),
        cost_estimate=pl.CostEstimate(flops=4_200_000_000, transcendentals=0, bytes_accessed=6_000_000),
    )(s, g, w1, w2)


def edge_kernel(here, s_hbm, g_hbm, above_hbm, below_hbm, hedge, sums, w1_hbm, w2_hbm, out_in, out_hbm, sum_ref,
                xe, w1, w2, xw, hw, o, sems, osem):
    copies = []
    for f, ref in enumerate((s_hbm, g_hbm)):
        copies.append(pltpu.make_async_copy(above_hbm.at[f], xe.at[2 * f, pl.ds(0, 2)], sems.at[len(copies)]))
        copies.append(pltpu.make_async_copy(ref.at[0, pl.ds(0, 2)], xe.at[2 * f, pl.ds(2, 2)], sems.at[len(copies)]))
        copies.append(pltpu.make_async_copy(ref.at[0, pl.ds(14, 2)], xe.at[2 * f + 1, pl.ds(0, 2)], sems.at[len(copies)]))
        copies.append(pltpu.make_async_copy(below_hbm.at[f], xe.at[2 * f + 1, pl.ds(2, 2)], sems.at[len(copies)]))
    cw1 = pltpu.make_async_copy(w1_hbm, w1, sems.at[8])
    cw2 = pltpu.make_async_copy(w2_hbm, w2, sems.at[9])
    for cp in copies:
        cp.start()
    cw1.start(); cw2.start()
    for cp in copies:
        cp.wait()
    for k in range(4):
        for r in range(4):
            xw[r, k] = widen(jnp.maximum(xe[k, r].astype(F32), 0.0))
    for k in range(4):
        for r in range(2):
            hw[r + 2 * (1 - k % 2), k] = widen(hedge[k, r].astype(F32))
    cw1.wait()

    def conv4(wide, weights):
        total = None
        for dy in range(3):
            lhs = wide[pl.ds(dy, 2)].reshape(2 * 4 * COLS, 3 * C)
            part = jnp.dot(lhs, weights[dy], preferred_element_type=F32)
            total = part if total is None else total + part
        return total

    h = jnp.maximum(conv4(xw, w1), 0.0)
    for r in range(2):
        for k in range(4):
            row = h[(r * 4 + k) * COLS:(r * 4 + k + 1) * COLS]
            if k % 2 == 0 and r == 0:
                row = jnp.where(here[0] > 0, row, 0.0)
            if k % 2 == 1 and r == 1:
                row = jnp.where(here[0] < here[1] - 1, row, 0.0)
            hw[r + 2 * (k % 2), k] = widen(row)
    cw2.wait()
    y = conv4(hw, w2)
    tot = [sums[0], sums[1]]
    outs = []
    for k in range(4):
        f = k // 2
        for r in range(2):
            v = y[(r * 4 + k) * COLS:(r * 4 + k + 1) * COLS] + xe[k, r + 2 * (1 - k % 2)].astype(F32)
            v = jnp.maximum(v, 0.0)
            o[k, r] = v
            tot[f] = tot[f] + jnp.sum(v.reshape(8, 8, C), axis=0)
        cp = pltpu.make_async_copy(o.at[k], out_hbm.at[f, 0, pl.ds(14 * (k % 2), 2)], osem.at[k])
        cp.start()
        outs.append(cp)
    for f in range(2):
        sum_ref[f:f + 1] = jnp.sum(tot[f], axis=0, keepdims=True)
    for cp in outs:
        cp.wait()


def edges(here, s, g, above, below, hedge, sums, w1, w2, out):
    anyspec = pl.BlockSpec(memory_space=pl.ANY)
    vm = pl.BlockSpec(memory_space=pltpu.VMEM)
    return pl.pallas_call(
        edge_kernel,
        name="edge_rows",
        out_shape=(jax.ShapeDtypeStruct(out.shape, F32), jax.ShapeDtypeStruct((2, C), F32)),
        in_specs=[pl.BlockSpec(memory_space=pltpu.SMEM)] + [anyspec] * 4 + [vm] * 2 + [anyspec] * 3,
        out_specs=(anyspec, vm),
        input_output_aliases={9: 0},
        scratch_shapes=[
            pltpu.VMEM((4, 4, COLS, C), BF),
            pltpu.VMEM((3, 3 * C, C), BF),
            pltpu.VMEM((3, 3 * C, C), BF),
            pltpu.VMEM((4, 4, COLS, 3 * C), BF),
            pltpu.VMEM((4, 4, COLS, 3 * C), BF),
            pltpu.VMEM((4, 2, COLS, C), F32),
            pltpu.SemaphoreType.DMA((10,)),
            pltpu.SemaphoreType.DMA((4,)),
        ],
        compiler_params=pltpu.CompilerParams(vmem_limit_bytes=24 * MIB),
        cost_estimate=pl.CostEstimate(flops=1_200_000_000, transcendentals=0, bytes_accessed=4_000_000),
    )(here, s, g, above, below, hedge, sums, w1, w2, out)
def head_kernel(mine, sharp, tot, sproj, gproj, loss_ref, gs_hbm, gg_hbm, buf, sem):
    pairs = tot.shape[1]
    s_pool = tot[0, :, :C].astype(BF)
    g_pool = tot[1, :, :C].astype(BF)
    label = tot[0, :, C:C + 1]
    temp = sharp[0]
    s_emb = jnp.dot(s_pool, sproj[...], preferred_element_type=F32)
    g_emb = jnp.dot(g_pool, gproj[...], preferred_element_type=F32)
    s_inv = lax.rsqrt(jnp.sum(s_emb * s_emb, axis=-1, keepdims=True) + 1e-06)
    g_inv = lax.rsqrt(jnp.sum(g_emb * g_emb, axis=-1, keepdims=True) + 1e-06)
    s_unit = s_emb * s_inv
    g_unit = g_emb * g_inv
    s_bf = s_unit.astype(BF)
    g_bf = g_unit.astype(BF)
    logits = temp * lax.dot_general(s_bf, g_bf, (((1,), (1,)), ((), ())), preferred_element_type=F32)
    ex = jnp.exp(logits)
    row_total = jnp.sum(ex, axis=1, keepdims=True)
    column = lax.broadcasted_iota(jnp.int32, (pairs, pairs), 1).astype(F32)
    matched = column == label
    positive = jnp.sum(jnp.where(matched, logits, 0.0), axis=1, keepdims=True)
    losses = jnp.log(row_total) - positive
    row = lax.broadcasted_iota(jnp.int32, (pairs, 1), 0)
    loss_ref[0] = jnp.sum(jnp.where(row == mine[0], losses, 0.0))
    lgrad = (ex / row_total - jnp.where(matched, 1.0, 0.0)).astype(BF)
    s_ug = temp * jnp.dot(lgrad, g_bf, preferred_element_type=F32)
    g_ug = temp * lax.dot_general(lgrad, s_bf, (((0,), (0,)), ((), ())), preferred_element_type=F32)
    s_eg = ((s_ug - s_unit * jnp.sum(s_unit * s_ug, axis=-1, keepdims=True)) * s_inv).astype(BF)
    g_eg = ((g_ug - g_unit * jnp.sum(g_unit * g_ug, axis=-1, keepdims=True)) * g_inv).astype(BF)
    outs = []
    for k, (pool, grad, dest) in enumerate(((s_pool, s_eg, gs_hbm), (g_pool, g_eg, gg_hbm))):
        buf[k] = lax.dot_general(pool, grad, (((0,), (0,)), ((), ())), preferred_element_type=F32)
        cp = pltpu.make_async_copy(buf.at[k], dest, sem.at[k])
        cp.start()
        outs.append(cp)
    for cp in outs:
        cp.wait()


def head(mine, sharp, tot, sproj, gproj):
    anyspec = pl.BlockSpec(memory_space=pl.ANY)
    vm = pl.BlockSpec(memory_space=pltpu.VMEM)
    sm = pl.BlockSpec(memory_space=pltpu.SMEM)
    return pl.pallas_call(
        head_kernel,
        name="contrastive_head",
        out_shape=(jax.ShapeDtypeStruct((1,), F32), jax.ShapeDtypeStruct((C, E), F32),
                   jax.ShapeDtypeStruct((C, E), F32)),
        in_specs=[sm, sm, vm, vm, vm],
        out_specs=(sm, anyspec, anyspec),
        scratch_shapes=[pltpu.VMEM((2, C, E), F32), pltpu.SemaphoreType.DMA((2,))],
        compiler_params=pltpu.CompilerParams(vmem_limit_bytes=16 * MIB),
    )(mine, sharp, tot, sproj, gproj)


def shards(state_maps, goal_maps, conv_one, conv_two, state_proj, goal_proj, inv_temp, pair_index):
    strips, batch = lax.axis_size("strip"), lax.axis_size("batch")
    here = lax.axis_index("strip").astype(jnp.int32)
    mine = lax.axis_index("batch").astype(jnp.int32)
    w1 = conv_one.reshape(3, 3 * C, C)
    w2 = conv_two.reshape(3, 3 * C, C)
    down = [(i, i + 1) for i in range(strips - 1)]
    up = [(i + 1, i) for i in range(strips - 1)]
    tails = jnp.concatenate([state_maps[:, ROWS - 2:], goal_maps[:, ROWS - 2:]], axis=0)
    heads = jnp.concatenate([state_maps[:, :2], goal_maps[:, :2]], axis=0)
    above = lax.ppermute(tails, "strip", down)
    below = lax.ppermute(heads, "strip", up)
    out, hedge, sums = interior(state_maps, goal_maps, w1, w2)
    place = jnp.stack([here, jnp.full((), strips, jnp.int32)])
    out, total = edges(place, state_maps, goal_maps, above, below, hedge, sums, w1, w2, out)
    label = jnp.full((2, 128), pair_index[0].astype(F32))
    share = jnp.concatenate([total * (1.0 / (strips * ROWS * COLS)), label], axis=1)
    pair_groups = [[2 * i, 2 * i + 1] for i in range(strips // 2)]
    share = lax.psum(share, "strip", axis_index_groups=pair_groups).astype(BF)
    groups = [[b * strips + s for b in range(batch) for s in range(core, strips, 2)] for core in range(2)]
    members = batch * strips // 2
    copies = jnp.broadcast_to(share, (members, *share.shape))
    got = lax.all_to_all(copies, ("batch", "strip"), 0, 0, tiled=True, axis_index_groups=groups)
    got = got.reshape(batch, strips // 2, 2, C + 128).astype(F32)
    tot = jnp.moveaxis(jnp.sum(got, axis=1), 1, 0)
    tot = tot * jnp.where(jnp.arange(C + 128) < C, 1.0, 1.0 / strips)
    loss, gs, gg = head(mine.reshape(1), inv_temp, tot, state_proj, goal_proj)
    return (loss, gs, gg, out)


def solution(mesh):
    placed = (
        P("batch", "strip", None, None),
        P("batch", "strip", None, None),
        P(),
        P(),
        P(),
        P(),
        P(),
        P("batch"),
    )
    return jax.shard_map(
        shards,
        mesh=mesh,
        in_specs=placed,
        out_specs=(P("batch"), P(), P(), P(None, "batch", "strip", None, None)),
        check_vma=False,
    )
```

time: 131 us -> 65.5 us (0.50)
  the two profiles are of different devices: /device:TPU:2 before, /device:TPU:1 now
where the time goes in v1:
time: 65.5 us; the launch traced here: 64.9 us
  starting transfers between devices  22.8 us (35%)
  Pallas kernels  14.9 us (23%)
  waiting for transfers between devices  11 us (17%)
  local copies, waits for them, and re-layouts  10.1 us (15%)
  blocking collectives  2.48 us (4%)
  between operations  2.08 us (3%)
  other arithmetic  1.61 us (2%)
    all_to_all x1, starting transfers between devices, shards(): lax.all_to_all(copies, ('batch', 'strip'), 0, 0, tiled=True, axis_index_g...  14.6 us
    all_to_all x1, waiting for transfers between devices, shards(): lax.all_to_all(copies, ('batch', 'strip'), 0, 0, tiled=True, axis_index_g...  11 us
    unnamed x24, local copies, waits for them, and re-layouts  8.35 us
    pallas_call x1, Pallas kernels, interior(): pl.pallas_call(functools.partial(interior_kernel, step1, step2), name='in...  6.32 us
    pallas_call x1, Pallas kernels, edges(): pl.pallas_call(edge_kernel, name='edge_rows', out_shape=(jax.ShapeDtypeSt...  5.53 us
    ppermute x1, starting transfers between devices, shards(): below = lax.ppermute(heads, 'strip', up)  5.14 us
    ppermute x1, starting transfers between devices, shards(): above = lax.ppermute(tails, 'strip', down)  3.05 us
    pallas_call x1, Pallas kernels, head(): pl.pallas_call(head_kernel, name='contrastive_head', out_shape=(jax.Shape...  3 us
  transfers between devices with their start and end apart: 3, of which 1 were waited for; matrix products, arithmetic and copies ran while one was open for 1% of the time, Pallas kernels for 10%

profile of v1, /device:TPU:1, one launch (start us, length us, event | category | flops | bytes accessed | tf_op | source)
XLA Modules:
  0.0 64.9 jit_solution(1434206918000950608)
XLA Ops:
  0.6 1.0 %fusion.2 = (bf16[1,2,64,256]{3,2,1,0:T(8,128)(2,1)S(1)}, bf16[1,2,64,256]{3,2,1,0:T(8,128)(2,1)S(1)}, bf16[1,2,64,256]{3,2,1,0:T(8,128)(2,1)S(1)}, bf16[1,2,64,256]{3,2,1,0:T(8,128)(2,1)S(1)}) fusion(bf16[1,16,64,256]{3,2,1,0:T(8,128)(2,1)} %s_hbm.3, bf16[1,16,64,256]{3,2,1,0:T(8,128)(2,1)} %g_hbm.3), kind=kLoop, calls=%fused_computation.9 | loop fusion | bytes 524288 | tf_op jit(solution)/shard_map/slice | solution.py:238
  1.6 0.7 %pad_maximum_fusion.1 = bf16[2,2,64,256]{3,2,1,0:T(8,128)(2,1)} fusion(bf16[1,2,64,256]{3,2,1,0:T(8,128)(2,1)S(1)} %get-tuple-element.25, bf16[1,2,64,256]{3,2,1,0:T(8,128)(2,1)S(1)} %get-tuple-element.20), kind=kLoop, calls=%fused_computation.2 | loop fusion | flops 65536 | bytes 262144 | tf_op jit(solution)/shard_map/concatenate | solution.py:238
  2.3 5.1 %collective-permute-start.1 = (bf16[2,2,64,256]{3,2,1,0:T(8,128)(2,1)}, bf16[2,2,64,256]{3,2,1,0:T(8,128)(2,1)S(1)}, u32[]{:S(2)}, u32[]{:S(2)}) collective-permute-start(bf16[2,2,64,256]{3,2,1,0:T(8,128)(2,1)} %pad_maximum_fusion.1), channel_id=1, source_target_pairs={{1,0},{2,1},{3,2},{4,3},{5,4},{6,5},{7,6},{9,8},{10,9},{11,10},{12... | collective-permute-start | bytes 393224 | tf_op jit(solution)/shard_map/ppermute | solution.py:240
  7.4 0.7 %pad_maximum_fusion = bf16[2,2,64,256]{3,2,1,0:T(8,128)(2,1)} fusion(bf16[1,2,64,256]{3,2,1,0:T(8,128)(2,1)S(1)} %get-tuple-element.24, bf16[1,2,64,256]{3,2,1,0:T(8,128)(2,1)S(1)} %get-tuple-element.21), kind=kLoop, calls=%fused_computation.1 | loop fusion | flops 65536 | bytes 262144 | tf_op jit(solution)/shard_map/concatenate | solution.py:237
  8.1 3.1 %collective-permute-start = (bf16[2,2,64,256]{3,2,1,0:T(8,128)(2,1)}, bf16[2,2,64,256]{3,2,1,0:T(8,128)(2,1)}, u32[]{:S(2)}, u32[]{:S(2)}) collective-permute-start(bf16[2,2,64,256]{3,2,1,0:T(8,128)(2,1)} %pad_maximum_fusion), channel_id=1, source_target_pairs={{0,1},{1,2},{2,3},{3,4},{4,5},{5,6},{6,7},{8,9},{9,10},{10,11},{11... | collective-permute-start | bytes 393224 | tf_op jit(solution)/shard_map/ppermute | solution.py:239
  11.1 0.0 copy-start
  11.1 1.3 %copy-done = bf16[3,3,256,256]{3,2,1,0:T(8,128)(2,1)S(1)} copy-done((bf16[3,3,256,256]{3,2,1,0:T(8,128)(2,1)S(1)}, bf16[3,3,256,256]{3,2,1,0:T(8,128)(2,1)}, u32[]{:S(2)}) %copy-start) | copy-done | bytes 1179672
  12.4 1.3 %copy-done.2 = bf16[3,3,256,256]{3,2,1,0:T(8,128)(2,1)S(1)} copy-done((bf16[3,3,256,256]{3,2,1,0:T(8,128)(2,1)S(1)}, bf16[3,3,256,256]{3,2,1,0:T(8,128)(2,1)}, u32[]{:S(2)}) %copy-start.2) | copy-done | bytes 1179672
  13.7 1.0 %copy-done.4 = bf16[1,16,64,256]{3,2,1,0:T(8,128)(2,1)S(1)} copy-done((bf16[1,16,64,256]{3,2,1,0:T(8,128)(2,1)S(1)}, bf16[1,16,64,256]{3,2,1,0:T(8,128)(2,1)}, u32[]{:S(2)}) %copy-start.4) | copy-done | bytes 524312
  14.7 1.0 %copy-done.6 = bf16[1,16,64,256]{3,2,1,0:T(8,128)(2,1)S(1)} copy-done((bf16[1,16,64,256]{3,2,1,0:T(8,128)(2,1)S(1)}, bf16[1,16,64,256]{3,2,1,0:T(8,128)(2,1)}, u32[]{:S(2)}) %copy-start.6) | copy-done | bytes 524312
  15.8 6.3 %interior_rows.1 = (f32[2,1,16,64,256]{4,3,2,1,0:T(8,128)}, bf16[4,2,64,256]{3,2,1,0:T(8,128)(2,1)S(1)}, f32[2,8,256]{2,1,0:T(8,128)S(1)}) custom-call(bf16[1,16,64,256]{3,2,1,0:T(8,128)(2,1)S(1)} %copy-done.4, bf16[1,16,64,256]{3,2,1,0:T(8,128)(2,1)S(1)} %copy-done.6, bf16[3,768,256]{2,1,0:T(8,128)(2,1)S(1)} %bitcast.10, bf16[3,768,256]{2,1,0:T(8,128)(2,1)S(1)} %bitcast.12), custom_call_target="tpu_custom_call" | custom-call | flops 4200000000 | bytes 6000000 | tf_op jit(solution)/shard_map/interior_rows/pallas_call | solution.py:69
  22.1 0.0 copy-start.10
  22.1 0.7 %copy-done.10 = bf16[4,2,64,256]{3,2,1,0:T(8,128)(2,1)} copy-done((bf16[4,2,64,256]{3,2,1,0:T(8,128)(2,1)}, bf16[4,2,64,256]{3,2,1,0:T(8,128)(2,1)S(1)}, u32[]{:S(2)}) %copy-start.10) | copy-done | bytes 262168
  23.5 0.1 pad_add_fusion.here
  23.5 0.0 collective-permute-done.1.below_hbm
  23.5 0.0 collective-permute-done.above_hbm
  23.5 0.0 copy-done.1
  23.5 0.0 copy-done.3
  23.6 0.0 copy-done.5
  23.6 0.0 copy-done.7
  23.6 0.0 copy-start.11
  23.6 0.9 %copy-done.11 = bf16[4,2,64,256]{3,2,1,0:T(8,128)(2,1)S(1)} copy-done((bf16[4,2,64,256]{3,2,1,0:T(8,128)(2,1)S(1)}, bf16[4,2,64,256]{3,2,1,0:T(8,128)(2,1)}, u32[]{:S(2)}) %copy-start.11) | copy-done | bytes 262168
  24.5 5.5 %edge_rows.1 = (f32[2,1,16,64,256]{4,3,2,1,0:T(8,128)}, f32[2,256]{1,0:T(2,128)S(1)}) custom-call(s32[2]{0:T(128)S(1)} %pad_add_fusion.here, bf16[1,16,64,256]{3,2,1,0:T(8,128)(2,1)S(1)} %copy-done.5, bf16[1,16,64,256]{3,2,1,0:T(8,128)(2,1)S(1)} %copy-done.7, ...), custom_call_target="tpu_custom_call", output_to_operand_aliasing={{0}: (9, {})} | custom-call | flops 1200000000 | bytes 4000000 | tf_op jit(solution)/shard_map/edge_rows/pallas_call | solution.py:155
  30.1 2.5 %psum.7 = bf16[2,384]{1,0:T(2,128)(2,1)S(1)} all-reduce(f32[2,384]{1,0:T(2,128)S(1)} %concatenate.11), channel_id=1, replica_groups={{0,1},{2,3},{4,5},{6,7},{8,9},{10,11},{12,13},{14,15},{16,17},{18,19},{..., use_global_device_ids=true, to_apply=%region_0.0 | all-reduce | flops 768 | bytes 4608 | tf_op jit(solution)/shard_map/psum | solution.py:247
  32.6 0.8 %broadcast_in_dim.13 = bf16[128,2,384]{2,1,0:T(2,128)(2,1)} broadcast(bf16[2,384]{1,0:T(2,128)(2,1)S(1)} %psum.7), dimensions={1,2} | broadcast | bytes 198144 | tf_op jit(solution)/shard_map/broadcast_in_dim | solution.py:250
  33.4 14.6 %all-to-all-start = ((bf16[128,2,384]{2,1,0:T(2,128)(2,1)}), bf16[128,2,384]{2,1,0:T(2,128)(2,1)S(1)}, u32[]{:S(2)}, u32[]{:S(2)}) async-start(bf16[128,2,384]{2,1,0:T(2,128)(2,1)} %broadcast_in_dim.13), calls=%async_computation | async-start | bytes 393216 | tf_op jit(solution)/shard_map/all_to_all | solution.py:251
  48.6 11.0 %all-to-all-done = bf16[128,2,384]{2,1,0:T(2,128)(2,1)S(1)} async-done(((bf16[128,2,384]{2,1,0:T(2,128)(2,1)}), bf16[128,2,384]{2,1,0:T(2,128)(2,1)S(1)}, u32[]{:S(2)}, u32[]{:S(2)}) %all-to-all-start) | async-done | bytes 196640 | tf_op jit(solution)/shard_map/all_to_all | solution.py:251
  59.6 0.2 convert_reduce_fusion
  59.8 0.0 copy-start.8
  59.9 1.0 %copy-done.8 = bf16[256,1024]{1,0:T(8,128)(2,1)S(1)} copy-done((bf16[256,1024]{1,0:T(8,128)(2,1)S(1)}, bf16[256,1024]{1,0:T(8,128)(2,1)}, u32[]{:S(2)}) %copy-start.8) | copy-done | bytes 524312
  60.9 1.0 %copy-done.9 = bf16[256,1024]{1,0:T(8,128)(2,1)S(1)} copy-done((bf16[256,1024]{1,0:T(8,128)(2,1)S(1)}, bf16[256,1024]{1,0:T(8,128)(2,1)}, u32[]{:S(2)}) %copy-start.9) | copy-done | bytes 524312
  61.9 3.0 %contrastive_head.1 = (f32[1]{0:T(128)}, f32[256,1024]{1,0:T(8,128)}, f32[256,1024]{1,0:T(8,128)}) custom-call(s32[1]{0:T(128)} %bitcast.mine, f32[1]{0:T(128)S(6)} %copy.19.sharp, f32[2,32,384]{2,1,0:T(8,128)S(1)} %fusion.tot, bf16[256,1024]{1,0:T(8,128)(2,1)S(1)} %copy-done.8, bf16[256,1024]{1,0:T(8,128)(2,1)S(1)} %copy-done.9), custom_call_target="tpu_custom_call" | custom-call | tf_op jit(solution)/shard_map/contrastive_head/pallas_call | solution.py:217
  (12 shorter events, 0.0 us)
Async XLA Ops:
  2.3 21.3 %collective-permute-start.1 = (bf16[2,2,64,256]{3,2,1,0:T(8,128)(2,1)}, bf16[2,2,64,256]{3,2,1,0:T(8,128)(2,1)S(1)}, u32[]{:S(2)}, u32[]{:S(2)}) collective-permute-start(bf16[2,2,64,256]{3,2,1,0:T(8,128)(2,1)} %pad_maximum_fusion.1), channel_id=1, source_target_pairs={{1,0},{2,1},{3,2},{4,3},{5,4},{6,5},{7,6},{9,8},{10,9},{11,10},{12... | collective-permute-start | bytes 393224 | tf_op jit(solution)/shard_map/ppermute | solution.py:240
  8.1 15.5 %collective-permute-start = (bf16[2,2,64,256]{3,2,1,0:T(8,128)(2,1)}, bf16[2,2,64,256]{3,2,1,0:T(8,128)(2,1)}, u32[]{:S(2)}, u32[]{:S(2)}) collective-permute-start(bf16[2,2,64,256]{3,2,1,0:T(8,128)(2,1)} %pad_maximum_fusion), channel_id=1, source_target_pairs={{0,1},{1,2},{2,3},{3,4},{4,5},{5,6},{6,7},{8,9},{9,10},{10,11},{11... | collective-permute-start | bytes 393224 | tf_op jit(solution)/shard_map/ppermute | solution.py:239
  11.1 1.3 %copy-start = (bf16[3,3,256,256]{3,2,1,0:T(8,128)(2,1)S(1)}, bf16[3,3,256,256]{3,2,1,0:T(8,128)(2,1)}, u32[]{:S(2)}) copy-start(bf16[3,3,256,256]{3,2,1,0:T(8,128)(2,1)} %param.10) | copy-start | bytes 3538948
  12.4 1.3 %copy-start.2 = (bf16[3,3,256,256]{3,2,1,0:T(8,128)(2,1)S(1)}, bf16[3,3,256,256]{3,2,1,0:T(8,128)(2,1)}, u32[]{:S(2)}) copy-start(bf16[3,3,256,256]{3,2,1,0:T(8,128)(2,1)} %param.11) | copy-start | bytes 3538948
  13.7 1.0 %copy-start.4 = (bf16[1,16,64,256]{3,2,1,0:T(8,128)(2,1)S(1)}, bf16[1,16,64,256]{3,2,1,0:T(8,128)(2,1)}, u32[]{:S(2)}) copy-start(bf16[1,16,64,256]{3,2,1,0:T(8,128)(2,1)} %s_hbm.3) | copy-start | bytes 1572868
  14.7 1.0 %copy-start.6 = (bf16[1,16,64,256]{3,2,1,0:T(8,128)(2,1)S(1)}, bf16[1,16,64,256]{3,2,1,0:T(8,128)(2,1)}, u32[]{:S(2)}) copy-start(bf16[1,16,64,256]{3,2,1,0:T(8,128)(2,1)} %g_hbm.3) | copy-start | bytes 1572868
  15.8 7.8 %copy-start.1 = (bf16[3,3,256,256]{3,2,1,0:T(8,128)(2,1)S(1)}, bf16[3,3,256,256]{3,2,1,0:T(8,128)(2,1)}, u32[]{:S(2)}) copy-start(bf16[3,3,256,256]{3,2,1,0:T(8,128)(2,1)} %param.10) | copy-start | bytes 3538948
  15.8 7.8 %copy-start.3 = (bf16[3,3,256,256]{3,2,1,0:T(8,128)(2,1)S(1)}, bf16[3,3,256,256]{3,2,1,0:T(8,128)(2,1)}, u32[]{:S(2)}) copy-start(bf16[3,3,256,256]{3,2,1,0:T(8,128)(2,1)} %param.11) | copy-start | bytes 3538948
  15.8 7.8 %copy-start.5 = (bf16[1,16,64,256]{3,2,1,0:T(8,128)(2,1)S(1)}, bf16[1,16,64,256]{3,2,1,0:T(8,128)(2,1)}, u32[]{:S(2)}) copy-start(bf16[1,16,64,256]{3,2,1,0:T(8,128)(2,1)} %s_hbm.3) | copy-start | bytes 1572868
  15.8 7.8 %copy-start.7 = (bf16[1,16,64,256]{3,2,1,0:T(8,128)(2,1)S(1)}, bf16[1,16,64,256]{3,2,1,0:T(8,128)(2,1)}, u32[]{:S(2)}) copy-start(bf16[1,16,64,256]{3,2,1,0:T(8,128)(2,1)} %g_hbm.3) | copy-start | bytes 1572868
  22.1 0.7 %copy-start.10 = (bf16[4,2,64,256]{3,2,1,0:T(8,128)(2,1)}, bf16[4,2,64,256]{3,2,1,0:T(8,128)(2,1)S(1)}, u32[]{:S(2)}) copy-start(bf16[4,2,64,256]{3,2,1,0:T(8,128)(2,1)S(1)} %get-tuple-element.12.hedge) | copy-start | bytes 786436
  23.6 1.0 %copy-start.11 = (bf16[4,2,64,256]{3,2,1,0:T(8,128)(2,1)S(1)}, bf16[4,2,64,256]{3,2,1,0:T(8,128)(2,1)}, u32[]{:S(2)}) copy-start(bf16[4,2,64,256]{3,2,1,0:T(8,128)(2,1)} %copy-done.10) | copy-start | bytes 786436
  33.4 26.3 %all-to-all-start = ((bf16[128,2,384]{2,1,0:T(2,128)(2,1)}), bf16[128,2,384]{2,1,0:T(2,128)(2,1)S(1)}, u32[]{:S(2)}, u32[]{:S(2)}) async-start(bf16[128,2,384]{2,1,0:T(2,128)(2,1)} %broadcast_in_dim.13), calls=%async_computation | async-start | bytes 393216 | tf_op jit(solution)/shard_map/all_to_all | solution.py:251
  59.8 1.0 %copy-start.8 = (bf16[256,1024]{1,0:T(8,128)(2,1)S(1)}, bf16[256,1024]{1,0:T(8,128)(2,1)}, u32[]{:S(2)}) copy-start(bf16[256,1024]{1,0:T(8,128)(2,1)} %sproj.1) | copy-start | bytes 1572868
  60.9 1.0 %copy-start.9 = (bf16[256,1024]{1,0:T(8,128)(2,1)S(1)}, bf16[256,1024]{1,0:T(8,128)(2,1)}, u32[]{:S(2)}) copy-start(bf16[256,1024]{1,0:T(8,128)(2,1)} %gproj.1) | copy-start | bytes 1572868

commit v2 on v1

v2 whole, which is shorter than its diff:
```python
import functools
import jax
import jax.numpy as jnp
from jax import lax
from jax.experimental import pallas as pl
from jax.experimental.pallas import tpu as pltpu
from jax.sharding import PartitionSpec as P

ROWS, COLS, C, E = 16, 64, 256, 1024
BF, F32 = jnp.bfloat16, jnp.float32
MIB = 1 << 20
HBM = pl.BlockSpec(memory_space=pltpu.MemorySpace.HBM)
VM = pl.BlockSpec(memory_space=pltpu.MemorySpace.VMEM)
SM = pl.BlockSpec(memory_space=pltpu.MemorySpace.SMEM)


def pack_kernel(here, s_hbm, g_hbm, chip, cross, sems):
    odd = lax.rem(here[0], 2)
    copies = []
    for f, ref in enumerate((s_hbm, g_hbm)):
        tail = (ROWS - 2) * (1 - odd)
        head = (ROWS - 2) * odd
        copies.append(pltpu.make_async_copy(ref.at[0, pl.ds(tail, 2)], chip.at[f], sems.at[f]))
        copies.append(pltpu.make_async_copy(ref.at[0, pl.ds(head, 2)], cross.at[f], sems.at[2 + f]))
    for cp in copies:
        cp.start()
    for cp in copies:
        cp.wait()


def pack(here, s, g):
    side = jax.ShapeDtypeStruct((2, 2, COLS, C), BF)
    return pl.pallas_call(
        pack_kernel,
        name="pack_halo_rows",
        out_shape=(side, side),
        in_specs=[SM, HBM, HBM],
        out_specs=(VM, VM),
        scratch_shapes=[pltpu.SemaphoreType.DMA((4,))],
        compiler_params=pltpu.CompilerParams(vmem_limit_bytes=2 * MIB),
    )(here, s, g)


def widen(row):
    col = lax.broadcasted_iota(jnp.int32, row.shape, 0)
    left = jnp.where(col == 0, 0.0, pltpu.roll(row, 1, 0))
    right = jnp.where(col == COLS - 1, 0.0, pltpu.roll(row, COLS - 1, 0))
    return jnp.concatenate([left.astype(BF), row.astype(BF), right.astype(BF)], axis=-1)


def conv(wide, first, rows, weights):
    total = None
    for dy in range(3):
        lhs = wide[pl.ds(first + dy, rows)].reshape(rows * COLS, 3 * C)
        part = jnp.dot(lhs, weights[dy], preferred_element_type=F32)
        total = part if total is None else total + part
    return total


def conv_of(rows, weights):
    total = None
    for dy in range(3):
        lhs = jnp.concatenate([rows[dy], rows[dy + 1]], axis=0)
        part = jnp.dot(lhs, weights[dy], preferred_element_type=F32)
        total = part if total is None else total + part
    return total


def spans(total, step):
    return [(r, min(step, total - r)) for r in range(0, total, step)]


def interior_kernel(step1, step2, s_hbm, g_hbm, w1_hbm, w2_hbm, x, xw, hw, o, sum_ref, w1, w2, sems):
    cx = [[pltpu.make_async_copy(ref.at[0, pl.ds(8 * p, 8)], x.at[f, pl.ds(8 * p, 8)], sems.at[2 * f + p])
           for p in range(2)] for f, ref in enumerate((s_hbm, g_hbm))]
    cw1 = pltpu.make_async_copy(w1_hbm, w1, sems.at[4])
    cw2 = pltpu.make_async_copy(w2_hbm, w2, sems.at[5])
    cx[0][0].start(); cw1.start(); cx[0][1].start(); cw2.start(); cx[1][0].start(); cx[1][1].start()

    def spread(f, rows):
        for r in rows:
            xw[f, r] = widen(jnp.maximum(x[f, r].astype(F32), 0.0))

    def first(f, r, n):
        h = jnp.maximum(conv(xw.at[f], r, n, w1), 0.0)
        for k in range(n):
            hw[f, r + k] = widen(h[k * COLS:(k + 1) * COLS])

    def second(f, r, n, acc):
        y = conv(hw.at[f], r, n, w2)
        y = jnp.maximum(y + x[f, r + 2:r + 2 + n].reshape(n * COLS, C).astype(F32), 0.0)
        o[f, r:r + n] = y.reshape(n, COLS, C)
        part = jnp.sum(y.reshape(n * COLS // 8, 8, C), axis=0)
        return part if acc is None else acc + part

    cx[0][0].wait()
    spread(0, range(8))
    cx[0][1].wait()
    spread(0, range(8, 16))
    cw1.wait()
    for r, n in spans(14, step1):
        first(0, r, n)
    cx[1][0].wait(); cx[1][1].wait(); cw2.wait()
    acc = None
    todo = list(range(16))
    plan = spans(12, step2)
    for i, (r, n) in enumerate(plan):
        share = todo[i * 16 // len(plan):(i + 1) * 16 // len(plan)]
        spread(1, share)
        acc = second(0, r, n, acc)
    sum_ref[0] = acc
    for r, n in spans(14, step1):
        first(1, r, n)
    acc = None
    for r, n in spans(12, step2):
        acc = second(1, r, n, acc)
    sum_ref[1] = acc


def interior(s, g, w1, w2, step1=7, step2=6):
    wide = jax.ShapeDtypeStruct((3, 3 * C, C), BF)
    return pl.pallas_call(
        functools.partial(interior_kernel, step1, step2),
        name="interior_rows",
        out_shape=(jax.ShapeDtypeStruct((2, ROWS, COLS, C), BF),
                   jax.ShapeDtypeStruct((2, ROWS, COLS, 3 * C), BF),
                   jax.ShapeDtypeStruct((2, 14, COLS, 3 * C), BF),
                   jax.ShapeDtypeStruct((2, 12, COLS, C), F32),
                   jax.ShapeDtypeStruct((2, 8, C), F32), wide, wide),
        in_specs=[HBM] * 4,
        out_specs=(VM,) * 7,
        scratch_shapes=[pltpu.SemaphoreType.DMA((6,))],
        compiler_params=pltpu.CompilerParams(vmem_limit_bytes=24 * MIB),
        cost_estimate=pl.CostEstimate(flops=4_200_000_000, transcendentals=0, bytes_accessed=6_000_000),
    )(s, g, w1, w2)


def edge_kernel(here, chip, cross, x, xw, hw, sums, w1, w2, sp_hbm, gp_hbm, o, share, sp, gp, halo, hh, sems):
    csp = pltpu.make_async_copy(sp_hbm, sp, sems.at[0])
    cgp = pltpu.make_async_copy(gp_hbm, gp, sems.at[1])
    csp.start(); cgp.start()
    odd = lax.rem(here[0], 2)
    for f in range(2):
        for r in range(2):
            a = widen(jnp.maximum(chip[f, r].astype(F32), 0.0))
            b = widen(jnp.maximum(cross[f, r].astype(F32), 0.0))
            halo[2 * f + 1 - odd, r] = a
            halo[2 * f + odd, r] = b
    for k in range(4):
        f = k // 2
        if k % 2 == 0:
            rows = [halo[k, 0], halo[k, 1], xw[f, 0], xw[f, 1]]
        else:
            rows = [xw[f, ROWS - 2], xw[f, ROWS - 1], halo[k, 0], halo[k, 1]]
        h = jnp.maximum(conv_of(rows, w1), 0.0)
        for r in range(2):
            row = h[r * COLS:(r + 1) * COLS]
            if k % 2 == 0 and r == 0:
                row = jnp.where(here[0] > 0, row, 0.0)
            if k % 2 == 1 and r == 1:
                row = jnp.where(here[0] < here[1] - 1, row, 0.0)
            hh[k, r] = widen(row)
    tot = [sums[0], sums[1]]
    for k in range(4):
        f = k // 2
        if k % 2 == 0:
            rows = [hh[k, 0], hh[k, 1], hw[f, 0], hw[f, 1]]
        else:
            rows = [hw[f, 12], hw[f, 13], hh[k, 0], hh[k, 1]]
        y = conv_of(rows, w2)
        y = jnp.maximum(y + x[f, 14 * (k % 2):14 * (k % 2) + 2].reshape(2 * COLS, C).astype(F32), 0.0)
        o[k] = y.reshape(2, COLS, C)
        tot[f] = tot[f] + jnp.sum(y.reshape(16, 8, C), axis=0)
    scale = 1.0 / (here[1] * (ROWS * COLS)).astype(F32)
    for f in range(2):
        share[f:f + 1, :C] = jnp.sum(tot[f], axis=0, keepdims=True) * scale
    share[:, C:] = jnp.full((2, 128), here[2], jnp.int32).astype(F32)
    csp.wait(); cgp.wait()


def edges(here, chip, cross, x, xw, hw, sums, w1, w2, sp, gp):
    proj = jax.ShapeDtypeStruct((C, E), BF)
    return pl.pallas_call(
        edge_kernel,
        name="edge_rows",
        out_shape=(jax.ShapeDtypeStruct((4, 2, COLS, C), F32), jax.ShapeDtypeStruct((2, C + 128), F32), proj, proj),
        in_specs=[SM] + [VM] * 8 + [HBM] * 2,
        out_specs=(VM,) * 4,
        scratch_shapes=[
            pltpu.VMEM((4, 2, COLS, 3 * C), BF),
            pltpu.VMEM((4, 2, COLS, 3 * C), BF),
            pltpu.SemaphoreType.DMA((2,)),
        ],
        compiler_params=pltpu.CompilerParams(vmem_limit_bytes=24 * MIB),
        cost_estimate=pl.CostEstimate(flops=1_200_000_000, transcendentals=0, bytes_accessed=4_000_000),
    )(here, chip, cross, x, xw, hw, sums, w1, w2, sp, gp)


def head_kernel(mine, sharp, tot, sproj, gproj, o, oe, loss_ref, gs_hbm, gg_hbm, out_hbm, buf, sem, osem):
    outs = []
    for f in range(2):
        outs.append(pltpu.make_async_copy(o.at[f], out_hbm.at[f, 0, pl.ds(2, 12)], osem.at[3 * f]))
        for k in range(2):
            outs.append(pltpu.make_async_copy(oe.at[2 * f + k], out_hbm.at[f, 0, pl.ds(14 * k, 2)], osem.at[3 * f + 1 + k]))
    for cp in outs:
        cp.start()
    pairs = tot.shape[1]
    s_pool = tot[0, :, :C].astype(BF)
    g_pool = tot[1, :, :C].astype(BF)
    label = tot[0, :, C:C + 1]
    temp = sharp[0]
    s_emb = jnp.dot(s_pool, sproj[...], preferred_element_type=F32)
    g_emb = jnp.dot(g_pool, gproj[...], preferred_element_type=F32)
    s_inv = lax.rsqrt(jnp.sum(s_emb * s_emb, axis=-1, keepdims=True) + 1e-06)
    g_inv = lax.rsqrt(jnp.sum(g_emb * g_emb, axis=-1, keepdims=True) + 1e-06)
    s_unit = s_emb * s_inv
    g_unit = g_emb * g_inv
    s_bf = s_unit.astype(BF)
    g_bf = g_unit.astype(BF)
    logits = temp * lax.dot_general(s_bf, g_bf, (((1,), (1,)), ((), ())), preferred_element_type=F32)
    ex = jnp.exp(logits)
    row_total = jnp.sum(ex, axis=1, keepdims=True)
    column = lax.broadcasted_iota(jnp.int32, (pairs, pairs), 1).astype(F32)
    matched = column == label
    positive = jnp.sum(jnp.where(matched, logits, 0.0), axis=1, keepdims=True)
    losses = jnp.log(row_total) - positive
    row = lax.broadcasted_iota(jnp.int32, (pairs, 1), 0)
    lgrad = (ex / row_total - jnp.where(matched, 1.0, 0.0)).astype(BF)
    s_ug = temp * jnp.dot(lgrad, g_bf, preferred_element_type=F32)
    g_ug = temp * lax.dot_general(lgrad, s_bf, (((0,), (0,)), ((), ())), preferred_element_type=F32)
    s_eg = ((s_ug - s_unit * jnp.sum(s_unit * s_ug, axis=-1, keepdims=True)) * s_inv).astype(BF)
    g_eg = ((g_ug - g_unit * jnp.sum(g_unit * g_ug, axis=-1, keepdims=True)) * g_inv).astype(BF)
    for k, (pool, grad, dest) in enumerate(((s_pool, s_eg, gs_hbm), (g_pool, g_eg, gg_hbm))):
        for p in range(2):
            half = pl.ds(p * (C // 2), C // 2)
            buf[k, half] = lax.dot_general(pool[:, p * (C // 2):(p + 1) * (C // 2)], grad, (((0,), (0,)), ((), ())),
                                           preferred_element_type=F32)
            cp = pltpu.make_async_copy(buf.at[k, half], dest.at[half], sem.at[2 * k + p])
            cp.start()
            outs.append(cp)
    loss_ref[0] = jnp.sum(jnp.where(row == mine[0], losses, 0.0))
    for cp in outs:
        cp.wait()


def head(mine, sharp, tot, sproj, gproj, o, oe):
    return pl.pallas_call(
        head_kernel,
        name="contrastive_head",
        out_shape=(jax.ShapeDtypeStruct((1,), F32), jax.ShapeDtypeStruct((C, E), F32),
                   jax.ShapeDtypeStruct((C, E), F32), jax.ShapeDtypeStruct((2, 1, ROWS, COLS, C), F32)),
        in_specs=[SM, SM] + [VM] * 5,
        out_specs=(SM, HBM, HBM, HBM),
        scratch_shapes=[pltpu.VMEM((2, C, E), F32), pltpu.SemaphoreType.DMA((4,)), pltpu.SemaphoreType.DMA((6,))],
        compiler_params=pltpu.CompilerParams(vmem_limit_bytes=16 * MIB),
    )(mine, sharp, tot, sproj, gproj, o, oe)


def shards(state_maps, goal_maps, conv_one, conv_two, state_proj, goal_proj, inv_temp, pair_index):
    strips, batch = lax.axis_size("strip"), lax.axis_size("batch")
    mine = lax.axis_index("batch").astype(jnp.int32)
    here = jnp.stack([lax.axis_index("strip").astype(jnp.int32), jnp.int32(strips), pair_index[0]])
    w1 = conv_one.reshape(3, 3 * C, C)
    w2 = conv_two.reshape(3, 3 * C, C)
    chip, cross = pack(here, state_maps, goal_maps)
    chip = lax.ppermute(chip, "strip", [(i, i ^ 1) for i in range(strips)])
    cross = lax.ppermute(cross, "strip", [(i, i + 2 * (i % 2) - 1) for i in range(1, strips - 1)])
    x, xw, hw, o, sums, w1, w2 = interior(state_maps, goal_maps, w1, w2)
    oe, share, sp, gp = edges(here, chip, cross, x, xw, hw, sums, w1, w2, state_proj, goal_proj)
    share = lax.psum(share, "strip", axis_index_groups=[[2 * i, 2 * i + 1] for i in range(strips // 2)]).astype(BF)
    groups = [[b * strips + s for b in range(batch) for s in range(core, strips, 2)] for core in range(2)]
    copies = jnp.broadcast_to(share, (batch * strips // 2, *share.shape))
    got = lax.all_to_all(copies, ("batch", "strip"), 0, 0, tiled=True, axis_index_groups=groups)
    got = got.reshape(batch, strips // 2, 2, C + 128).astype(F32)
    tot = jnp.moveaxis(jnp.sum(got, axis=1), 1, 0)
    tot = tot * jnp.where(jnp.arange(C + 128) < C, 1.0, 1.0 / strips)
    return head(mine.reshape(1), inv_temp, tot, sp, gp, o, oe)


def solution(mesh):
    placed = (
        P("batch", "strip", None, None),
        P("batch", "strip", None, None),
        P(),
        P(),
        P(),
        P(),
        P(),
        P("batch"),
    )
    return jax.shard_map(
        shards,
        mesh=mesh,
        in_specs=placed,
        out_specs=(P("batch"), P(), P(), P(None, "batch", "strip", None, None)),
        check_vma=False,
    )
```

time: 65.5 us -> 56 us (0.85)
  Pallas kernels: 14.9 us -> 12.1 us
  starting transfers between devices: 22.8 us -> 20.1 us
  local copies, waits for them, and re-layouts: 10.1 us -> 7.49 us
  other arithmetic: 1.61 us -> 0.27 us
    pallas_call x1, Pallas kernels: 5.53 us -> 2.22 us  [edges(): pl.pallas_call(edge_kernel, name='edge_rows', out_shape=(jax.ShapeDtypeSt...]
    ppermute x2, starting transfers between devices: 8.19 us -> 6.39 us  [the longest x1 3.33 us: shards(): chip = lax.ppermute(chip, 'strip', [(i, i ^ 1) for i in range(strips)])]
    unnamed x24 -> x16, local copies, waits for them, and re-layouts: 8.35 us -> 6.71 us
    concatenate x2 -> x0, other arithmetic: 1.33 us -> none  [the longest x1 0.67 us: shards(): jnp.concatenate([state_maps[:, ROWS - 2:], goal_maps[:, ROWS - 2:]], axis=0)]
    slice x1 -> x0, local copies, waits for them, and re-layouts: 0.96 us -> none  [shards(): heads = jnp.concatenate([state_maps[:, :2], goal_maps[:, :2]], axis=0)]
    pallas_call x0 -> x1, Pallas kernels: none -> 0.93 us  [pack(): pl.pallas_call(pack_kernel, name='pack_halo_rows', out_shape=(side, side)...]
    all_to_all x1, starting transfers between devices: 14.6 us -> 13.7 us  [shards(): lax.all_to_all(copies, ('batch', 'strip'), 0, 0, tiled=True, axis_index_g...]
    pallas_call x1, Pallas kernels: 6.32 us -> 5.57 us  [interior(): pl.pallas_call(functools.partial(interior_kernel, step1, step2), name='in...]
  transfers between devices with their start and end apart: 3 -> 3, of which waited for: 1 -> 1; matrix products, arithmetic and copies ran while one was open for 1% -> 0% of each run, Pallas kernels for 10% -> 10%
where the time goes in v2:
time: 56 us; the launch traced here: 55.5 us
  starting transfers between devices  20.1 us (36%)
  Pallas kernels  12.1 us (22%)
  waiting for transfers between devices  11 us (20%)
  local copies, waits for them, and re-layouts  7.49 us (13%)
  blocking collectives  2.48 us (4%)
  between operations  2.04 us (4%)
    all_to_all x1, starting transfers between devices, shards(): lax.all_to_all(copies, ('batch', 'strip'), 0, 0, tiled=True, axis_index_g...  13.7 us
    all_to_all x1, waiting for transfers between devices, shards(): lax.all_to_all(copies, ('batch', 'strip'), 0, 0, tiled=True, axis_index_g...  11 us
    unnamed x16, local copies, waits for them, and re-layouts  6.71 us
    pallas_call x1, Pallas kernels, interior(): pl.pallas_call(functools.partial(interior_kernel, step1, step2), name='in...  5.57 us
    pallas_call x1, Pallas kernels, head(): pl.pallas_call(head_kernel, name='contrastive_head', out_shape=(jax.Shape...  3.38 us
    ppermute x1, starting transfers between devices, shards(): chip = lax.ppermute(chip, 'strip', [(i, i ^ 1) for i in range(strips)])  3.33 us
    ppermute x1, starting transfers between devices, shards(): lax.ppermute(cross, 'strip', [(i, i + 2 * (i % 2) - 1) for i in range(1,...  3.06 us
    psum x1, blocking collectives, shards(): lax.psum(share, 'strip', axis_index_groups=[[2 * i, 2 * i + 1] for i in r...  2.48 us
  transfers between devices with their start and end apart: 3, of which 1 were waited for; matrix products, arithmetic and copies ran while one was open for 0% of the time, Pallas kernels for 10%

profile of v2, /device:TPU:1, one launch (start us, length us, event | category | flops | bytes accessed | tf_op | source)
XLA Modules:
  0.0 55.5 jit_solution(11348411170531642758)
XLA Ops:
  1.3 0.1 pad_add_fusion.here
  1.4 0.0 copy-start
  1.4 1.0 %copy-done = bf16[1,16,64,256]{3,2,1,0:T(8,128)(2,1)S(1)} copy-done((bf16[1,16,64,256]{3,2,1,0:T(8,128)(2,1)S(1)}, bf16[1,16,64,256]{3,2,1,0:T(8,128)(2,1)}, u32[]{:S(2)}) %copy-start) | copy-done | bytes 524312
  2.4 0.0 copy-start.2
  2.4 1.0 %copy-done.2 = bf16[1,16,64,256]{3,2,1,0:T(8,128)(2,1)S(1)} copy-done((bf16[1,16,64,256]{3,2,1,0:T(8,128)(2,1)S(1)}, bf16[1,16,64,256]{3,2,1,0:T(8,128)(2,1)}, u32[]{:S(2)}) %copy-start.2) | copy-done | bytes 524312
  3.4 0.9 %pack_halo_rows.1 = (bf16[2,2,64,256]{3,2,1,0:T(8,128)(2,1)S(1)}, bf16[2,2,64,256]{3,2,1,0:T(8,128)(2,1)S(1)}) custom-call(s32[3]{0:T(128)S(1)} %pad_add_fusion.here, bf16[1,16,64,256]{3,2,1,0:T(8,128)(2,1)S(1)} %copy-done, bf16[1,16,64,256]{3,2,1,0:T(8,128)(2,1)S(1)} %copy-done.2), custom_call_target="tpu_custom_call" | custom-call | tf_op jit(solution)/shard_map/pack_halo_rows/pallas_call | solution.py:33
  4.4 3.3 %collective-permute-start = (bf16[2,2,64,256]{3,2,1,0:T(8,128)(2,1)S(1)}, bf16[2,2,64,256]{3,2,1,0:T(8,128)(2,1)S(1)}, u32[]{:S(2)}, u32[]{:S(2)}) collective-permute-start(bf16[2,2,64,256]{3,2,1,0:T(8,128)(2,1)S(1)} %get-tuple-element.17), channel_id=1, source_target_pairs={{0,1},{1,0},{2,3},{3,2},{4,5},{5,4},{6,7},{7,6},{8,9},{9,8},{10,11... | collective-permute-start | bytes 393224 | tf_op jit(solution)/shard_map/ppermute | solution.py:266
  7.7 3.1 %collective-permute-start.1 = (bf16[2,2,64,256]{3,2,1,0:T(8,128)(2,1)S(1)}, bf16[2,2,64,256]{3,2,1,0:T(8,128)(2,1)S(1)}, u32[]{:S(2)}, u32[]{:S(2)}) collective-permute-start(bf16[2,2,64,256]{3,2,1,0:T(8,128)(2,1)S(1)} %get-tuple-element.18), channel_id=1, source_target_pairs={{1,2},{2,1},{3,4},{4,3},{5,6},{6,5},{9,10},{10,9},{11,12},{12,11},... | collective-permute-start | bytes 393224 | tf_op jit(solution)/shard_map/ppermute | solution.py:267
  10.8 0.0 copy-start.1
  10.8 1.0 %copy-done.1 = bf16[1,16,64,256]{3,2,1,0:T(8,128)(2,1)S(1)} copy-done((bf16[1,16,64,256]{3,2,1,0:T(8,128)(2,1)S(1)}, bf16[1,16,64,256]{3,2,1,0:T(8,128)(2,1)}, u32[]{:S(2)}) %copy-start.1) | copy-done | bytes 524312
  11.8 0.0 copy-start.3
  11.8 1.0 %copy-done.3 = bf16[1,16,64,256]{3,2,1,0:T(8,128)(2,1)S(1)} copy-done((bf16[1,16,64,256]{3,2,1,0:T(8,128)(2,1)S(1)}, bf16[1,16,64,256]{3,2,1,0:T(8,128)(2,1)}, u32[]{:S(2)}) %copy-start.3) | copy-done | bytes 524312
  12.9 0.0 copy-start.6
  12.9 1.3 %copy-done.6 = bf16[3,3,256,256]{3,2,1,0:T(8,128)(2,1)S(1)} copy-done((bf16[3,3,256,256]{3,2,1,0:T(8,128)(2,1)S(1)}, bf16[3,3,256,256]{3,2,1,0:T(8,128)(2,1)}, u32[]{:S(2)}) %copy-start.6) | copy-done | bytes 1179672
  14.1 0.0 copy-start.7
  14.1 1.3 %copy-done.7 = bf16[3,3,256,256]{3,2,1,0:T(8,128)(2,1)S(1)} copy-done((bf16[3,3,256,256]{3,2,1,0:T(8,128)(2,1)S(1)}, bf16[3,3,256,256]{3,2,1,0:T(8,128)(2,1)}, u32[]{:S(2)}) %copy-start.7) | copy-done | bytes 1179672
  15.4 0.0 copy-start.4
  15.4 0.0 copy-start.5
  15.4 5.6 %interior_rows.1 = (bf16[2,16,64,256]{3,2,1,0:T(8,128)(2,1)S(1)}, bf16[2,16,64,768]{3,2,1,0:T(8,128)(2,1)S(1)}, bf16[2,14,64,768]{3,2,1,0:T(8,128)(2,1)S(1)}, f3...) custom-call(bf16[1,16,64,256]{3,2,1,0:T(8,128)(2,1)S(1)} %copy-done., ...), custom_call_target="tpu_custom_call" | custom-call | flops 4200000000 | bytes 6000000 | tf_op jit(solution)/shard_map/interior_rows/pallas_call | solution.py:122
  21.0 0.0 collective-permute-done.chip
  21.0 0.0 collective-permute-done.1.cross
  21.0 0.0 copy-done.4
  21.0 0.0 copy-done.5
  21.0 2.2 %edge_rows.1 = (f32[4,2,64,256]{3,2,1,0:T(8,128)S(1)}, f32[2,384]{1,0:T(2,128)S(1)}, bf16[256,1024]{1,0:T(8,128)(2,1)S(1)}, bf16[256,1024]{1,0:T(8,128)(2,1)S(1)}) custom-call(s32[3]{0:T(128)S(1)} %pad_add_fusion.here, bf16[2,2,64,256]{3,2,1,0:T(8,128)(2,1)S(1)} %collective-permute-done.chip, bf16[2,2,64,256]{3,2,1,0:T(8,128)(2,1)S(1)} %collective-permute-done.1.cross, ...), custom_call_target="tpu_custom_call" | custom-call | flops 1200000000 | bytes 4000000 | tf_op jit(solution)/shard_map/edge_rows/pallas_call | solution.py:183
  23.3 2.5 %psum.7 = bf16[2,384]{1,0:T(2,128)(2,1)S(1)} all-reduce(f32[2,384]{1,0:T(2,128)S(1)} %get-tuple-element.25), channel_id=1, replica_groups={{0,1},{2,3},{4,5},{6,7},{8,9},{10,11},{12,13},{14,15},{16,17},{18,19},{..., use_global_device_ids=true, to_apply=%region_0.0 | all-reduce | flops 768 | bytes 4608 | tf_op jit(solution)/shard_map/psum | solution.py:270
  25.7 0.8 %broadcast_in_dim.12 = bf16[128,2,384]{2,1,0:T(2,128)(2,1)} broadcast(bf16[2,384]{1,0:T(2,128)(2,1)S(1)} %psum.7), dimensions={1,2} | broadcast | bytes 198144 | tf_op jit(solution)/shard_map/broadcast_in_dim | solution.py:272
  26.5 13.7 %all-to-all-start = ((bf16[128,2,384]{2,1,0:T(2,128)(2,1)}), bf16[128,2,384]{2,1,0:T(2,128)(2,1)S(1)}, u32[]{:S(2)}, u32[]{:S(2)}) async-start(bf16[128,2,384]{2,1,0:T(2,128)(2,1)} %broadcast_in_dim.12), calls=%async_computation | async-start | bytes 393216 | tf_op jit(solution)/shard_map/all_to_all | solution.py:273
  40.9 11.0 %all-to-all-done = bf16[128,2,384]{2,1,0:T(2,128)(2,1)S(1)} async-done(((bf16[128,2,384]{2,1,0:T(2,128)(2,1)}), bf16[128,2,384]{2,1,0:T(2,128)(2,1)S(1)}, u32[]{:S(2)}, u32[]{:S(2)}) %all-to-all-start) | async-done | bytes 196640 | tf_op jit(solution)/shard_map/all_to_all | solution.py:273
  51.9 0.2 convert_reduce_fusion
  52.1 3.4 %contrastive_head.1 = (f32[1]{0:T(128)}, f32[256,1024]{1,0:T(8,128)}, f32[256,1024]{1,0:T(8,128)}, f32[2,1,16,64,256]{4,3,2,1,0:T(8,128)}) custom-call(s32[1]{0:T(128)} %bitcast.mine, f32[1]{0:T(128)S(6)} %copy.17.sharp, f32[2,32,384]{2,1,0:T(8,128)S(1)} %fusion.tot, bf16[256,1024]{1,0:T(8,128)(2,1)S(1)} %get-tuple-element.26.sproj, ...), custom_call_target="tpu_custom_call" | custom-call | tf_op jit(solution)/shard_map/contrastive_head/pallas_call | solution.py:247
  (2 shorter events, 0.0 us)
Async XLA Ops:
  1.4 1.0 %copy-start = (bf16[1,16,64,256]{3,2,1,0:T(8,128)(2,1)S(1)}, bf16[1,16,64,256]{3,2,1,0:T(8,128)(2,1)}, u32[]{:S(2)}) copy-start(bf16[1,16,64,256]{3,2,1,0:T(8,128)(2,1)} %s_hbm.3) | copy-start | bytes 1572868
  2.4 1.0 %copy-start.2 = (bf16[1,16,64,256]{3,2,1,0:T(8,128)(2,1)S(1)}, bf16[1,16,64,256]{3,2,1,0:T(8,128)(2,1)}, u32[]{:S(2)}) copy-start(bf16[1,16,64,256]{3,2,1,0:T(8,128)(2,1)} %g_hbm.3) | copy-start | bytes 1572868
  4.4 16.6 %collective-permute-start = (bf16[2,2,64,256]{3,2,1,0:T(8,128)(2,1)S(1)}, bf16[2,2,64,256]{3,2,1,0:T(8,128)(2,1)S(1)}, u32[]{:S(2)}, u32[]{:S(2)}) collective-permute-start(bf16[2,2,64,256]{3,2,1,0:T(8,128)(2,1)S(1)} %get-tuple-element.17), channel_id=1, source_target_pairs={{0,1},{1,0},{2,3},{3,2},{4,5},{5,4},{6,7},{7,6},{8,9},{9,8},{10,11... | collective-permute-start | bytes 393224 | tf_op jit(solution)/shard_map/ppermute | solution.py:266
  7.7 13.3 %collective-permute-start.1 = (bf16[2,2,64,256]{3,2,1,0:T(8,128)(2,1)S(1)}, bf16[2,2,64,256]{3,2,1,0:T(8,128)(2,1)S(1)}, u32[]{:S(2)}, u32[]{:S(2)}) collective-permute-start(bf16[2,2,64,256]{3,2,1,0:T(8,128)(2,1)S(1)} %get-tuple-element.18), channel_id=1, source_target_pairs={{1,2},{2,1},{3,4},{4,3},{5,6},{6,5},{9,10},{10,9},{11,12},{12,11},... | collective-permute-start | bytes 393224 | tf_op jit(solution)/shard_map/ppermute | solution.py:267
  10.8 1.0 %copy-start.1 = (bf16[1,16,64,256]{3,2,1,0:T(8,128)(2,1)S(1)}, bf16[1,16,64,256]{3,2,1,0:T(8,128)(2,1)}, u32[]{:S(2)}) copy-start(bf16[1,16,64,256]{3,2,1,0:T(8,128)(2,1)} %s_hbm.3) | copy-start | bytes 1572868
  11.8 1.0 %copy-start.3 = (bf16[1,16,64,256]{3,2,1,0:T(8,128)(2,1)S(1)}, bf16[1,16,64,256]{3,2,1,0:T(8,128)(2,1)}, u32[]{:S(2)}) copy-start(bf16[1,16,64,256]{3,2,1,0:T(8,128)(2,1)} %g_hbm.3) | copy-start | bytes 1572868
  12.9 1.3 %copy-start.6 = (bf16[3,3,256,256]{3,2,1,0:T(8,128)(2,1)S(1)}, bf16[3,3,256,256]{3,2,1,0:T(8,128)(2,1)}, u32[]{:S(2)}) copy-start(bf16[3,3,256,256]{3,2,1,0:T(8,128)(2,1)} %param.10) | copy-start | bytes 3538948
  14.1 1.3 %copy-start.7 = (bf16[3,3,256,256]{3,2,1,0:T(8,128)(2,1)S(1)}, bf16[3,3,256,256]{3,2,1,0:T(8,128)(2,1)}, u32[]{:S(2)}) copy-start(bf16[3,3,256,256]{3,2,1,0:T(8,128)(2,1)} %param.11) | copy-start | bytes 3538948
  15.4 5.6 %copy-start.4 = (bf16[256,1024]{1,0:T(8,128)(2,1)S(1)}, bf16[256,1024]{1,0:T(8,128)(2,1)}, u32[]{:S(2)}) copy-start(bf16[256,1024]{1,0:T(8,128)(2,1)} %sp_hbm.1) | copy-start | bytes 1572868
  15.4 5.6 %copy-start.5 = (bf16[256,1024]{1,0:T(8,128)(2,1)S(1)}, bf16[256,1024]{1,0:T(8,128)(2,1)}, u32[]{:S(2)}) copy-start(bf16[256,1024]{1,0:T(8,128)(2,1)} %gp_hbm.1) | copy-start | bytes 1572868
  26.5 25.4 %all-to-all-start = ((bf16[128,2,384]{2,1,0:T(2,128)(2,1)}), bf16[128,2,384]{2,1,0:T(2,128)(2,1)S(1)}, u32[]{:S(2)}, u32[]{:S(2)}) async-start(bf16[128,2,384]{2,1,0:T(2,128)(2,1)} %broadcast_in_dim.12), calls=%async_computation | async-start | bytes 393216 | tf_op jit(solution)/shard_map/all_to_all | solution.py:273

commit v3 on v2

--- a/solution.py
+++ b/solution.py
@@ -12,6 +12,10 @@
 HBM = pl.BlockSpec(memory_space=pltpu.MemorySpace.HBM)
 VM = pl.BlockSpec(memory_space=pltpu.MemorySpace.VMEM)
 SM = pl.BlockSpec(memory_space=pltpu.MemorySpace.SMEM)
+
+
+def in_hbm(*arrays):
+    return [pltpu.with_memory_space_constraint(a, pltpu.MemorySpace.HBM) for a in arrays]
 
 
 def pack_kernel(here, s_hbm, g_hbm, chip, cross, sems):
@@ -38,7 +42,7 @@
         out_specs=(VM, VM),
         scratch_shapes=[pltpu.SemaphoreType.DMA((4,))],
         compiler_params=pltpu.CompilerParams(vmem_limit_bytes=2 * MIB),
-    )(here, s, g)
+    )(here, *in_hbm(s, g))
 
 
 def widen(row):
@@ -132,7 +136,7 @@
         scratch_shapes=[pltpu.SemaphoreType.DMA((6,))],
         compiler_params=pltpu.CompilerParams(vmem_limit_bytes=24 * MIB),
         cost_estimate=pl.CostEstimate(flops=4_200_000_000, transcendentals=0, bytes_accessed=6_000_000),
-    )(s, g, w1, w2)
+    )(*in_hbm(s, g, w1, w2))
 
 
 def edge_kernel(here, chip, cross, x, xw, hw, sums, w1, w2, sp_hbm, gp_hbm, o, share, sp, gp, halo, hh, sems):
@@ -193,7 +197,7 @@
         ],
         compiler_params=pltpu.CompilerParams(vmem_limit_bytes=24 * MIB),
         cost_estimate=pl.CostEstimate(flops=1_200_000_000, transcendentals=0, bytes_accessed=4_000_000),
-    )(here, chip, cross, x, xw, hw, sums, w1, w2, sp, gp)
+    )(here, chip, cross, x, xw, hw, sums, w1, w2, *in_hbm(sp, gp))
 
 
 def head_kernel(mine, sharp, tot, sproj, gproj, o, oe, loss_ref, gs_hbm, gg_hbm, out_hbm, buf, sem, osem):

time: 56 us -> 51.3 us (0.916)
  local copies, waits for them, and re-layouts: 7.49 us -> 0.78 us
  Pallas kernels: 12.1 us -> 14.4 us
    unnamed x16 -> x0, local copies, waits for them, and re-layouts: 6.71 us -> none
    pallas_call x1, Pallas kernels: 2.22 us -> 3.21 us  [edges(): pl.pallas_call(edge_kernel, name='edge_rows', out_shape=(jax.ShapeDtypeSt...]
    pallas_call x1, Pallas kernels: 5.57 us -> 6.26 us  [interior(): pl.pallas_call(functools.partial(interior_kernel, step1, step2), name='in...]
    pallas_call x1, Pallas kernels: 0.93 us -> 1.52 us  [pack(): pl.pallas_call(pack_kernel, name='pack_halo_rows', out_shape=(side, side)...]
  transfers between devices with their start and end apart: 3 -> 3, of which waited for: 1 -> 1; matrix products, arithmetic and copies ran while one was open for 0% -> 0% of each run, Pallas kernels for 10% -> 12%
where the time goes in v3:
time: 51.3 us; the launch traced here: 51 us
  starting transfers between devices  20.1 us (39%)
  Pallas kernels  14.4 us (28%)
  waiting for transfers between devices  11 us (21%)
  blocking collectives  2.48 us (5%)
  between operations  2.01 us (4%)
  local copies, waits for them, and re-layouts  0.78 us (2%)
    all_to_all x1, starting transfers between devices, shards(): lax.all_to_all(copies, ('batch', 'strip'), 0, 0, tiled=True, axis_index_g...  13.7 us
    all_to_all x1, waiting for transfers between devices, shards(): lax.all_to_all(copies, ('batch', 'strip'), 0, 0, tiled=True, axis_index_g...  11 us
    pallas_call x1, Pallas kernels, interior(): pl.pallas_call(functools.partial(interior_kernel, step1, step2), name='in...  6.26 us
    pallas_call x1, Pallas kernels, head(): pl.pallas_call(head_kernel, name='contrastive_head', out_shape=(jax.Shape...  3.38 us
    ppermute x1, starting transfers between devices, shards(): chip = lax.ppermute(chip, 'strip', [(i, i ^ 1) for i in range(strips)])  3.33 us
    pallas_call x1, Pallas kernels, edges(): pl.pallas_call(edge_kernel, name='edge_rows', out_shape=(jax.ShapeDtypeSt...  3.21 us
    ppermute x1, starting transfers between devices, shards(): lax.ppermute(cross, 'strip', [(i, i + 2 * (i % 2) - 1) for i in range(1,...  3.06 us
    psum x1, blocking collectives, shards(): lax.psum(share, 'strip', axis_index_groups=[[2 * i, 2 * i + 1] for i in r...  2.48 us
  transfers between devices with their start and end apart: 3, of which 1 were waited for; matrix products, arithmetic and copies ran while one was open for 0% of the time, Pallas kernels for 12%

profile of v3, /device:TPU:1, one launch (start us, length us, event | category | flops | bytes accessed | tf_op | source)
XLA Modules:
  0.0 51.0 jit_solution(17270503694738932195)
XLA Ops:
  1.3 0.1 pad_add_fusion.here
  1.4 1.5 %pack_halo_rows.1 = (bf16[2,2,64,256]{3,2,1,0:T(8,128)(2,1)S(1)}, bf16[2,2,64,256]{3,2,1,0:T(8,128)(2,1)S(1)}) custom-call(s32[3]{0:T(128)S(1)} %pad_add_fusion.here, bf16[1,16,64,256]{3,2,1,0:T(8,128)(2,1)} %s_hbm.3, bf16[1,16,64,256]{3,2,1,0:T(8,128)(2,1)} %g_hbm.3), custom_call_target="tpu_custom_call" | custom-call | tf_op jit(solution)/shard_map/pack_halo_rows/pallas_call | solution.py:37
  2.9 3.3 %collective-permute-start = (bf16[2,2,64,256]{3,2,1,0:T(8,128)(2,1)S(1)}, bf16[2,2,64,256]{3,2,1,0:T(8,128)(2,1)S(1)}, u32[]{:S(2)}, u32[]{:S(2)}) collective-permute-start(bf16[2,2,64,256]{3,2,1,0:T(8,128)(2,1)S(1)} %get-tuple-element.17), channel_id=1, source_target_pairs={{0,1},{1,0},{2,3},{3,2},{4,5},{5,4},{6,7},{7,6},{8,9},{9,8},{10,11... | collective-permute-start | bytes 393224 | tf_op jit(solution)/shard_map/ppermute | solution.py:270
  6.2 3.1 %collective-permute-start.1 = (bf16[2,2,64,256]{3,2,1,0:T(8,128)(2,1)S(1)}, bf16[2,2,64,256]{3,2,1,0:T(8,128)(2,1)S(1)}, u32[]{:S(2)}, u32[]{:S(2)}) collective-permute-start(bf16[2,2,64,256]{3,2,1,0:T(8,128)(2,1)S(1)} %get-tuple-element.18), channel_id=1, source_target_pairs={{1,2},{2,1},{3,4},{4,3},{5,6},{6,5},{9,10},{10,9},{11,12},{12,11},... | collective-permute-start | bytes 393224 | tf_op jit(solution)/shard_map/ppermute | solution.py:271
  9.3 6.3 %interior_rows.1 = (bf16[2,16,64,256]{3,2,1,0:T(8,128)(2,1)S(1)}, bf16[2,16,64,768]{3,2,1,0:T(8,128)(2,1)S(1)}, bf16[2,14,64,768]{3,2,1,0:T(8,128)(2,1)S(1)}, f3...) custom-call(bf16[1,16,64,256]{3,2,1,0:T(8,128)(2,1)} %s_hbm.3, ...), custom_call_target="tpu_custom_call" | custom-call | flops 4200000000 | bytes 6000000 | tf_op jit(solution)/shard_map/interior_rows/pallas_call | solution.py:126
  15.6 0.0 collective-permute-done.chip
  15.6 0.0 collective-permute-done.1.cross
  15.6 3.2 %edge_rows.1 = (f32[4,2,64,256]{3,2,1,0:T(8,128)S(1)}, f32[2,384]{1,0:T(2,128)S(1)}, bf16[256,1024]{1,0:T(8,128)(2,1)S(1)}, bf16[256,1024]{1,0:T(8,128)(2,1)S(1)}) custom-call(s32[3]{0:T(128)S(1)} %pad_add_fusion.here, bf16[2,2,64,256]{3,2,1,0:T(8,128)(2,1)S(1)} %collective-permute-done.chip, bf16[2,2,64,256]{3,2,1,0:T(8,128)(2,1)S(1)} %collective-permute-done.1.cross, ...), custom_call_target="tpu_custom_call" | custom-call | flops 1200000000 | bytes 4000000 | tf_op jit(solution)/shard_map/edge_rows/pallas_call | solution.py:187
  18.8 2.5 %psum.7 = bf16[2,384]{1,0:T(2,128)(2,1)S(1)} all-reduce(f32[2,384]{1,0:T(2,128)S(1)} %get-tuple-element.25), channel_id=1, replica_groups={{0,1},{2,3},{4,5},{6,7},{8,9},{10,11},{12,13},{14,15},{16,17},{18,19},{..., use_global_device_ids=true, to_apply=%region_0.0 | all-reduce | flops 768 | bytes 4608 | tf_op jit(solution)/shard_map/psum | solution.py:274
  21.3 0.8 %broadcast_in_dim.12 = bf16[128,2,384]{2,1,0:T(2,128)(2,1)} broadcast(bf16[2,384]{1,0:T(2,128)(2,1)S(1)} %psum.7), dimensions={1,2} | broadcast | bytes 198144 | tf_op jit(solution)/shard_map/broadcast_in_dim | solution.py:276
  22.1 13.7 %all-to-all-start = ((bf16[128,2,384]{2,1,0:T(2,128)(2,1)}), bf16[128,2,384]{2,1,0:T(2,128)(2,1)S(1)}, u32[]{:S(2)}, u32[]{:S(2)}) async-start(bf16[128,2,384]{2,1,0:T(2,128)(2,1)} %broadcast_in_dim.12), calls=%async_computation | async-start | bytes 393216 | tf_op jit(solution)/shard_map/all_to_all | solution.py:277
  36.4 11.0 %all-to-all-done = bf16[128,2,384]{2,1,0:T(2,128)(2,1)S(1)} async-done(((bf16[128,2,384]{2,1,0:T(2,128)(2,1)}), bf16[128,2,384]{2,1,0:T(2,128)(2,1)S(1)}, u32[]{:S(2)}, u32[]{:S(2)}) %all-to-all-start) | async-done | bytes 196640 | tf_op jit(solution)/shard_map/all_to_all | solution.py:277
  47.5 0.2 convert_reduce_fusion
  47.7 3.4 %contrastive_head.1 = (f32[1]{0:T(128)}, f32[256,1024]{1,0:T(8,128)}, f32[256,1024]{1,0:T(8,128)}, f32[2,1,16,64,256]{4,3,2,1,0:T(8,128)}) custom-call(s32[1]{0:T(128)} %bitcast.mine, f32[1]{0:T(128)S(6)} %copy.17.sharp, f32[2,32,384]{2,1,0:T(8,128)S(1)} %fusion.tot, bf16[256,1024]{1,0:T(8,128)(2,1)S(1)} %get-tuple-element.26.sproj, ...), custom_call_target="tpu_custom_call" | custom-call | tf_op jit(solution)/shard_map/contrastive_head/pallas_call | solution.py:251
  (2 shorter events, 0.0 us)
Async XLA Ops:
  2.9 12.7 %collective-permute-start = (bf16[2,2,64,256]{3,2,1,0:T(8,128)(2,1)S(1)}, bf16[2,2,64,256]{3,2,1,0:T(8,128)(2,1)S(1)}, u32[]{:S(2)}, u32[]{:S(2)}) collective-permute-start(bf16[2,2,64,256]{3,2,1,0:T(8,128)(2,1)S(1)} %get-tuple-element.17), channel_id=1, source_target_pairs={{0,1},{1,0},{2,3},{3,2},{4,5},{5,4},{6,7},{7,6},{8,9},{9,8},{10,11... | collective-permute-start | bytes 393224 | tf_op jit(solution)/shard_map/ppermute | solution.py:270
  6.2 9.4 %collective-permute-start.1 = (bf16[2,2,64,256]{3,2,1,0:T(8,128)(2,1)S(1)}, bf16[2,2,64,256]{3,2,1,0:T(8,128)(2,1)S(1)}, u32[]{:S(2)}, u32[]{:S(2)}) collective-permute-start(bf16[2,2,64,256]{3,2,1,0:T(8,128)(2,1)S(1)} %get-tuple-element.18), channel_id=1, source_target_pairs={{1,2},{2,1},{3,4},{4,3},{5,6},{6,5},{9,10},{10,9},{11,12},{12,11},... | collective-permute-start | bytes 393224 | tf_op jit(solution)/shard_map/ppermute | solution.py:271
  22.1 25.4 %all-to-all-start = ((bf16[128,2,384]{2,1,0:T(2,128)(2,1)}), bf16[128,2,384]{2,1,0:T(2,128)(2,1)S(1)}, u32[]{:S(2)}, u32[]{:S(2)}) async-start(bf16[128,2,384]{2,1,0:T(2,128)(2,1)} %broadcast_in_dim.12), calls=%async_computation | async-start | bytes 393216 | tf_op jit(solution)/shard_map/all_to_all | solution.py:277

commit v4 on v3

v4 whole, which is shorter than its diff:
```python
import functools
import jax
import jax.numpy as jnp
from jax import lax
from jax.experimental import pallas as pl
from jax.experimental.pallas import tpu as pltpu
from jax.sharding import PartitionSpec as P

ROWS, COLS, C, E = 16, 64, 256, 1024
BF, F32 = jnp.bfloat16, jnp.float32
MIB = 1 << 20
HBM = pl.BlockSpec(memory_space=pltpu.MemorySpace.HBM)
VM = pl.BlockSpec(memory_space=pltpu.MemorySpace.VMEM)
SM = pl.BlockSpec(memory_space=pltpu.MemorySpace.SMEM)


def in_hbm(*arrays):
    return [pltpu.with_memory_space_constraint(a, pltpu.MemorySpace.HBM) for a in arrays]


def load_kernel(s_hbm, g_hbm, w1_hbm, chip, cross, x, w1, sems):
    odd = lax.rem(lax.axis_index("strip"), 2)
    copies = []
    for f, ref in enumerate((s_hbm, g_hbm)):
        tail = (ROWS - 2) * (1 - odd)
        head = (ROWS - 2) * odd
        copies.append((ref.at[0, pl.ds(tail, 2)], chip.at[f]))
        copies.append((ref.at[0, pl.ds(head, 2)], cross.at[f]))
    for f, ref in enumerate((s_hbm, g_hbm)):
        copies.append((ref.at[0], x.at[f]))
    for dy in range(3):
        copies.append((w1_hbm.at[dy], w1.at[dy]))
    copies = [pltpu.make_async_copy(a, b, sems.at[k]) for k, (a, b) in enumerate(copies)]
    for cp in copies:
        cp.start()
    for cp in copies:
        cp.wait()


def load(s, g, w1):
    side = jax.ShapeDtypeStruct((2, 2, COLS, C), BF)
    return pl.pallas_call(
        load_kernel,
        name="load_rows",
        out_shape=(side, side, jax.ShapeDtypeStruct((2, ROWS, COLS, C), BF), jax.ShapeDtypeStruct(w1.shape, BF)),
        in_specs=[HBM] * 3,
        out_specs=(VM,) * 4,
        scratch_shapes=[pltpu.SemaphoreType.DMA((9,))],
        compiler_params=pltpu.CompilerParams(vmem_limit_bytes=8 * MIB),
    )(*in_hbm(s, g, w1))


def widen(row):
    col = lax.broadcasted_iota(jnp.int32, row.shape, 0)
    left = jnp.where(col == 0, 0.0, pltpu.roll(row, 1, 0))
    right = jnp.where(col == COLS - 1, 0.0, pltpu.roll(row, COLS - 1, 0))
    return jnp.concatenate([left.astype(BF), row.astype(BF), right.astype(BF)], axis=-1)


def conv(wide, first, rows, weights):
    total = None
    for dy in range(3):
        lhs = wide[pl.ds(first + dy, rows)].reshape(rows * COLS, 3 * C)
        part = jnp.dot(lhs, weights[dy], preferred_element_type=F32)
        total = part if total is None else total + part
    return total


def conv_of(rows, weights):
    total = None
    for dy in range(3):
        lhs = jnp.concatenate([rows[dy], rows[dy + 1]], axis=0)
        part = jnp.dot(lhs, weights[dy], preferred_element_type=F32)
        total = part if total is None else total + part
    return total


def spans(total, step):
    return [(r, min(step, total - r)) for r in range(0, total, step)]


def interior_kernel(step1, step2, x, w1, w2_hbm, sp_hbm, gp_hbm, xw, hw, o, sum_ref, w2, sp, gp, sems):
    cw2 = pltpu.make_async_copy(w2_hbm, w2, sems.at[0])
    csp = pltpu.make_async_copy(sp_hbm, sp, sems.at[1])
    cgp = pltpu.make_async_copy(gp_hbm, gp, sems.at[2])
    cw2.start(); csp.start(); cgp.start()

    def spread(f, rows):
        for r in rows:
            xw[f, r] = widen(jnp.maximum(x[f, r].astype(F32), 0.0))

    def first(f, r, n):
        h = jnp.maximum(conv(xw.at[f], r, n, w1), 0.0)
        for k in range(n):
            hw[f, r + k] = widen(h[k * COLS:(k + 1) * COLS])

    def second(f, r, n, acc):
        y = conv(hw.at[f], r, n, w2)
        y = jnp.maximum(y + x[f, r + 2:r + 2 + n].reshape(n * COLS, C).astype(F32), 0.0)
        o[f, r:r + n] = y.reshape(n, COLS, C)
        part = jnp.sum(y.reshape(n * COLS // 8, 8, C), axis=0)
        return part if acc is None else acc + part

    spread(0, range(step1 + 2))
    plan = spans(14, step1)
    done = step1 + 2
    for i, (r, n) in enumerate(plan):
        if i + 1 < len(plan):
            upto = plan[i + 1][0] + plan[i + 1][1] + 2
            spread(0, range(done, upto))
            done = upto
        first(0, r, n)
    cw2.wait()
    acc = None
    plan = spans(12, step2)
    for i, (r, n) in enumerate(plan):
        spread(1, range(i * 16 // len(plan), (i + 1) * 16 // len(plan)))
        acc = second(0, r, n, acc)
    sum_ref[0] = acc
    for r, n in spans(14, step1):
        first(1, r, n)
    acc = None
    for r, n in spans(12, step2):
        acc = second(1, r, n, acc)
    sum_ref[1] = acc
    csp.wait(); cgp.wait()


def interior(x, w1, w2, sp, gp, step1=7, step2=6):
    proj = jax.ShapeDtypeStruct((C, E), BF)
    return pl.pallas_call(
        functools.partial(interior_kernel, step1, step2),
        name="interior_rows",
        out_shape=(jax.ShapeDtypeStruct((2, ROWS, COLS, 3 * C), BF),
                   jax.ShapeDtypeStruct((2, 14, COLS, 3 * C), BF),
                   jax.ShapeDtypeStruct((2, 12, COLS, C), F32),
                   jax.ShapeDtypeStruct((2, 8, C), F32), jax.ShapeDtypeStruct(w2.shape, BF), proj, proj),
        in_specs=[VM] * 2 + [HBM] * 3,
        out_specs=(VM,) * 7,
        scratch_shapes=[pltpu.SemaphoreType.DMA((3,))],
        compiler_params=pltpu.CompilerParams(vmem_limit_bytes=24 * MIB),
        cost_estimate=pl.CostEstimate(flops=4_200_000_000, transcendentals=0, bytes_accessed=6_000_000),
    )(x, w1, *in_hbm(w2, sp, gp))


def edge_kernel(label, chip, cross, x, xw, hw, sums, w1, w2, o, copies, halo, hh):
    here, strips = lax.axis_index("strip"), lax.axis_size("strip")
    odd = lax.rem(here, 2)
    for f in range(2):
        for r in range(2):
            halo[2 * f + 1 - odd, r] = widen(jnp.maximum(chip[f, r].astype(F32), 0.0))
            halo[2 * f + odd, r] = widen(jnp.maximum(cross[f, r].astype(F32), 0.0))
    for k in range(4):
        f = k // 2
        if k % 2 == 0:
            rows = [halo[k, 0], halo[k, 1], xw[f, 0], xw[f, 1]]
        else:
            rows = [xw[f, ROWS - 2], xw[f, ROWS - 1], halo[k, 0], halo[k, 1]]
        h = jnp.maximum(conv_of(rows, w1), 0.0)
        for r in range(2):
            row = h[r * COLS:(r + 1) * COLS]
            if k % 2 == 0 and r == 0:
                row = jnp.where(here > 0, row, 0.0)
            if k % 2 == 1 and r == 1:
                row = jnp.where(here < strips - 1, row, 0.0)
            hh[k, r] = widen(row)
    tot = [sums[0], sums[1]]
    for k in range(4):
        f = k // 2
        if k % 2 == 0:
            rows = [hh[k, 0], hh[k, 1], hw[f, 0], hw[f, 1]]
        else:
            rows = [hw[f, 12], hw[f, 13], hh[k, 0], hh[k, 1]]
        y = conv_of(rows, w2)
        y = jnp.maximum(y + x[f, 14 * (k % 2):14 * (k % 2) + 2].reshape(2 * COLS, C).astype(F32), 0.0)
        o[k] = y.reshape(2, COLS, C)
        tot[f] = tot[f] + jnp.sum(y.reshape(16, 8, C), axis=0)
    scale = 1.0 / (strips * ROWS * COLS)
    mark = jnp.full((1, 128), label[0], jnp.int32).astype(F32) * (1.0 / strips)
    for f in range(2):
        row = jnp.concatenate([jnp.sum(tot[f], axis=0, keepdims=True) * scale, mark], axis=1)
        for n in range(copies.shape[0]):
            copies[n, f:f + 1] = row


def edges(label, chip, cross, x, xw, hw, sums, w1, w2, members):
    return pl.pallas_call(
        edge_kernel,
        name="edge_rows",
        out_shape=(jax.ShapeDtypeStruct((4, 2, COLS, C), F32), jax.ShapeDtypeStruct((members, 2, C + 128), F32)),
        in_specs=[SM] + [VM] * 8,
        out_specs=(VM,) * 2,
        scratch_shapes=[
            pltpu.VMEM((4, 2, COLS, 3 * C), BF),
            pltpu.VMEM((4, 2, COLS, 3 * C), BF),
        ],
        compiler_params=pltpu.CompilerParams(vmem_limit_bytes=24 * MIB),
        cost_estimate=pl.CostEstimate(flops=1_200_000_000, transcendentals=0, bytes_accessed=4_000_000),
    )(label, chip, cross, x, xw, hw, sums, w1, w2)


def write_kernel(o, oe, out_hbm, sems):
    outs = []
    for f in range(2):
        outs.append(pltpu.make_async_copy(o.at[f], out_hbm.at[f, 0, pl.ds(2, 12)], sems.at[3 * f]))
        for k in range(2):
            outs.append(pltpu.make_async_copy(oe.at[2 * f + k], out_hbm.at[f, 0, pl.ds(14 * k, 2)], sems.at[3 * f + 1 + k]))
    for cp in outs:
        cp.start()
    for cp in outs:
        cp.wait()


def write(o, oe):
    return pl.pallas_call(
        write_kernel,
        name="write_maps",
        out_shape=jax.ShapeDtypeStruct((2, 1, ROWS, COLS, C), F32),
        in_specs=[VM] * 2,
        out_specs=HBM,
        scratch_shapes=[pltpu.SemaphoreType.DMA((6,))],
        compiler_params=pltpu.CompilerParams(vmem_limit_bytes=2 * MIB),
        cost_estimate=pl.CostEstimate(flops=0, transcendentals=0, bytes_accessed=4_000_000),
    )(o, oe)


def head_kernel(sharp, tot, sproj, gproj, loss_ref, gs_hbm, gg_hbm, buf, sem):
    pairs = tot.shape[1]
    s_pool = tot[0, :, :C].astype(BF)
    g_pool = tot[1, :, :C].astype(BF)
    label = tot[0, :, C:C + 1]
    temp = sharp[0]
    s_emb = jnp.dot(s_pool, sproj[...], preferred_element_type=F32)
    g_emb = jnp.dot(g_pool, gproj[...], preferred_element_type=F32)
    s_inv = lax.rsqrt(jnp.sum(s_emb * s_emb, axis=-1, keepdims=True) + 1e-06)
    g_inv = lax.rsqrt(jnp.sum(g_emb * g_emb, axis=-1, keepdims=True) + 1e-06)
    s_unit = s_emb * s_inv
    g_unit = g_emb * g_inv
    s_bf = s_unit.astype(BF)
    g_bf = g_unit.astype(BF)
    logits = temp * lax.dot_general(s_bf, g_bf, (((1,), (1,)), ((), ())), preferred_element_type=F32)
    ex = jnp.exp(logits)
    row_total = jnp.sum(ex, axis=1, keepdims=True)
    column = lax.broadcasted_iota(jnp.int32, (pairs, pairs), 1).astype(F32)
    matched = column == label
    positive = jnp.sum(jnp.where(matched, logits, 0.0), axis=1, keepdims=True)
    losses = jnp.log(row_total) - positive
    row = lax.broadcasted_iota(jnp.int32, (pairs, 1), 0)
    lgrad = (ex / row_total - jnp.where(matched, 1.0, 0.0)).astype(BF)
    s_ug = temp * jnp.dot(lgrad, g_bf, preferred_element_type=F32)
    g_ug = temp * lax.dot_general(lgrad, s_bf, (((0,), (0,)), ((), ())), preferred_element_type=F32)
    s_eg = ((s_ug - s_unit * jnp.sum(s_unit * s_ug, axis=-1, keepdims=True)) * s_inv).astype(BF)
    g_eg = ((g_ug - g_unit * jnp.sum(g_unit * g_ug, axis=-1, keepdims=True)) * g_inv).astype(BF)
    outs = []
    for k, (pool, grad, dest) in enumerate(((s_pool, s_eg, gs_hbm), (g_pool, g_eg, gg_hbm))):
        for p in range(2):
            half = pl.ds(p * (C // 2), C // 2)
            buf[k, half] = lax.dot_general(pool[:, p * (C // 2):(p + 1) * (C // 2)], grad, (((0,), (0,)), ((), ())),
                                           preferred_element_type=F32)
            cp = pltpu.make_async_copy(buf.at[k, half], dest.at[half], sem.at[2 * k + p])
            cp.start()
            outs.append(cp)
    loss_ref[0] = jnp.sum(jnp.where(row == lax.axis_index("batch"), losses, 0.0))
    for cp in outs:
        cp.wait()


def head(sharp, tot, sproj, gproj):
    return pl.pallas_call(
        head_kernel,
        name="contrastive_head",
        out_shape=(jax.ShapeDtypeStruct((1,), F32), jax.ShapeDtypeStruct((C, E), F32),
                   jax.ShapeDtypeStruct((C, E), F32)),
        in_specs=[SM] + [VM] * 3,
        out_specs=(SM, HBM, HBM),
        scratch_shapes=[pltpu.VMEM((2, C, E), F32), pltpu.SemaphoreType.DMA((4,))],
        compiler_params=pltpu.CompilerParams(vmem_limit_bytes=16 * MIB),
    )(sharp, tot, sproj, gproj)


def gather_groups(batch, strips, inner):
    lines = {}
    for b in range(batch):
        for s in range(strips):
            half, plane = divmod(b, batch // 2)
            lines.setdefault(plane if inner else (half, s), []).append(b * strips + s)
    return list(lines.values())


def shards(state_maps, goal_maps, conv_one, conv_two, state_proj, goal_proj, inv_temp, pair_index):
    strips, batch = lax.axis_size("strip"), lax.axis_size("batch")
    w1 = conv_one.reshape(3, 3 * C, C)
    w2 = conv_two.reshape(3, 3 * C, C)
    chip, cross, x, w1 = load(state_maps, goal_maps, w1)
    chip = lax.ppermute(chip, "strip", [(i, i ^ 1) for i in range(strips)])
    cross = lax.ppermute(cross, "strip", [(i, i + 2 * (i % 2) - 1) for i in range(1, strips - 1)])
    xw, hw, o, sums, w2, sp, gp = interior(x, w1, w2, state_proj, goal_proj)
    oe, copies = edges(pair_index, chip, cross, x, xw, hw, sums, w1, w2, 2 * strips)
    both = ("batch", "strip")
    line = lax.all_to_all(copies, both, 0, 0, tiled=True, axis_index_groups=gather_groups(batch, strips, True))
    means = jnp.sum(line.reshape(2, strips, 2, C + 128), axis=1).astype(BF).reshape(4, C + 128)
    copies = jnp.broadcast_to(means, (batch // 2, 4, C + 128))
    got = lax.all_to_all(copies, both, 0, 0, tiled=True, axis_index_groups=gather_groups(batch, strips, False))
    tot = jnp.transpose(got.reshape(batch // 2, 2, 2, C + 128).astype(F32), (2, 1, 0, 3)).reshape(2, batch, C + 128)
    out = write(o, oe)
    loss, gs, gg = head(inv_temp, tot, sp, gp)
    return loss, gs, gg, out


def solution(mesh):
    placed = (
        P("batch", "strip", None, None),
        P("batch", "strip", None, None),
        P(),
        P(),
        P(),
        P(),
        P(),
        P("batch"),
    )
    return jax.shard_map(
        shards,
        mesh=mesh,
        in_specs=placed,
        out_specs=(P("batch"), P(), P(), P(None, "batch", "strip", None, None)),
        check_vma=False,
    )
```

time: 51.3 us -> 47.9 us (0.934)
  blocking collectives: 2.48 us -> 14.9 us
  starting transfers between devices: 20.1 us -> 13.1 us
  waiting for transfers between devices: 11 us -> 4.49 us
  Pallas kernels: 14.4 us -> 12.3 us
    all_to_all x0 -> x1, blocking collectives: none -> 14.9 us  [shards(): lax.all_to_all(copies, both, 0, 0, tiled=True, axis_index_groups=gather_g...]
    all_to_all x1, starting transfers between devices: 13.7 us -> 6.76 us  [shards(): lax.all_to_all(copies, both, 0, 0, tiled=True, axis_index_groups=gather_g...]
    all_to_all x1, waiting for transfers between devices: 11 us -> 4.48 us  [shards(): lax.all_to_all(copies, both, 0, 0, tiled=True, axis_index_groups=gather_g...]
    psum x1 -> x0, blocking collectives: 2.48 us -> none  [shards(): lax.psum(share, 'strip', axis_index_groups=[[2 * i, 2 * i + 1] for i in r...]
    pallas_call x1, Pallas kernels: 3.21 us -> 1.53 us  [edges(): pl.pallas_call(edge_kernel, name='edge_rows', out_shape=(jax.ShapeDtypeSt...]
    pallas_call x1 -> x2, Pallas kernels: 1.52 us -> 3.14 us  [the longest x1 1.78 us: load(): pl.pallas_call(load_kernel, name='load_rows', out_shape=(side, side, jax....]
    pallas_call x1, Pallas kernels: 6.26 us -> 4.74 us  [interior(): pl.pallas_call(functools.partial(interior_kernel, step1, step2), name='in...]
  transfers between devices with their start and end apart: 3 -> 3, of which waited for: 1 -> 1; matrix products, arithmetic and copies ran while one was open for 0% -> 0% of each run, Pallas kernels for 12% -> 13%
where the time goes in v4:
time: 47.9 us; the launch traced here: 47.6 us
  blocking collectives  14.9 us (31%)
  starting transfers between devices  13.1 us (27%)
  Pallas kernels  12.3 us (26%)
  waiting for transfers between devices  4.49 us (9%)
  between operations  2.01 us (4%)
  local copies, waits for them, and re-layouts  0.68 us (1%)
    all_to_all x1, blocking collectives, shards(): lax.all_to_all(copies, both, 0, 0, tiled=True, axis_index_groups=gather_g...  14.9 us
    all_to_all x1, starting transfers between devices, shards(): lax.all_to_all(copies, both, 0, 0, tiled=True, axis_index_groups=gather_g...  6.76 us
    pallas_call x1, Pallas kernels, interior(): pl.pallas_call(functools.partial(interior_kernel, step1, step2), name='in...  4.74 us
    all_to_all x1, waiting for transfers between devices, shards(): lax.all_to_all(copies, both, 0, 0, tiled=True, axis_index_groups=gather_g...  4.48 us
    ppermute x1, starting transfers between devices, shards(): chip = lax.ppermute(chip, 'strip', [(i, i ^ 1) for i in range(strips)])  3.33 us
    ppermute x1, starting transfers between devices, shards(): lax.ppermute(cross, 'strip', [(i, i + 2 * (i % 2) - 1) for i in range(1,...  3.06 us
    pallas_call x1, Pallas kernels, head(): pl.pallas_call(head_kernel, name='contrastive_head', out_shape=(jax.Shape...  2.94 us
    pallas_call x1, Pallas kernels, load(): pl.pallas_call(load_kernel, name='load_rows', out_shape=(side, side, jax....  1.78 us
  transfers between devices with their start and end apart: 3, of which 1 were waited for; matrix products, arithmetic and copies ran while one was open for 0% of the time, Pallas kernels for 13%

profile of v4, /device:TPU:1, one launch (start us, length us, event | category | flops | bytes accessed | tf_op | source)
XLA Modules:
  0.0 47.6 jit_solution(12433047667269813838)
XLA Ops:
  0.6 1.8 %load_rows.1 = (bf16[2,2,64,256]{3,2,1,0:T(8,128)(2,1)S(1)}, bf16[2,2,64,256]{3,2,1,0:T(8,128)(2,1)S(1)}, bf16[2,16,64,256]{3,2,1,0:T(8,128)(2,1)S(1)}, bf16[3,768,256]{2,1,0:T(8,128)(2,1)S(1)}) custom-call(bf16[1,16,64,256]{3,2,1,0:T(8,128)(2,1)} %s_hbm.1, bf16[1,16,64,256]{3,2,1,0:T(8,128)(2,1)} %g_hbm.1, bf16[3,768,256]{2,1,0:T(8,128)(2,1)} %bitcast.10), custom_call_target="tpu_custom_call" | custom-call | tf_op jit(solution)/shard_map/load_rows/pallas_call | solution.py:42
  2.4 3.3 %collective-permute-start = (bf16[2,2,64,256]{3,2,1,0:T(8,128)(2,1)S(1)}, bf16[2,2,64,256]{3,2,1,0:T(8,128)(2,1)S(1)}, u32[]{:S(2)}, u32[]{:S(2)}) collective-permute-start(bf16[2,2,64,256]{3,2,1,0:T(8,128)(2,1)S(1)} %get-tuple-element.20), channel_id=1, source_target_pairs={{0,1},{1,0},{2,3},{3,2},{4,5},{5,4},{6,7},{7,6},{8,9},{9,8},{10,11... | collective-permute-start | bytes 393224 | tf_op jit(solution)/shard_map/ppermute | solution.py:295
  5.7 3.1 %collective-permute-start.1 = (bf16[2,2,64,256]{3,2,1,0:T(8,128)(2,1)S(1)}, bf16[2,2,64,256]{3,2,1,0:T(8,128)(2,1)S(1)}, u32[]{:S(2)}, u32[]{:S(2)}) collective-permute-start(bf16[2,2,64,256]{3,2,1,0:T(8,128)(2,1)S(1)} %get-tuple-element.21), channel_id=1, source_target_pairs={{1,2},{2,1},{3,4},{4,3},{5,6},{6,5},{9,10},{10,9},{11,12},{12,11},... | collective-permute-start | bytes 393224 | tf_op jit(solution)/shard_map/ppermute | solution.py:296
  8.8 4.7 %interior_rows.1 = (bf16[2,16,64,768]{3,2,1,0:T(8,128)(2,1)S(1)}, bf16[2,14,64,768]{3,2,1,0:T(8,128)(2,1)S(1)}, f32[2,12,64,256]{3,2,1,0:T(8,128)S(1)}, f32[2,8,...) custom-call(bf16[2,16,64,256]{3,2,1,0:T(8,128)(2,1)S(1)} %get-tuple-, ...), custom_call_target="tpu_custom_call" | custom-call | flops 4200000000 | bytes 6000000 | tf_op jit(solution)/shard_map/interior_rows/pallas_call | solution.py:131
  14.2 0.0 collective-permute-done.chip
  14.2 0.0 collective-permute-done.1.cross
  14.2 1.5 %edge_rows.1 = (f32[4,2,64,256]{3,2,1,0:T(8,128)S(1)}, f32[16,2,384]{2,1,0:T(2,128)S(1)}) custom-call(s32[1]{0:T(128)S(6)} %copy.16.label, bf16[2,2,64,256]{3,2,1,0:T(8,128)(2,1)S(1)} %collective-permute-done.chip, bf16[2,2,64,256]{3,2,1,0:T(8,128)(2,1)S(1)} %collective-permute-done.1.cross, bf16[2,16,64,256]{3,2,1,0:T(8,128)(2,1)S(1)} %get-tuple-element.22.x, ...), custom_call_target="tpu_custom_call" | custom-call | flops 1200000000 | bytes 4000000 | tf_op jit(solution)/shard_map/edge_rows/pallas_call | solution.py:187
  15.8 14.9 %all_to_all.10 = f32[16,2,384]{2,1,0:T(2,128)S(1)} all-to-all(f32[16,2,384]{2,1,0:T(2,128)S(1)} %get-tuple-element.28), channel_id=1, replica_groups={{0,1,2,3,4,5,6,7,128,129,130,131,132,133,134,135},{8,9,10,11,12,13,14,1..., dimensions={0} | all-to-all | bytes 98304 | tf_op jit(solution)/shard_map/all_to_all | solution.py:300
  30.7 0.6 %broadcast_in_dim.3 = bf16[16,4,384]{2,1,0:T(4,128)(2,1)} broadcast(bf16[4,384]{1,0:T(4,128)(2,1)S(1)} %convert_element_type.12), dimensions={1,2} | broadcast | bytes 52224 | tf_op jit(solution)/shard_map/broadcast_in_dim | solution.py:302
  31.3 6.8 %all-to-all-start.1 = ((bf16[16,4,384]{2,1,0:T(4,128)(2,1)}), bf16[16,4,384]{2,1,0:T(4,128)(2,1)S(1)}, u32[]{:S(2)}, u32[]{:S(2)}) async-start(bf16[16,4,384]{2,1,0:T(4,128)(2,1)} %broadcast_in_dim.3), calls=%async_computation.1 | async-start | bytes 98304 | tf_op jit(solution)/shard_map/all_to_all | solution.py:303
  38.8 1.4 %write_maps.1 = f32[2,1,16,64,256]{4,3,2,1,0:T(8,128)} custom-call(f32[2,12,64,256]{3,2,1,0:T(8,128)S(1)} %get-tuple-element.34.o, f32[4,2,64,256]{3,2,1,0:T(8,128)S(1)} %get-tuple-element.35.oe), custom_call_target="tpu_custom_call" | custom-call | bytes 4000000 | tf_op jit(solution)/shard_map/write_maps/pallas_call | solution.py:215
  40.1 4.5 %all-to-all-done.1 = bf16[16,4,384]{2,1,0:T(4,128)(2,1)S(1)} async-done(((bf16[16,4,384]{2,1,0:T(4,128)(2,1)}), bf16[16,4,384]{2,1,0:T(4,128)(2,1)S(1)}, u32[]{:S(2)}, u32[]{:S(2)}) %all-to-all-start.1) | async-done | bytes 49184 | tf_op jit(solution)/shard_map/all_to_all | solution.py:303
  44.7 2.9 %contrastive_head.1 = (f32[1]{0:T(128)}, f32[256,1024]{1,0:T(8,128)}, f32[256,1024]{1,0:T(8,128)}) custom-call(f32[1]{0:T(128)S(6)} %copy.15.sharp, f32[2,32,384]{2,1,0:T(8,128)S(1)} %bitcast.9, bf16[256,1024]{1,0:T(8,128)(2,1)S(1)} %get-tuple-element.29.sproj, bf16[256,1024]{1,0:T(8,128)(2,1)S(1)} %get-tuple-element.30.gproj), custom_call_target="tpu_custom_call" | custom-call | tf_op jit(solution)/shard_map/contrastive_head/pallas_call | solution.py:269
  (5 shorter events, 0.1 us)
Async XLA Ops:
  2.4 11.8 %collective-permute-start = (bf16[2,2,64,256]{3,2,1,0:T(8,128)(2,1)S(1)}, bf16[2,2,64,256]{3,2,1,0:T(8,128)(2,1)S(1)}, u32[]{:S(2)}, u32[]{:S(2)}) collective-permute-start(bf16[2,2,64,256]{3,2,1,0:T(8,128)(2,1)S(1)} %get-tuple-element.20), channel_id=1, source_target_pairs={{0,1},{1,0},{2,3},{3,2},{4,5},{5,4},{6,7},{7,6},{8,9},{9,8},{10,11... | collective-permute-start | bytes 393224 | tf_op jit(solution)/shard_map/ppermute | solution.py:295
  5.7 8.5 %collective-permute-start.1 = (bf16[2,2,64,256]{3,2,1,0:T(8,128)(2,1)S(1)}, bf16[2,2,64,256]{3,2,1,0:T(8,128)(2,1)S(1)}, u32[]{:S(2)}, u32[]{:S(2)}) collective-permute-start(bf16[2,2,64,256]{3,2,1,0:T(8,128)(2,1)S(1)} %get-tuple-element.21), channel_id=1, source_target_pairs={{1,2},{2,1},{3,4},{4,3},{5,6},{6,5},{9,10},{10,9},{11,12},{12,11},... | collective-permute-start | bytes 393224 | tf_op jit(solution)/shard_map/ppermute | solution.py:296
  31.3 13.3 %all-to-all-start.1 = ((bf16[16,4,384]{2,1,0:T(4,128)(2,1)}), bf16[16,4,384]{2,1,0:T(4,128)(2,1)S(1)}, u32[]{:S(2)}, u32[]{:S(2)}) async-start(bf16[16,4,384]{2,1,0:T(4,128)(2,1)} %broadcast_in_dim.3), calls=%async_computation.1 | async-start | bytes 98304 | tf_op jit(solution)/shard_map/all_to_all | solution.py:303

commit v5 on v4

--- a/solution.py
+++ b/solution.py
@@ -18,18 +18,33 @@
     return [pltpu.with_memory_space_constraint(a, pltpu.MemorySpace.HBM) for a in arrays]
 
 
-def load_kernel(s_hbm, g_hbm, w1_hbm, chip, cross, x, w1, sems):
+def pack_kernel(s_hbm, g_hbm, cross, sems):
     odd = lax.rem(lax.axis_index("strip"), 2)
-    copies = []
-    for f, ref in enumerate((s_hbm, g_hbm)):
-        tail = (ROWS - 2) * (1 - odd)
-        head = (ROWS - 2) * odd
-        copies.append((ref.at[0, pl.ds(tail, 2)], chip.at[f]))
-        copies.append((ref.at[0, pl.ds(head, 2)], cross.at[f]))
-    for f, ref in enumerate((s_hbm, g_hbm)):
-        copies.append((ref.at[0], x.at[f]))
-    for dy in range(3):
-        copies.append((w1_hbm.at[dy], w1.at[dy]))
+    copies = [pltpu.make_async_copy(ref.at[0, pl.ds((ROWS - 2) * odd, 2)], cross.at[f], sems.at[f])
+              for f, ref in enumerate((s_hbm, g_hbm))]
+    for cp in copies:
+        cp.start()
+    for cp in copies:
+        cp.wait()
+
+
+def pack(s, g):
+    return pl.pallas_call(
+        pack_kernel,
+        name="pack_rows",
+        out_shape=jax.ShapeDtypeStruct((2, 2, COLS, C), BF),
+        in_specs=[HBM] * 2,
+        out_specs=VM,
+        scratch_shapes=[pltpu.SemaphoreType.DMA((2,))],
+        compiler_params=pltpu.CompilerParams(vmem_limit_bytes=2 * MIB),
+    )(*in_hbm(s, g))
+
+
+def load_kernel(s_hbm, g_hbm, w1_hbm, packed, chip, x, w1, sems):
+    odd = lax.rem(lax.axis_index("strip"), 2)
+    copies = [(ref.at[0, pl.ds((ROWS - 2) * (1 - odd), 2)], chip.at[f]) for f, ref in enumerate((s_hbm, g_hbm))]
+    copies += [(ref.at[0], x.at[f]) for f, ref in enumerate((s_hbm, g_hbm))]
+    copies += [(w1_hbm.at[dy], w1.at[dy]) for dy in range(3)]
     copies = [pltpu.make_async_copy(a, b, sems.at[k]) for k, (a, b) in enumerate(copies)]
     for cp in copies:
         cp.start()
@@ -37,17 +52,17 @@
         cp.wait()
 
 
-def load(s, g, w1):
-    side = jax.ShapeDtypeStruct((2, 2, COLS, C), BF)
+def load(s, g, w1, packed):
     return pl.pallas_call(
         load_kernel,
         name="load_rows",
-        out_shape=(side, side, jax.ShapeDtypeStruct((2, ROWS, COLS, C), BF), jax.ShapeDtypeStruct(w1.shape, BF)),
-        in_specs=[HBM] * 3,
-        out_specs=(VM,) * 4,
-        scratch_shapes=[pltpu.SemaphoreType.DMA((9,))],
+        out_shape=(jax.ShapeDtypeStruct((2, 2, COLS, C), BF), jax.ShapeDtypeStruct((2, ROWS, COLS, C), BF),
+                   jax.ShapeDtypeStruct(w1.shape, BF)),
+        in_specs=[HBM] * 3 + [VM],
+        out_specs=(VM,) * 3,
+        scratch_shapes=[pltpu.SemaphoreType.DMA((7,))],
         compiler_params=pltpu.CompilerParams(vmem_limit_bytes=8 * MIB),
-    )(*in_hbm(s, g, w1))
+    )(*in_hbm(s, g, w1), packed)
 
 
 def widen(row):
@@ -126,7 +141,7 @@
     csp.wait(); cgp.wait()
 
 
-def interior(x, w1, w2, sp, gp, step1=7, step2=6):
+def interior(x, w1, w2, sp, gp, step1=7, step2=4):
     proj = jax.ShapeDtypeStruct((C, E), BF)
     return pl.pallas_call(
         functools.partial(interior_kernel, step1, step2),
@@ -143,7 +158,10 @@
     )(x, w1, *in_hbm(w2, sp, gp))
 
 
-def edge_kernel(label, chip, cross, x, xw, hw, sums, w1, w2, o, copies, halo, hh):
+def edge_kernel(label, chip, cross, x, xw, hw, sums, w1, w2, inner, o, copies, out_hbm, halo, hh, sems):
+    outs = [pltpu.make_async_copy(inner.at[f], out_hbm.at[f, 0, pl.ds(2, ROWS - 4)], sems.at[f]) for f in range(2)]
+    for cp in outs:
+        cp.start()
     here, strips = lax.axis_index("strip"), lax.axis_size("strip")
     odd = lax.rem(here, 2)
     for f in range(2):
@@ -176,60 +194,43 @@
         o[k] = y.reshape(2, COLS, C)
         tot[f] = tot[f] + jnp.sum(y.reshape(16, 8, C), axis=0)
     scale = 1.0 / (strips * ROWS * COLS)
-    mark = jnp.full((1, 128), label[0], jnp.int32).astype(F32) * (1.0 / strips)
+    mark = jnp.broadcast_to(label[...].astype(F32) * (1.0 / strips), (1, 128))
     for f in range(2):
         row = jnp.concatenate([jnp.sum(tot[f], axis=0, keepdims=True) * scale, mark], axis=1)
         for n in range(copies.shape[0]):
             copies[n, f:f + 1] = row
-
-
-def edges(label, chip, cross, x, xw, hw, sums, w1, w2, members):
+    for cp in outs:
+        cp.wait()
+
+
+def edges(label, chip, cross, x, xw, hw, sums, w1, w2, inner, members):
     return pl.pallas_call(
         edge_kernel,
         name="edge_rows",
-        out_shape=(jax.ShapeDtypeStruct((4, 2, COLS, C), F32), jax.ShapeDtypeStruct((members, 2, C + 128), F32)),
-        in_specs=[SM] + [VM] * 8,
-        out_specs=(VM,) * 2,
+        out_shape=(jax.ShapeDtypeStruct((4, 2, COLS, C), F32), jax.ShapeDtypeStruct((members, 2, C + 128), F32),
+                   jax.ShapeDtypeStruct((2, 1, ROWS, COLS, C), F32)),
+        in_specs=[VM] * 10,
+        out_specs=(VM, VM, HBM),
         scratch_shapes=[
             pltpu.VMEM((4, 2, COLS, 3 * C), BF),
             pltpu.VMEM((4, 2, COLS, 3 * C), BF),
+            pltpu.SemaphoreType.DMA((2,)),
         ],
         compiler_params=pltpu.CompilerParams(vmem_limit_bytes=24 * MIB),
         cost_estimate=pl.CostEstimate(flops=1_200_000_000, transcendentals=0, bytes_accessed=4_000_000),
-    )(label, chip, cross, x, xw, hw, sums, w1, w2)
-
-
-def write_kernel(o, oe, out_hbm, sems):
+    )(label, chip, cross, x, xw, hw, sums, w1, w2, inner)
+
+
+def head_kernel(sharp, tot, sproj, gproj, oe, partial_hbm, loss_ref, gs_hbm, gg_hbm, out_hbm, buf, sem, osem):
     outs = []
-    for f in range(2):
-        outs.append(pltpu.make_async_copy(o.at[f], out_hbm.at[f, 0, pl.ds(2, 12)], sems.at[3 * f]))
-        for k in range(2):
-            outs.append(pltpu.make_async_copy(oe.at[2 * f + k], out_hbm.at[f, 0, pl.ds(14 * k, 2)], sems.at[3 * f + 1 + k]))
-    for cp in outs:
-        cp.start()
-    for cp in outs:
-        cp.wait()
-
-
-def write(o, oe):
-    return pl.pallas_call(
-        write_kernel,
-        name="write_maps",
-        out_shape=jax.ShapeDtypeStruct((2, 1, ROWS, COLS, C), F32),
-        in_specs=[VM] * 2,
-        out_specs=HBM,
-        scratch_shapes=[pltpu.SemaphoreType.DMA((6,))],
-        compiler_params=pltpu.CompilerParams(vmem_limit_bytes=2 * MIB),
-        cost_estimate=pl.CostEstimate(flops=0, transcendentals=0, bytes_accessed=4_000_000),
-    )(o, oe)
-
-
-def head_kernel(sharp, tot, sproj, gproj, loss_ref, gs_hbm, gg_hbm, buf, sem):
+    for k in range(4):
+        outs.append(pltpu.make_async_copy(oe.at[k], out_hbm.at[k // 2, 0, pl.ds((ROWS - 2) * (k % 2), 2)], osem.at[k]))
+        outs[-1].start()
     pairs = tot.shape[1]
     s_pool = tot[0, :, :C].astype(BF)
     g_pool = tot[1, :, :C].astype(BF)
     label = tot[0, :, C:C + 1]
-    temp = sharp[0]
+    temp = sharp[...]
     s_emb = jnp.dot(s_pool, sproj[...], preferred_element_type=F32)
     g_emb = jnp.dot(g_pool, gproj[...], preferred_element_type=F32)
     s_inv = lax.rsqrt(jnp.sum(s_emb * s_emb, axis=-1, keepdims=True) + 1e-06)
@@ -243,16 +244,10 @@
     row_total = jnp.sum(ex, axis=1, keepdims=True)
     column = lax.broadcasted_iota(jnp.int32, (pairs, pairs), 1).astype(F32)
     matched = column == label
-    positive = jnp.sum(jnp.where(matched, logits, 0.0), axis=1, keepdims=True)
-    losses = jnp.log(row_total) - positive
-    row = lax.broadcasted_iota(jnp.int32, (pairs, 1), 0)
     lgrad = (ex / row_total - jnp.where(matched, 1.0, 0.0)).astype(BF)
-    s_ug = temp * jnp.dot(lgrad, g_bf, preferred_element_type=F32)
-    g_ug = temp * lax.dot_general(lgrad, s_bf, (((0,), (0,)), ((), ())), preferred_element_type=F32)
-    s_eg = ((s_ug - s_unit * jnp.sum(s_unit * s_ug, axis=-1, keepdims=True)) * s_inv).astype(BF)
-    g_eg = ((g_ug - g_unit * jnp.sum(g_unit * g_ug, axis=-1, keepdims=True)) * g_inv).astype(BF)
-    outs = []
-    for k, (pool, grad, dest) in enumerate(((s_pool, s_eg, gs_hbm), (g_pool, g_eg, gg_hbm))):
+
+    def finish(k, unit_grad, unit, inverse, pool, dest):
+        grad = ((unit_grad - unit * jnp.sum(unit * unit_grad, axis=-1, keepdims=True)) * inverse).astype(BF)
         for p in range(2):
             half = pl.ds(p * (C // 2), C // 2)
             buf[k, half] = lax.dot_general(pool[:, p * (C // 2):(p + 1) * (C // 2)], grad, (((0,), (0,)), ((), ())),
@@ -260,22 +255,31 @@
             cp = pltpu.make_async_copy(buf.at[k, half], dest.at[half], sem.at[2 * k + p])
             cp.start()
             outs.append(cp)
+
+    s_ug = temp * jnp.dot(lgrad, g_bf, preferred_element_type=F32)
+    finish(0, s_ug, s_unit, s_inv, s_pool, gs_hbm)
+    g_ug = temp * lax.dot_general(lgrad, s_bf, (((0,), (0,)), ((), ())), preferred_element_type=F32)
+    finish(1, g_ug, g_unit, g_inv, g_pool, gg_hbm)
+    positive = jnp.sum(jnp.where(matched, logits, 0.0), axis=1, keepdims=True)
+    losses = jnp.log(row_total) - positive
+    row = lax.broadcasted_iota(jnp.int32, (pairs, 1), 0)
     loss_ref[0] = jnp.sum(jnp.where(row == lax.axis_index("batch"), losses, 0.0))
     for cp in outs:
         cp.wait()
 
 
-def head(sharp, tot, sproj, gproj):
+def head(sharp, tot, sproj, gproj, oe, out):
     return pl.pallas_call(
         head_kernel,
         name="contrastive_head",
         out_shape=(jax.ShapeDtypeStruct((1,), F32), jax.ShapeDtypeStruct((C, E), F32),
-                   jax.ShapeDtypeStruct((C, E), F32)),
-        in_specs=[SM] + [VM] * 3,
-        out_specs=(SM, HBM, HBM),
-        scratch_shapes=[pltpu.VMEM((2, C, E), F32), pltpu.SemaphoreType.DMA((4,))],
+                   jax.ShapeDtypeStruct((C, E), F32), jax.ShapeDtypeStruct(out.shape, F32)),
+        in_specs=[VM] * 5 + [HBM],
+        out_specs=(SM, HBM, HBM, HBM),
+        input_output_aliases={5: 3},
+        scratch_shapes=[pltpu.VMEM((2, C, E), F32), pltpu.SemaphoreType.DMA((4,)), pltpu.SemaphoreType.DMA((4,))],
         compiler_params=pltpu.CompilerParams(vmem_limit_bytes=16 * MIB),
-    )(sharp, tot, sproj, gproj)
+    )(sharp, tot, sproj, gproj, oe, out)
 
 
 def gather_groups(batch, strips, inner):
@@ -291,20 +295,20 @@
     strips, batch = lax.axis_size("strip"), lax.axis_size("batch")
     w1 = conv_one.reshape(3, 3 * C, C)
     w2 = conv_two.reshape(3, 3 * C, C)
-    chip, cross, x, w1 = load(state_maps, goal_maps, w1)
+    cross = pack(state_maps, goal_maps)
+    chip, x, w1 = load(state_maps, goal_maps, w1, cross)
+    cross = lax.ppermute(cross, "strip", [(i, i + 2 * (i % 2) - 1) for i in range(1, strips - 1)])
     chip = lax.ppermute(chip, "strip", [(i, i ^ 1) for i in range(strips)])
-    cross = lax.ppermute(cross, "strip", [(i, i + 2 * (i % 2) - 1) for i in range(1, strips - 1)])
-    xw, hw, o, sums, w2, sp, gp = interior(x, w1, w2, state_proj, goal_proj)
-    oe, copies = edges(pair_index, chip, cross, x, xw, hw, sums, w1, w2, 2 * strips)
+    xw, hw, inner, sums, w2, sp, gp = interior(x, w1, w2, state_proj, goal_proj)
+    label = pair_index.reshape(1, 1)
+    oe, copies, out = edges(label, chip, cross, x, xw, hw, sums, w1, w2, inner, 2 * strips)
     both = ("batch", "strip")
     line = lax.all_to_all(copies, both, 0, 0, tiled=True, axis_index_groups=gather_groups(batch, strips, True))
     means = jnp.sum(line.reshape(2, strips, 2, C + 128), axis=1).astype(BF).reshape(4, C + 128)
     copies = jnp.broadcast_to(means, (batch // 2, 4, C + 128))
     got = lax.all_to_all(copies, both, 0, 0, tiled=True, axis_index_groups=gather_groups(batch, strips, False))
     tot = jnp.transpose(got.reshape(batch // 2, 2, 2, C + 128).astype(F32), (2, 1, 0, 3)).reshape(2, batch, C + 128)
-    out = write(o, oe)
-    loss, gs, gg = head(inv_temp, tot, sp, gp)
-    return loss, gs, gg, out
+    return head(inv_temp.reshape(1, 1), tot, sp, gp, oe, out)
 
 
 def solution(mesh):

time: 47.9 us -> 48.2 us (level)
  waiting for transfers between devices: 4.49 us -> 5.85 us
  Pallas kernels: 12.3 us -> 11.8 us
  blocking collectives: 14.9 us -> 14.4 us
    ppermute x1, starting transfers between devices: 3.33 us -> 0.09 us  [shards(): chip = lax.ppermute(chip, 'strip', [(i, i ^ 1) for i in range(strips)])]
    ppermute x1, starting transfers between devices: 3.06 us -> 6.29 us  [shards(): lax.ppermute(cross, 'strip', [(i, i + 2 * (i % 2) - 1) for i in range(1,...]
    all_to_all x1, waiting for transfers between devices: 4.48 us -> 5.85 us  [shards(): lax.all_to_all(copies, both, 0, 0, tiled=True, axis_index_groups=gather_g...]
    pallas_call x2, Pallas kernels: 3.14 us -> 2.6 us  [the longest x1 1.7 us: load(): pl.pallas_call(load_kernel, name='load_rows', out_shape=(jax.ShapeDtypeSt...]
where the time goes in v5:
time: 48.2 us; the launch traced here: 47.9 us
  blocking collectives  14.4 us (30%)
  starting transfers between devices  13.1 us (27%)
  Pallas kernels  11.8 us (24%)
  waiting for transfers between devices  5.85 us (12%)
  between operations  2.02 us (4%)
  local copies, waits for them, and re-layouts  0.68 us (1%)
    all_to_all x1, blocking collectives, shards(): lax.all_to_all(copies, both, 0, 0, tiled=True, axis_index_groups=gather_g...  14.4 us
    all_to_all x1, starting transfers between devices, shards(): lax.all_to_all(copies, both, 0, 0, tiled=True, axis_index_groups=gather_g...  6.75 us
    ppermute x1, starting transfers between devices, shards(): lax.ppermute(cross, 'strip', [(i, i + 2 * (i % 2) - 1) for i in range(1,...  6.29 us
    all_to_all x1, waiting for transfers between devices, shards(): lax.all_to_all(copies, both, 0, 0, tiled=True, axis_index_groups=gather_g...  5.85 us
    pallas_call x1, Pallas kernels, interior(): pl.pallas_call(functools.partial(interior_kernel, step1, step2), name='in...  4.55 us
    pallas_call x1, Pallas kernels, head(): pl.pallas_call(head_kernel, name='contrastive_head', out_shape=(jax.Shape...  3.05 us
    pallas_call x1, Pallas kernels, load(): pl.pallas_call(load_kernel, name='load_rows', out_shape=(jax.ShapeDtypeSt...  1.7 us
    pallas_call x1, Pallas kernels, edges(): pl.pallas_call(edge_kernel, name='edge_rows', out_shape=(jax.ShapeDtypeSt...  1.56 us
  transfers between devices with their start and end apart: 3, of which 1 were waited for; matrix products, arithmetic and copies ran while one was open for 0% of the time, Pallas kernels for 13%

profile of v5, /device:TPU:1, one launch (start us, length us, event | category | flops | bytes accessed | tf_op | source)
XLA Modules:
  0.0 47.9 jit_solution(2099869320913167358)
XLA Ops:
  0.6 0.9 %pack_rows.1.packed = bf16[2,2,64,256]{3,2,1,0:T(8,128)(2,1)S(1)} custom-call(bf16[1,16,64,256]{3,2,1,0:T(8,128)(2,1)} %s_hbm.3, bf16[1,16,64,256]{3,2,1,0:T(8,128)(2,1)} %g_hbm.3), custom_call_target="tpu_custom_call" | custom-call | tf_op jit(solution)/shard_map/pack_rows/pallas_call | solution.py:32
  1.5 6.3 %collective-permute-start.1 = (bf16[2,2,64,256]{3,2,1,0:T(8,128)(2,1)S(1)}, bf16[2,2,64,256]{3,2,1,0:T(8,128)(2,1)S(1)}, u32[]{:S(2)}, u32[]{:S(2)}) collective-permute-start(bf16[2,2,64,256]{3,2,1,0:T(8,128)(2,1)S(1)} %pack_rows.1.packed), channel_id=1, source_target_pairs={{1,2},{2,1},{3,4},{4,3},{5,6},{6,5},{9,10},{10,9},{11,12},{12,11},... | collective-permute-start | bytes 393224 | tf_op jit(solution)/shard_map/ppermute | solution.py:300
  7.8 1.7 %load_rows.1 = (bf16[2,2,64,256]{3,2,1,0:T(8,128)(2,1)S(1)}, bf16[2,16,64,256]{3,2,1,0:T(8,128)(2,1)S(1)}, bf16[3,768,256]{2,1,0:T(8,128)(2,1)S(1)}) custom-call(bf16[1,16,64,256]{3,2,1,0:T(8,128)(2,1)} %s_hbm.3, bf16[1,16,64,256]{3,2,1,0:T(8,128)(2,1)} %g_hbm.3, bf16[3,768,256]{2,1,0:T(8,128)(2,1)} %bitcast.14, bf16[2,2,64,256]{3,2,1,0:T(8,128)(2,1)S(1)} %pack_rows.1.packed), custom_call_target="tpu_custom_call" | custom-call | tf_op jit(solution)/shard_map/load_rows/pallas_call | solution.py:56
  9.5 0.1 collective-permute-start
  9.6 4.6 %interior_rows.1 = (bf16[2,16,64,768]{3,2,1,0:T(8,128)(2,1)S(1)}, bf16[2,14,64,768]{3,2,1,0:T(8,128)(2,1)S(1)}, f32[2,12,64,256]{3,2,1,0:T(8,128)S(1)}, f32[2,8,...) custom-call(bf16[2,16,64,256]{3,2,1,0:T(8,128)(2,1)S(1)} %get-tuple-, ...), custom_call_target="tpu_custom_call" | custom-call | flops 4200000000 | bytes 6000000 | tf_op jit(solution)/shard_map/interior_rows/pallas_call | solution.py:146
  14.8 0.0 collective-permute-done.chip
  14.9 0.0 collective-permute-done.1.cross
  14.9 1.6 %edge_rows.1 = (f32[4,2,64,256]{3,2,1,0:T(8,128)S(1)}, f32[16,2,384]{2,1,0:T(2,128)S(1)}, f32[2,1,16,64,256]{4,3,2,1,0:T(8,128)}) custom-call(s32[1,1]{1,0:T(1,128)} %bitcast.12.label, bf16[2,2,64,256]{3,2,1,0:T(8,128)(2,1)S(1)} %collective-permute-done.chip, bf16[2,2,64,256]{3,2,1,0:T(8,128)(2,1)S(1)} %collective-permute-done.1.cross, ...), custom_call_target="tpu_custom_call" | custom-call | flops 1200000000 | bytes 4000000 | tf_op jit(solution)/shard_map/edge_rows/pallas_call | solution.py:207
  16.4 14.4 %all_to_all.10 = f32[16,2,384]{2,1,0:T(2,128)S(1)} all-to-all(f32[16,2,384]{2,1,0:T(2,128)S(1)} %get-tuple-element.25), channel_id=1, replica_groups={{0,1,2,3,4,5,6,7,128,129,130,131,132,133,134,135},{8,9,10,11,12,13,14,1..., dimensions={0} | all-to-all | bytes 98304 | tf_op jit(solution)/shard_map/all_to_all | solution.py:306
  30.9 0.6 %broadcast_in_dim.3 = bf16[16,4,384]{2,1,0:T(4,128)(2,1)} broadcast(bf16[4,384]{1,0:T(4,128)(2,1)S(1)} %convert_element_type.12), dimensions={1,2} | broadcast | bytes 52224 | tf_op jit(solution)/shard_map/broadcast_in_dim | solution.py:308
  31.6 6.8 %all-to-all-start.1 = ((bf16[16,4,384]{2,1,0:T(4,128)(2,1)}), bf16[16,4,384]{2,1,0:T(4,128)(2,1)S(1)}, u32[]{:S(2)}, u32[]{:S(2)}) async-start(bf16[16,4,384]{2,1,0:T(4,128)(2,1)} %broadcast_in_dim.3), calls=%async_computation.1 | async-start | bytes 98304 | tf_op jit(solution)/shard_map/all_to_all | solution.py:309
  39.0 5.8 %all-to-all-done.1 = bf16[16,4,384]{2,1,0:T(4,128)(2,1)S(1)} async-done(((bf16[16,4,384]{2,1,0:T(4,128)(2,1)}), bf16[16,4,384]{2,1,0:T(4,128)(2,1)S(1)}, u32[]{:S(2)}, u32[]{:S(2)}) %all-to-all-start.1) | async-done | bytes 49184 | tf_op jit(solution)/shard_map/all_to_all | solution.py:309
  44.9 3.0 %contrastive_head.1 = (f32[1]{0:T(128)}, f32[256,1024]{1,0:T(8,128)}, f32[256,1024]{1,0:T(8,128)}, f32[2,1,16,64,256]{4,3,2,1,0:T(8,128)}) custom-call(f32[1,1]{1,0:T(1,128)} %bitcast.11.sharp, f32[2,32,384]{2,1,0:T(8,128)S(1)} %bitcast.13, bf16[256,1024]{1,0:T(8,128)(2,1)S(1)} %get-tuple-element.26.sproj, ...), custom_call_target="tpu_custom_call", output_to_operand_aliasing={{3}: (5, {})} | custom-call | tf_op jit(solution)/shard_map/contrastive_head/pallas_call | solution.py:272
  (5 shorter events, 0.1 us)
Async XLA Ops:
  1.5 13.3 %collective-permute-start.1 = (bf16[2,2,64,256]{3,2,1,0:T(8,128)(2,1)S(1)}, bf16[2,2,64,256]{3,2,1,0:T(8,128)(2,1)S(1)}, u32[]{:S(2)}, u32[]{:S(2)}) collective-permute-start(bf16[2,2,64,256]{3,2,1,0:T(8,128)(2,1)S(1)} %pack_rows.1.packed), channel_id=1, source_target_pairs={{1,2},{2,1},{3,4},{4,3},{5,6},{6,5},{9,10},{10,9},{11,12},{12,11},... | collective-permute-start | bytes 393224 | tf_op jit(solution)/shard_map/ppermute | solution.py:300
  9.5 5.3 %collective-permute-start = (bf16[2,2,64,256]{3,2,1,0:T(8,128)(2,1)S(1)}, bf16[2,2,64,256]{3,2,1,0:T(8,128)(2,1)S(1)}, u32[]{:S(2)}, u32[]{:S(2)}) collective-permute-start(bf16[2,2,64,256]{3,2,1,0:T(8,128)(2,1)S(1)} %get-tuple-element.17), channel_id=1, source_target_pairs={{0,1},{1,0},{2,3},{3,2},{4,5},{5,4},{6,7},{7,6},{8,9},{9,8},{10,11... | collective-permute-start | bytes 393224 | tf_op jit(solution)/shard_map/ppermute | solution.py:301
  31.6 13.3 %all-to-all-start.1 = ((bf16[16,4,384]{2,1,0:T(4,128)(2,1)}), bf16[16,4,384]{2,1,0:T(4,128)(2,1)S(1)}, u32[]{:S(2)}, u32[]{:S(2)}) async-start(bf16[16,4,384]{2,1,0:T(4,128)(2,1)} %broadcast_in_dim.3), calls=%async_computation.1 | async-start | bytes 98304 | tf_op jit(solution)/shard_map/all_to_all | solution.py:309

commit v6 on v4

--- a/solution.py
+++ b/solution.py
@@ -18,7 +18,7 @@
     return [pltpu.with_memory_space_constraint(a, pltpu.MemorySpace.HBM) for a in arrays]
 
 
-def load_kernel(s_hbm, g_hbm, w1_hbm, chip, cross, x, w1, sems):
+def load_kernel(s_hbm, g_hbm, w1_hbm, cross, chip, x, w1, sems):
     odd = lax.rem(lax.axis_index("strip"), 2)
     copies = []
     for f, ref in enumerate((s_hbm, g_hbm)):
@@ -26,8 +26,7 @@
         head = (ROWS - 2) * odd
         copies.append((ref.at[0, pl.ds(tail, 2)], chip.at[f]))
         copies.append((ref.at[0, pl.ds(head, 2)], cross.at[f]))
-    for f, ref in enumerate((s_hbm, g_hbm)):
-        copies.append((ref.at[0], x.at[f]))
+    copies.append((s_hbm.at[0], x.at[0]))
     for dy in range(3):
         copies.append((w1_hbm.at[dy], w1.at[dy]))
     copies = [pltpu.make_async_copy(a, b, sems.at[k]) for k, (a, b) in enumerate(copies)]
@@ -42,10 +41,10 @@
     return pl.pallas_call(
         load_kernel,
         name="load_rows",
-        out_shape=(side, side, jax.ShapeDtypeStruct((2, ROWS, COLS, C), BF), jax.ShapeDtypeStruct(w1.shape, BF)),
+        out_shape=(side, side, jax.ShapeDtypeStruct((1, ROWS, COLS, C), BF), jax.ShapeDtypeStruct(w1.shape, BF)),
         in_specs=[HBM] * 3,
         out_specs=(VM,) * 4,
-        scratch_shapes=[pltpu.SemaphoreType.DMA((9,))],
+        scratch_shapes=[pltpu.SemaphoreType.DMA((8,))],
         compiler_params=pltpu.CompilerParams(vmem_limit_bytes=8 * MIB),
     )(*in_hbm(s, g, w1))
 
@@ -79,15 +78,17 @@
     return [(r, min(step, total - r)) for r in range(0, total, step)]
 
 
-def interior_kernel(step1, step2, x, w1, w2_hbm, sp_hbm, gp_hbm, xw, hw, o, sum_ref, w2, sp, gp, sems):
+def interior_kernel(step1, step2, x0, w1, g_hbm, w2_hbm, sp_hbm, gp_hbm, xw, hw, o, sum_ref, x1, w2, sp, gp, sems):
     cw2 = pltpu.make_async_copy(w2_hbm, w2, sems.at[0])
     csp = pltpu.make_async_copy(sp_hbm, sp, sems.at[1])
     cgp = pltpu.make_async_copy(gp_hbm, gp, sems.at[2])
-    cw2.start(); csp.start(); cgp.start()
+    cx1 = pltpu.make_async_copy(g_hbm.at[0], x1.at[0], sems.at[3])
+    cw2.start(); cx1.start(); csp.start(); cgp.start()
+    x = (x0.at[0], x1.at[0])
 
     def spread(f, rows):
         for r in rows:
-            xw[f, r] = widen(jnp.maximum(x[f, r].astype(F32), 0.0))
+            xw[f, r] = widen(jnp.maximum(x[f][r].astype(F32), 0.0))
 
     def first(f, r, n):
         h = jnp.maximum(conv(xw.at[f], r, n, w1), 0.0)
@@ -96,7 +97,7 @@
 
     def second(f, r, n, acc):
         y = conv(hw.at[f], r, n, w2)
-        y = jnp.maximum(y + x[f, r + 2:r + 2 + n].reshape(n * COLS, C).astype(F32), 0.0)
+        y = jnp.maximum(y + x[f][r + 2:r + 2 + n].reshape(n * COLS, C).astype(F32), 0.0)
         o[f, r:r + n] = y.reshape(n, COLS, C)
         part = jnp.sum(y.reshape(n * COLS // 8, 8, C), axis=0)
         return part if acc is None else acc + part
@@ -110,7 +111,7 @@
             spread(0, range(done, upto))
             done = upto
         first(0, r, n)
-    cw2.wait()
+    cw2.wait(); cx1.wait()
     acc = None
     plan = spans(12, step2)
     for i, (r, n) in enumerate(plan):
@@ -126,7 +127,7 @@
     csp.wait(); cgp.wait()
 
 
-def interior(x, w1, w2, sp, gp, step1=7, step2=6):
+def interior(x0, w1, g, w2, sp, gp, step1=7, step2=4):
     proj = jax.ShapeDtypeStruct((C, E), BF)
     return pl.pallas_call(
         functools.partial(interior_kernel, step1, step2),
@@ -134,16 +135,17 @@
         out_shape=(jax.ShapeDtypeStruct((2, ROWS, COLS, 3 * C), BF),
                    jax.ShapeDtypeStruct((2, 14, COLS, 3 * C), BF),
                    jax.ShapeDtypeStruct((2, 12, COLS, C), F32),
-                   jax.ShapeDtypeStruct((2, 8, C), F32), jax.ShapeDtypeStruct(w2.shape, BF), proj, proj),
-        in_specs=[VM] * 2 + [HBM] * 3,
-        out_specs=(VM,) * 7,
-        scratch_shapes=[pltpu.SemaphoreType.DMA((3,))],
+                   jax.ShapeDtypeStruct((2, 8, C), F32), jax.ShapeDtypeStruct(x0.shape, BF),
+                   jax.ShapeDtypeStruct(w2.shape, BF), proj, proj),
+        in_specs=[VM] * 2 + [HBM] * 4,
+        out_specs=(VM,) * 8,
+        scratch_shapes=[pltpu.SemaphoreType.DMA((4,))],
         compiler_params=pltpu.CompilerParams(vmem_limit_bytes=24 * MIB),
         cost_estimate=pl.CostEstimate(flops=4_200_000_000, transcendentals=0, bytes_accessed=6_000_000),
-    )(x, w1, *in_hbm(w2, sp, gp))
-
-
-def edge_kernel(label, chip, cross, x, xw, hw, sums, w1, w2, o, copies, halo, hh):
+    )(x0, w1, *in_hbm(g, w2, sp, gp))
+
+
+def edge_kernel(label, cross, chip, x0, x1, xw, hw, sums, w1, w2, o, copies, halo, hh):
     here, strips = lax.axis_index("strip"), lax.axis_size("strip")
     odd = lax.rem(here, 2)
     for f in range(2):
@@ -172,7 +174,7 @@
         else:
             rows = [hw[f, 12], hw[f, 13], hh[k, 0], hh[k, 1]]
         y = conv_of(rows, w2)
-        y = jnp.maximum(y + x[f, 14 * (k % 2):14 * (k % 2) + 2].reshape(2 * COLS, C).astype(F32), 0.0)
+        y = jnp.maximum(y + (x0, x1)[f][0, 14 * (k % 2):14 * (k % 2) + 2].reshape(2 * COLS, C).astype(F32), 0.0)
         o[k] = y.reshape(2, COLS, C)
         tot[f] = tot[f] + jnp.sum(y.reshape(16, 8, C), axis=0)
     scale = 1.0 / (strips * ROWS * COLS)
@@ -183,12 +185,12 @@
             copies[n, f:f + 1] = row
 
 
-def edges(label, chip, cross, x, xw, hw, sums, w1, w2, members):
+def edges(label, chip, cross, x0, x1, xw, hw, sums, w1, w2, members):
     return pl.pallas_call(
         edge_kernel,
         name="edge_rows",
         out_shape=(jax.ShapeDtypeStruct((4, 2, COLS, C), F32), jax.ShapeDtypeStruct((members, 2, C + 128), F32)),
-        in_specs=[SM] + [VM] * 8,
+        in_specs=[SM] + [VM] * 9,
         out_specs=(VM,) * 2,
         scratch_shapes=[
             pltpu.VMEM((4, 2, COLS, 3 * C), BF),
@@ -196,7 +198,7 @@
         ],
         compiler_params=pltpu.CompilerParams(vmem_limit_bytes=24 * MIB),
         cost_estimate=pl.CostEstimate(flops=1_200_000_000, transcendentals=0, bytes_accessed=4_000_000),
-    )(label, chip, cross, x, xw, hw, sums, w1, w2)
+    )(label, cross, chip, x0, x1, xw, hw, sums, w1, w2)
 
 
 def write_kernel(o, oe, out_hbm, sems):
@@ -243,16 +245,12 @@
     row_total = jnp.sum(ex, axis=1, keepdims=True)
     column = lax.broadcasted_iota(jnp.int32, (pairs, pairs), 1).astype(F32)
     matched = column == label
-    positive = jnp.sum(jnp.where(matched, logits, 0.0), axis=1, keepdims=True)
-    losses = jnp.log(row_total) - positive
-    row = lax.broadcasted_iota(jnp.int32, (pairs, 1), 0)
     lgrad = (ex / row_total - jnp.where(matched, 1.0, 0.0)).astype(BF)
-    s_ug = temp * jnp.dot(lgrad, g_bf, preferred_element_type=F32)
-    g_ug = temp * lax.dot_general(lgrad, s_bf, (((0,), (0,)), ((), ())), preferred_element_type=F32)
-    s_eg = ((s_ug - s_unit * jnp.sum(s_unit * s_ug, axis=-1, keepdims=True)) * s_inv).astype(BF)
-    g_eg = ((g_ug - g_unit * jnp.sum(g_unit * g_ug, axis=-1, keepdims=True)) * g_inv).astype(BF)
+
     outs = []
-    for k, (pool, grad, dest) in enumerate(((s_pool, s_eg, gs_hbm), (g_pool, g_eg, gg_hbm))):
+
+    def finish(k, unit_grad, unit, inverse, pool, dest):
+        grad = ((unit_grad - unit * jnp.sum(unit * unit_grad, axis=-1, keepdims=True)) * inverse).astype(BF)
         for p in range(2):
             half = pl.ds(p * (C // 2), C // 2)
             buf[k, half] = lax.dot_general(pool[:, p * (C // 2):(p + 1) * (C // 2)], grad, (((0,), (0,)), ((), ())),
@@ -260,6 +258,14 @@
             cp = pltpu.make_async_copy(buf.at[k, half], dest.at[half], sem.at[2 * k + p])
             cp.start()
             outs.append(cp)
+
+    s_ug = temp * jnp.dot(lgrad, g_bf, preferred_element_type=F32)
+    finish(0, s_ug, s_unit, s_inv, s_pool, gs_hbm)
+    g_ug = temp * lax.dot_general(lgrad, s_bf, (((0,), (0,)), ((), ())), preferred_element_type=F32)
+    finish(1, g_ug, g_unit, g_inv, g_pool, gg_hbm)
+    positive = jnp.sum(jnp.where(matched, logits, 0.0), axis=1, keepdims=True)
+    losses = jnp.log(row_total) - positive
+    row = lax.broadcasted_iota(jnp.int32, (pairs, 1), 0)
     loss_ref[0] = jnp.sum(jnp.where(row == lax.axis_index("batch"), losses, 0.0))
     for cp in outs:
         cp.wait()
@@ -291,11 +297,11 @@
     strips, batch = lax.axis_size("strip"), lax.axis_size("batch")
     w1 = conv_one.reshape(3, 3 * C, C)
     w2 = conv_two.reshape(3, 3 * C, C)
-    chip, cross, x, w1 = load(state_maps, goal_maps, w1)
+    cross, chip, x0, w1 = load(state_maps, goal_maps, w1)
+    cross = lax.ppermute(cross, "strip", [(i, i + 2 * (i % 2) - 1) for i in range(1, strips - 1)])
     chip = lax.ppermute(chip, "strip", [(i, i ^ 1) for i in range(strips)])
-    cross = lax.ppermute(cross, "strip", [(i, i + 2 * (i % 2) - 1) for i in range(1, strips - 1)])
-    xw, hw, o, sums, w2, sp, gp = interior(x, w1, w2, state_proj, goal_proj)
-    oe, copies = edges(pair_index, chip, cross, x, xw, hw, sums, w1, w2, 2 * strips)
+    xw, hw, o, sums, x1, w2, sp, gp = interior(x0, w1, goal_maps, w2, state_proj, goal_proj)
+    oe, copies = edges(pair_index, chip, cross, x0, x1, xw, hw, sums, w1, w2, 2 * strips)
     both = ("batch", "strip")
     line = lax.all_to_all(copies, both, 0, 0, tiled=True, axis_index_groups=gather_groups(batch, strips, True))
     means = jnp.sum(line.reshape(2, strips, 2, C + 128), axis=1).astype(BF).reshape(4, C + 128)

time: 47.9 us -> 47.6 us (level)
    ppermute x1, starting transfers between devices: 3.33 us -> 0.09 us  [shards(): chip = lax.ppermute(chip, 'strip', [(i, i ^ 1) for i in range(strips)])]
    ppermute x1, starting transfers between devices: 3.06 us -> 6.29 us  [shards(): lax.ppermute(cross, 'strip', [(i, i + 2 * (i % 2) - 1) for i in range(1,...]
where the time goes in v6:
time: 47.6 us; the launch traced here: 47.4 us
  blocking collectives  14.9 us (31%)
  starting transfers between devices  13.1 us (28%)
  Pallas kernels  12.1 us (25%)
  waiting for transfers between devices  4.49 us (9%)
  between operations  2.02 us (4%)
  local copies, waits for them, and re-layouts  0.68 us (1%)
    all_to_all x1, blocking collectives, shards(): lax.all_to_all(copies, both, 0, 0, tiled=True, axis_index_groups=gather_g...  14.9 us
    all_to_all x1, starting transfers between devices, shards(): lax.all_to_all(copies, both, 0, 0, tiled=True, axis_index_groups=gather_g...  6.76 us
    ppermute x1, starting transfers between devices, shards(): lax.ppermute(cross, 'strip', [(i, i + 2 * (i % 2) - 1) for i in range(1,...  6.29 us
    pallas_call x1, Pallas kernels, interior(): pl.pallas_call(functools.partial(interior_kernel, step1, step2), name='in...  4.6 us
    all_to_all x1, waiting for transfers between devices, shards(): lax.all_to_all(copies, both, 0, 0, tiled=True, axis_index_groups=gather_g...  4.48 us
    pallas_call x1, Pallas kernels, head(): pl.pallas_call(head_kernel, name='contrastive_head', out_shape=(jax.Shape...  2.96 us
    pallas_call x1, Pallas kernels, load(): pl.pallas_call(load_kernel, name='load_rows', out_shape=(side, side, jax....  1.61 us
    pallas_call x1, Pallas kernels, edges(): pl.pallas_call(edge_kernel, name='edge_rows', out_shape=(jax.ShapeDtypeSt...  1.53 us
  transfers between devices with their start and end apart: 3, of which 1 were waited for; matrix products, arithmetic and copies ran while one was open for 0% of the time, Pallas kernels for 13%

profile of v6, /device:TPU:1, one launch (start us, length us, event | category | flops | bytes accessed | tf_op | source)
XLA Modules:
  0.0 47.4 jit_solution(12718431928915096834)
XLA Ops:
  0.6 1.6 %load_rows.1 = (bf16[2,2,64,256]{3,2,1,0:T(8,128)(2,1)S(1)}, bf16[2,2,64,256]{3,2,1,0:T(8,128)(2,1)S(1)}, bf16[1,16,64,256]{3,2,1,0:T(8,128)(2,1)S(1)}, bf16[3,768,256]{2,1,0:T(8,128)(2,1)S(1)}) custom-call(bf16[1,16,64,256]{3,2,1,0:T(8,128)(2,1)} %s_hbm.1, bf16[1,16,64,256]{3,2,1,0:T(8,128)(2,1)} %g_hbm.3, bf16[3,768,256]{2,1,0:T(8,128)(2,1)} %bitcast.10), custom_call_target="tpu_custom_call" | custom-call | tf_op jit(solution)/shard_map/load_rows/pallas_call | solution.py:41
  2.3 6.3 %collective-permute-start = (bf16[2,2,64,256]{3,2,1,0:T(8,128)(2,1)S(1)}, bf16[2,2,64,256]{3,2,1,0:T(8,128)(2,1)S(1)}, u32[]{:S(2)}, u32[]{:S(2)}) collective-permute-start(bf16[2,2,64,256]{3,2,1,0:T(8,128)(2,1)S(1)} %get-tuple-element.21), channel_id=1, source_target_pairs={{1,2},{2,1},{3,4},{4,3},{5,6},{6,5},{9,10},{10,9},{11,12},{12,11},... | collective-permute-start | bytes 393224 | tf_op jit(solution)/shard_map/ppermute | solution.py:301
  8.6 0.1 collective-permute-start.1
  8.7 4.6 %interior_rows.1 = (bf16[2,16,64,768]{3,2,1,0:T(8,128)(2,1)S(1)}, bf16[2,14,64,768]{3,2,1,0:T(8,128)(2,1)S(1)}, f32[2,12,64,256]{3,2,1,0:T(8,128)S(1)}, f32[2,8,...) custom-call(bf16[1,16,64,256]{3,2,1,0:T(8,128)(2,1)S(1)} %get-tuple-, ...), custom_call_target="tpu_custom_call" | custom-call | flops 4200000000 | bytes 6000000 | tf_op jit(solution)/shard_map/interior_rows/pallas_call | solution.py:132
  13.9 0.0 collective-permute-done.cross
  13.9 0.0 collective-permute-done.1.chip
  13.9 1.5 %edge_rows.1 = (f32[4,2,64,256]{3,2,1,0:T(8,128)S(1)}, f32[16,2,384]{2,1,0:T(2,128)S(1)}) custom-call(s32[1]{0:T(128)S(6)} %copy.16.label, bf16[2,2,64,256]{3,2,1,0:T(8,128)(2,1)S(1)} %collective-permute-done.cross, bf16[2,2,64,256]{3,2,1,0:T(8,128)(2,1)S(1)} %collective-permute-done.1.chip, bf16[1,16,64,256]{3,2,1,0:T(8,128)(2,1)S(1)} %get-tuple-element.23.x0, ...), custom_call_target="tpu_custom_call" | custom-call | flops 1200000000 | bytes 4000000 | tf_op jit(solution)/shard_map/edge_rows/pallas_call | solution.py:189
  15.5 14.9 %all_to_all.10 = f32[16,2,384]{2,1,0:T(2,128)S(1)} all-to-all(f32[16,2,384]{2,1,0:T(2,128)S(1)} %get-tuple-element.30), channel_id=1, replica_groups={{0,1,2,3,4,5,6,7,128,129,130,131,132,133,134,135},{8,9,10,11,12,13,14,1..., dimensions={0} | all-to-all | bytes 98304 | tf_op jit(solution)/shard_map/all_to_all | solution.py:306
  30.4 0.6 %broadcast_in_dim.3 = bf16[16,4,384]{2,1,0:T(4,128)(2,1)} broadcast(bf16[4,384]{1,0:T(4,128)(2,1)S(1)} %convert_element_type.12), dimensions={1,2} | broadcast | bytes 52224 | tf_op jit(solution)/shard_map/broadcast_in_dim | solution.py:308
  31.1 6.8 %all-to-all-start.1 = ((bf16[16,4,384]{2,1,0:T(4,128)(2,1)}), bf16[16,4,384]{2,1,0:T(4,128)(2,1)S(1)}, u32[]{:S(2)}, u32[]{:S(2)}) async-start(bf16[16,4,384]{2,1,0:T(4,128)(2,1)} %broadcast_in_dim.3), calls=%async_computation.1 | async-start | bytes 98304 | tf_op jit(solution)/shard_map/all_to_all | solution.py:309
  38.5 1.4 %write_maps.1 = f32[2,1,16,64,256]{4,3,2,1,0:T(8,128)} custom-call(f32[2,12,64,256]{3,2,1,0:T(8,128)S(1)} %get-tuple-element.36.o, f32[4,2,64,256]{3,2,1,0:T(8,128)S(1)} %get-tuple-element.37.oe), custom_call_target="tpu_custom_call" | custom-call | bytes 4000000 | tf_op jit(solution)/shard_map/write_maps/pallas_call | solution.py:217
  39.9 4.5 %all-to-all-done.1 = bf16[16,4,384]{2,1,0:T(4,128)(2,1)S(1)} async-done(((bf16[16,4,384]{2,1,0:T(4,128)(2,1)}), bf16[16,4,384]{2,1,0:T(4,128)(2,1)S(1)}, u32[]{:S(2)}, u32[]{:S(2)}) %all-to-all-start.1) | async-done | bytes 49184 | tf_op jit(solution)/shard_map/all_to_all | solution.py:309
  44.4 3.0 %contrastive_head.1 = (f32[1]{0:T(128)}, f32[256,1024]{1,0:T(8,128)}, f32[256,1024]{1,0:T(8,128)}) custom-call(f32[1]{0:T(128)S(6)} %copy.15.sharp, f32[2,32,384]{2,1,0:T(8,128)S(1)} %bitcast.9, bf16[256,1024]{1,0:T(8,128)(2,1)S(1)} %get-tuple-element.31.sproj, bf16[256,1024]{1,0:T(8,128)(2,1)S(1)} %get-tuple-element.32.gproj), custom_call_target="tpu_custom_call" | custom-call | tf_op jit(solution)/shard_map/contrastive_head/pallas_call | solution.py:275
  (5 shorter events, 0.1 us)
Async XLA Ops:
  2.3 11.7 %collective-permute-start = (bf16[2,2,64,256]{3,2,1,0:T(8,128)(2,1)S(1)}, bf16[2,2,64,256]{3,2,1,0:T(8,128)(2,1)S(1)}, u32[]{:S(2)}, u32[]{:S(2)}) collective-permute-start(bf16[2,2,64,256]{3,2,1,0:T(8,128)(2,1)S(1)} %get-tuple-element.21), channel_id=1, source_target_pairs={{1,2},{2,1},{3,4},{4,3},{5,6},{6,5},{9,10},{10,9},{11,12},{12,11},... | collective-permute-start | bytes 393224 | tf_op jit(solution)/shard_map/ppermute | solution.py:301
  8.6 5.4 %collective-permute-start.1 = (bf16[2,2,64,256]{3,2,1,0:T(8,128)(2,1)S(1)}, bf16[2,2,64,256]{3,2,1,0:T(8,128)(2,1)S(1)}, u32[]{:S(2)}, u32[]{:S(2)}) collective-permute-start(bf16[2,2,64,256]{3,2,1,0:T(8,128)(2,1)S(1)} %get-tuple-element.22), channel_id=1, source_target_pairs={{0,1},{1,0},{2,3},{3,2},{4,5},{5,4},{6,7},{7,6},{8,9},{9,8},{10,11... | collective-permute-start | bytes 393224 | tf_op jit(solution)/shard_map/ppermute | solution.py:302
  31.1 13.3 %all-to-all-start.1 = ((bf16[16,4,384]{2,1,0:T(4,128)(2,1)}), bf16[16,4,384]{2,1,0:T(4,128)(2,1)S(1)}, u32[]{:S(2)}, u32[]{:S(2)}) async-start(bf16[16,4,384]{2,1,0:T(4,128)(2,1)} %broadcast_in_dim.3), calls=%async_computation.1 | async-start | bytes 98304 | tf_op jit(solution)/shard_map/all_to_all | solution.py:309

commit v7 on v5

--- a/solution.py
+++ b/solution.py
@@ -18,33 +18,16 @@
     return [pltpu.with_memory_space_constraint(a, pltpu.MemorySpace.HBM) for a in arrays]
 
 
-def pack_kernel(s_hbm, g_hbm, cross, sems):
+def load_kernel(s_hbm, g_hbm, w1_hbm, cross, chip, x, w1, sems):
     odd = lax.rem(lax.axis_index("strip"), 2)
-    copies = [pltpu.make_async_copy(ref.at[0, pl.ds((ROWS - 2) * odd, 2)], cross.at[f], sems.at[f])
-              for f, ref in enumerate((s_hbm, g_hbm))]
-    for cp in copies:
-        cp.start()
-    for cp in copies:
-        cp.wait()
-
-
-def pack(s, g):
-    return pl.pallas_call(
-        pack_kernel,
-        name="pack_rows",
-        out_shape=jax.ShapeDtypeStruct((2, 2, COLS, C), BF),
-        in_specs=[HBM] * 2,
-        out_specs=VM,
-        scratch_shapes=[pltpu.SemaphoreType.DMA((2,))],
-        compiler_params=pltpu.CompilerParams(vmem_limit_bytes=2 * MIB),
-    )(*in_hbm(s, g))
-
-
-def load_kernel(s_hbm, g_hbm, w1_hbm, packed, chip, x, w1, sems):
-    odd = lax.rem(lax.axis_index("strip"), 2)
-    copies = [(ref.at[0, pl.ds((ROWS - 2) * (1 - odd), 2)], chip.at[f]) for f, ref in enumerate((s_hbm, g_hbm))]
-    copies += [(ref.at[0], x.at[f]) for f, ref in enumerate((s_hbm, g_hbm))]
-    copies += [(w1_hbm.at[dy], w1.at[dy]) for dy in range(3)]
+    copies = []
+    for f, ref in enumerate((s_hbm, g_hbm)):
+        tail = (ROWS - 2) * (1 - odd)
+        head = (ROWS - 2) * odd
+        copies.append((ref.at[0, pl.ds(tail, 2)], chip.at[f]))
+        copies.append((ref.at[0, pl.ds(head, 2)], cross.at[f]))
+    copies.append((s_hbm.at[0], x.at[0]))
+    copies.append((w1_hbm.at[0], w1.at[0]))
     copies = [pltpu.make_async_copy(a, b, sems.at[k]) for k, (a, b) in enumerate(copies)]
     for cp in copies:
         cp.start()
@@ -52,17 +35,17 @@
         cp.wait()
 
 
-def load(s, g, w1, packed):
+def load(s, g, w1):
+    side = jax.ShapeDtypeStruct((2, 2, COLS, C), BF)
     return pl.pallas_call(
         load_kernel,
         name="load_rows",
-        out_shape=(jax.ShapeDtypeStruct((2, 2, COLS, C), BF), jax.ShapeDtypeStruct((2, ROWS, COLS, C), BF),
-                   jax.ShapeDtypeStruct(w1.shape, BF)),
-        in_specs=[HBM] * 3 + [VM],
-        out_specs=(VM,) * 3,
-        scratch_shapes=[pltpu.SemaphoreType.DMA((7,))],
+        out_shape=(side, side, jax.ShapeDtypeStruct((1, ROWS, COLS, C), BF), jax.ShapeDtypeStruct((1, 3 * C, C), BF)),
+        in_specs=[HBM] * 3,
+        out_specs=(VM,) * 4,
+        scratch_shapes=[pltpu.SemaphoreType.DMA((6,))],
         compiler_params=pltpu.CompilerParams(vmem_limit_bytes=8 * MIB),
-    )(*in_hbm(s, g, w1), packed)
+    )(*in_hbm(s, g, w1))
 
 
 def widen(row):
@@ -72,11 +55,13 @@
     return jnp.concatenate([left.astype(BF), row.astype(BF), right.astype(BF)], axis=-1)
 
 
-def conv(wide, first, rows, weights):
+def conv(wide, first, rows, weights, waits=None):
     total = None
     for dy in range(3):
+        if waits is not None and waits[dy] is not None:
+            waits[dy].wait()
         lhs = wide[pl.ds(first + dy, rows)].reshape(rows * COLS, 3 * C)
-        part = jnp.dot(lhs, weights[dy], preferred_element_type=F32)
+        part = jnp.dot(lhs, weights[dy][...], preferred_element_type=F32)
         total = part if total is None else total + part
     return total
 
@@ -85,7 +70,7 @@
     total = None
     for dy in range(3):
         lhs = jnp.concatenate([rows[dy], rows[dy + 1]], axis=0)
-        part = jnp.dot(lhs, weights[dy], preferred_element_type=F32)
+        part = jnp.dot(lhs, weights[dy][...], preferred_element_type=F32)
         total = part if total is None else total + part
     return total
 
@@ -94,24 +79,32 @@
     return [(r, min(step, total - r)) for r in range(0, total, step)]
 
 
-def interior_kernel(step1, step2, x, w1, w2_hbm, sp_hbm, gp_hbm, xw, hw, o, sum_ref, w2, sp, gp, sems):
+def interior_kernel(step1, step2, x0, w1a, label_hbm, sharp_hbm, w1_hbm, g_hbm, w2_hbm, sp_hbm, gp_hbm,
+                    xw, hw, o, sum_ref, marks, x1, w1b, w2, sp, gp, label, sharp, sems):
     cw2 = pltpu.make_async_copy(w2_hbm, w2, sems.at[0])
     csp = pltpu.make_async_copy(sp_hbm, sp, sems.at[1])
     cgp = pltpu.make_async_copy(gp_hbm, gp, sems.at[2])
-    cw2.start(); csp.start(); cgp.start()
+    cx1 = pltpu.make_async_copy(g_hbm.at[0], x1.at[0], sems.at[3])
+    clabel = pltpu.make_async_copy(label_hbm, label, sems.at[4])
+    csharp = pltpu.make_async_copy(sharp_hbm, sharp, sems.at[5])
+    cw1 = [pltpu.make_async_copy(w1_hbm.at[dy], w1b.at[dy - 1], sems.at[5 + dy]) for dy in (1, 2)]
+    cw1[0].start(); cw1[1].start(); cw2.start(); cx1.start(); csp.start(); cgp.start(); clabel.start(); csharp.start()
+    x = (x0.at[0], x1.at[0])
+    first_weights = [w1a.at[0], w1b.at[0], w1b.at[1]]
+    second_weights = [w2.at[dy] for dy in range(3)]
 
     def spread(f, rows):
         for r in rows:
-            xw[f, r] = widen(jnp.maximum(x[f, r].astype(F32), 0.0))
-
-    def first(f, r, n):
-        h = jnp.maximum(conv(xw.at[f], r, n, w1), 0.0)
+            xw[f, r] = widen(jnp.maximum(x[f][r].astype(F32), 0.0))
+
+    def first(f, r, n, waits=None):
+        h = jnp.maximum(conv(xw.at[f], r, n, first_weights, waits), 0.0)
         for k in range(n):
             hw[f, r + k] = widen(h[k * COLS:(k + 1) * COLS])
 
     def second(f, r, n, acc):
-        y = conv(hw.at[f], r, n, w2)
-        y = jnp.maximum(y + x[f, r + 2:r + 2 + n].reshape(n * COLS, C).astype(F32), 0.0)
+        y = conv(hw.at[f], r, n, second_weights)
+        y = jnp.maximum(y + x[f][r + 2:r + 2 + n].reshape(n * COLS, C).astype(F32), 0.0)
         o[f, r:r + n] = y.reshape(n, COLS, C)
         part = jnp.sum(y.reshape(n * COLS // 8, 8, C), axis=0)
         return part if acc is None else acc + part
@@ -124,8 +117,8 @@
             upto = plan[i + 1][0] + plan[i + 1][1] + 2
             spread(0, range(done, upto))
             done = upto
-        first(0, r, n)
-    cw2.wait()
+        first(0, r, n, [None] + cw1 if i == 0 else None)
+    cw2.wait(); cx1.wait()
     acc = None
     plan = spans(12, step2)
     for i, (r, n) in enumerate(plan):
@@ -138,10 +131,13 @@
     for r, n in spans(12, step2):
         acc = second(1, r, n, acc)
     sum_ref[1] = acc
+    clabel.wait(); csharp.wait()
+    marks[0:8] = jnp.full((8, 128), label[0], jnp.int32).astype(F32)
+    marks[8:16] = jnp.full((8, 128), sharp[0], F32)
     csp.wait(); cgp.wait()
 
 
-def interior(x, w1, w2, sp, gp, step1=7, step2=4):
+def interior(x0, w1a, label, sharp, w1, g, w2, sp, gp, step1=7, step2=4):
     proj = jax.ShapeDtypeStruct((C, E), BF)
     return pl.pallas_call(
         functools.partial(interior_kernel, step1, step2),
@@ -149,19 +145,22 @@
         out_shape=(jax.ShapeDtypeStruct((2, ROWS, COLS, 3 * C), BF),
                    jax.ShapeDtypeStruct((2, 14, COLS, 3 * C), BF),
                    jax.ShapeDtypeStruct((2, 12, COLS, C), F32),
-                   jax.ShapeDtypeStruct((2, 8, C), F32), jax.ShapeDtypeStruct(w2.shape, BF), proj, proj),
-        in_specs=[VM] * 2 + [HBM] * 3,
-        out_specs=(VM,) * 7,
-        scratch_shapes=[pltpu.SemaphoreType.DMA((3,))],
+                   jax.ShapeDtypeStruct((2, 8, C), F32), jax.ShapeDtypeStruct((16, 128), F32), jax.ShapeDtypeStruct(x0.shape, BF),
+                   jax.ShapeDtypeStruct((2, 3 * C, C), BF), jax.ShapeDtypeStruct(w2.shape, BF), proj, proj),
+        in_specs=[VM] * 2 + [HBM] * 7,
+        out_specs=(VM,) * 10,
+        scratch_shapes=[pltpu.SMEM((1,), jnp.int32), pltpu.SMEM((1,), F32), pltpu.SemaphoreType.DMA((8,))],
         compiler_params=pltpu.CompilerParams(vmem_limit_bytes=24 * MIB),
         cost_estimate=pl.CostEstimate(flops=4_200_000_000, transcendentals=0, bytes_accessed=6_000_000),
-    )(x, w1, *in_hbm(w2, sp, gp))
-
-
-def edge_kernel(label, chip, cross, x, xw, hw, sums, w1, w2, inner, o, copies, out_hbm, halo, hh, sems):
+    )(x0, w1a, label, sharp, *in_hbm(w1, g, w2, sp, gp))
+
+
+def edge_kernel(marks, cross, chip, x0, x1, xw, hw, sums, w1a, w1b, w2, inner, o, copies, out_hbm, halo, hh, sems):
     outs = [pltpu.make_async_copy(inner.at[f], out_hbm.at[f, 0, pl.ds(2, ROWS - 4)], sems.at[f]) for f in range(2)]
     for cp in outs:
         cp.start()
+    w1 = [w1a.at[0], w1b.at[0], w1b.at[1]]
+    w2 = [w2.at[dy] for dy in range(3)]
     here, strips = lax.axis_index("strip"), lax.axis_size("strip")
     odd = lax.rem(here, 2)
     for f in range(2):
@@ -190,11 +189,11 @@
         else:
             rows = [hw[f, 12], hw[f, 13], hh[k, 0], hh[k, 1]]
         y = conv_of(rows, w2)
-        y = jnp.maximum(y + x[f, 14 * (k % 2):14 * (k % 2) + 2].reshape(2 * COLS, C).astype(F32), 0.0)
+        y = jnp.maximum(y + (x0, x1)[f][0, 14 * (k % 2):14 * (k % 2) + 2].reshape(2 * COLS, C).astype(F32), 0.0)
         o[k] = y.reshape(2, COLS, C)
         tot[f] = tot[f] + jnp.sum(y.reshape(16, 8, C), axis=0)
     scale = 1.0 / (strips * ROWS * COLS)
-    mark = jnp.broadcast_to(label[...].astype(F32) * (1.0 / strips), (1, 128))
+    mark = marks[0:1] * (1.0 / strips)
     for f in range(2):
         row = jnp.concatenate([jnp.sum(tot[f], axis=0, keepdims=True) * scale, mark], axis=1)
         for n in range(copies.shape[0]):
@@ -203,13 +202,13 @@
         cp.wait()
 
 
-def edges(label, chip, cross, x, xw, hw, sums, w1, w2, inner, members):
+def edges(marks, cross, chip, x0, x1, xw, hw, sums, w1a, w1b, w2, inner, members):
     return pl.pallas_call(
         edge_kernel,
         name="edge_rows",
         out_shape=(jax.ShapeDtypeStruct((4, 2, COLS, C), F32), jax.ShapeDtypeStruct((members, 2, C + 128), F32),
                    jax.ShapeDtypeStruct((2, 1, ROWS, COLS, C), F32)),
-        in_specs=[VM] * 10,
+        in_specs=[VM] * 12,
         out_specs=(VM, VM, HBM),
         scratch_shapes=[
             pltpu.VMEM((4, 2, COLS, 3 * C), BF),
@@ -218,10 +217,10 @@
         ],
         compiler_params=pltpu.CompilerParams(vmem_limit_bytes=24 * MIB),
         cost_estimate=pl.CostEstimate(flops=1_200_000_000, transcendentals=0, bytes_accessed=4_000_000),
-    )(label, chip, cross, x, xw, hw, sums, w1, w2, inner)
-
-
-def head_kernel(sharp, tot, sproj, gproj, oe, partial_hbm, loss_ref, gs_hbm, gg_hbm, out_hbm, buf, sem, osem):
+    )(marks, cross, chip, x0, x1, xw, hw, sums, w1a, w1b, w2, inner)
+
+
+def head_kernel(marks, tot, sproj, gproj, oe, partial_hbm, loss_ref, gs_hbm, gg_hbm, out_hbm, buf, sem, osem):
     outs = []
     for k in range(4):
         outs.append(pltpu.make_async_copy(oe.at[k], out_hbm.at[k // 2, 0, pl.ds((ROWS - 2) * (k % 2), 2)], osem.at[k]))
@@ -230,7 +229,7 @@
     s_pool = tot[0, :, :C].astype(BF)
     g_pool = tot[1, :, :C].astype(BF)
     label = tot[0, :, C:C + 1]
-    temp = sharp[...]
+    temp = marks[8:9, 0:1]
     s_emb = jnp.dot(s_pool, sproj[...], preferred_element_type=F32)
     g_emb = jnp.dot(g_pool, gproj[...], preferred_element_type=F32)
     s_inv = lax.rsqrt(jnp.sum(s_emb * s_emb, axis=-1, keepdims=True) + 1e-06)
@@ -268,7 +267,7 @@
         cp.wait()
 
 
-def head(sharp, tot, sproj, gproj, oe, out):
+def head(marks, tot, sproj, gproj, oe, out):
     return pl.pallas_call(
         head_kernel,
         name="contrastive_head",
@@ -279,7 +278,7 @@
         input_output_aliases={5: 3},
         scratch_shapes=[pltpu.VMEM((2, C, E), F32), pltpu.SemaphoreType.DMA((4,)), pltpu.SemaphoreType.DMA((4,))],
         compiler_params=pltpu.CompilerParams(vmem_limit_bytes=16 * MIB),
-    )(sharp, tot, sproj, gproj, oe, out)
+    )(marks, tot, sproj, gproj, oe, out)
 
 
 def gather_groups(batch, strips, inner):
@@ -295,20 +294,19 @@
     strips, batch = lax.axis_size("strip"), lax.axis_size("batch")
     w1 = conv_one.reshape(3, 3 * C, C)
     w2 = conv_two.reshape(3, 3 * C, C)
-    cross = pack(state_maps, goal_maps)
-    chip, x, w1 = load(state_maps, goal_maps, w1, cross)
+    cross, chip, x0, w1a = load(state_maps, goal_maps, w1)
     cross = lax.ppermute(cross, "strip", [(i, i + 2 * (i % 2) - 1) for i in range(1, strips - 1)])
     chip = lax.ppermute(chip, "strip", [(i, i ^ 1) for i in range(strips)])
-    xw, hw, inner, sums, w2, sp, gp = interior(x, w1, w2, state_proj, goal_proj)
-    label = pair_index.reshape(1, 1)
-    oe, copies, out = edges(label, chip, cross, x, xw, hw, sums, w1, w2, inner, 2 * strips)
+    xw, hw, inner, sums, marks, x1, w1b, w2, sp, gp = interior(
+        x0, w1a, pair_index, inv_temp, w1, goal_maps, w2, state_proj, goal_proj)
+    oe, copies, out = edges(marks, cross, chip, x0, x1, xw, hw, sums, w1a, w1b, w2, inner, 2 * strips)
     both = ("batch", "strip")
     line = lax.all_to_all(copies, both, 0, 0, tiled=True, axis_index_groups=gather_groups(batch, strips, True))
     means = jnp.sum(line.reshape(2, strips, 2, C + 128), axis=1).astype(BF).reshape(4, C + 128)
     copies = jnp.broadcast_to(means, (batch // 2, 4, C + 128))
     got = lax.all_to_all(copies, both, 0, 0, tiled=True, axis_index_groups=gather_groups(batch, strips, False))
     tot = jnp.transpose(got.reshape(batch // 2, 2, 2, C + 128).astype(F32), (2, 1, 0, 3)).reshape(2, batch, C + 128)
-    return head(inv_temp.reshape(1, 1), tot, sp, gp, oe, out)
+    return head(marks, tot, sp, gp, oe, out)
 
 
 def solution(mesh):

time: 48.2 us -> 49.1 us (1.019)
  blocking collectives: 14.4 us -> 27.5 us
  starting transfers between devices: 13.1 us -> 6.38 us
  waiting for transfers between devices: 5.85 us -> 0.01 us
  Pallas kernels: 11.8 us -> 12.9 us
  local copies, waits for them, and re-layouts: 0.68 us -> 0.06 us
    all_to_all x1 -> x2, blocking collectives: 14.4 us -> 27.5 us  [shards(): lax.all_to_all(copies, both, 0, 0, tiled=True, axis_index_groups=gather_g...]
    all_to_all x1 -> x0, starting transfers between devices: 6.75 us -> none  [shards(): lax.all_to_all(copies, both, 0, 0, tiled=True, axis_index_groups=gather_g...]
    all_to_all x1 -> x0, waiting for transfers between devices: 5.85 us -> none  [shards(): lax.all_to_all(copies, both, 0, 0, tiled=True, axis_index_groups=gather_g...]
    pallas_call x1, Pallas kernels: 4.55 us -> 6.32 us  [interior(): pl.pallas_call(functools.partial(interior_kernel, step1, step2), name='in...]
    pallas_call x2 -> x1, Pallas kernels: 2.6 us -> 1.36 us  [load(): pl.pallas_call(load_kernel, name='load_rows', out_shape=(side, side, jax....]
    broadcast_in_dim x1, local copies, waits for them, and re-layouts: 0.64 us -> 0.02 us  [shards(): copies = jnp.broadcast_to(means, (batch // 2, 4, C + 128))]
    pallas_call x1, Pallas kernels: 1.56 us -> 2.15 us  [edges(): pl.pallas_call(edge_kernel, name='edge_rows', out_shape=(jax.ShapeDtypeSt...]
  transfers between devices with their start and end apart: 3 -> 2, of which waited for: 1 -> 0; matrix products, arithmetic and copies ran while one was open for 0% -> 0% of each run, Pallas kernels for 13% -> 13%
where the time goes in v7:
time: 49.1 us; the launch traced here: 48.9 us
  blocking collectives  27.5 us (56%)
  Pallas kernels  12.9 us (26%)
  starting transfers between devices  6.38 us (13%)
  between operations  2 us (4%)
    all_to_all x2, blocking collectives, shards(): lax.all_to_all(copies, both, 0, 0, tiled=True, axis_index_groups=gather_g...  27.5 us
    pallas_call x1, Pallas kernels, interior(): pl.pallas_call(functools.partial(interior_kernel, step1, step2), name='in...  6.32 us
    ppermute x1, starting transfers between devices, shards(): lax.ppermute(cross, 'strip', [(i, i + 2 * (i % 2) - 1) for i in range(1,...  6.29 us
    pallas_call x1, Pallas kernels, head(): pl.pallas_call(head_kernel, name='contrastive_head', out_shape=(jax.Shape...  3.05 us
    pallas_call x1, Pallas kernels, edges(): pl.pallas_call(edge_kernel, name='edge_rows', out_shape=(jax.ShapeDtypeSt...  2.15 us
    pallas_call x1, Pallas kernels, load(): pl.pallas_call(load_kernel, name='load_rows', out_shape=(side, side, jax....  1.36 us
  transfers between devices with their start and end apart: 2, of which 0 were waited for; matrix products, arithmetic and copies ran while one was open for 0% of the time, Pallas kernels for 13%

profile of v7, /device:TPU:1, one launch (start us, length us, event | category | flops | bytes accessed | tf_op | source)
XLA Modules:
  0.0 48.9 jit_solution(11593099014470617687)
XLA Ops:
  0.6 1.4 %load_rows.1 = (bf16[2,2,64,256]{3,2,1,0:T(8,128)(2,1)S(1)}, bf16[2,2,64,256]{3,2,1,0:T(8,128)(2,1)S(1)}, bf16[1,16,64,256]{3,2,1,0:T(8,128)(2,1)S(1)}, bf16[1,768,256]{2,1,0:T(8,128)(2,1)S(1)}) custom-call(bf16[1,16,64,256]{3,2,1,0:T(8,128)(2,1)} %s_hbm.1, bf16[1,16,64,256]{3,2,1,0:T(8,128)(2,1)} %g_hbm.3, bf16[3,768,256]{2,1,0:T(8,128)(2,1)} %bitcast.10), custom_call_target="tpu_custom_call" | custom-call | tf_op jit(solution)/shard_map/load_rows/pallas_call | solution.py:40
  2.0 6.3 %collective-permute-start = (bf16[2,2,64,256]{3,2,1,0:T(8,128)(2,1)S(1)}, bf16[2,2,64,256]{3,2,1,0:T(8,128)(2,1)S(1)}, u32[]{:S(2)}, u32[]{:S(2)}) collective-permute-start(bf16[2,2,64,256]{3,2,1,0:T(8,128)(2,1)S(1)} %get-tuple-element.24), channel_id=1, source_target_pairs={{1,2},{2,1},{3,4},{4,3},{5,6},{6,5},{9,10},{10,9},{11,12},{12,11},... | collective-permute-start | bytes 393224 | tf_op jit(solution)/shard_map/ppermute | solution.py:298
  8.3 0.1 collective-permute-start.1
  9.7 6.3 %interior_rows.1 = (bf16[2,16,64,768]{3,2,1,0:T(8,128)(2,1)S(1)}, bf16[2,14,64,768]{3,2,1,0:T(8,128)(2,1)S(1)}, f32[2,12,64,256]{3,2,1,0:T(8,128)S(1)}, f32[2,8,...) custom-call(bf16[1,16,64,256]{3,2,1,0:T(8,128)(2,1)S(1)} %get-tuple-, ...), custom_call_target="tpu_custom_call" | custom-call | flops 4200000000 | bytes 6000000 | tf_op jit(solution)/shard_map/interior_rows/pallas_call | solution.py:142
  16.0 0.0 collective-permute-done.cross
  16.0 0.0 collective-permute-done.1.chip
  16.0 2.2 %edge_rows.1 = (f32[4,2,64,256]{3,2,1,0:T(8,128)S(1)}, f32[16,2,384]{2,1,0:T(2,128)S(1)}, f32[2,1,16,64,256]{4,3,2,1,0:T(8,128)}) custom-call(f32[16,128]{1,0:T(8,128)S(1)} %get-tuple-element.23.marks, bf16[2,2,64,256]{3,2,1,0:T(8,128)(2,1)S(1)} %collective-permute-done.cross, bf16[2,2,64,256]{3,2,1,0:T(8,128)(2,1)S(1)} %collective-permute-done.1.chip, ...), custom_call_target="tpu_custom_call" | custom-call | flops 1200000000 | bytes 4000000 | tf_op jit(solution)/shard_map/edge_rows/pallas_call | solution.py:206
  18.2 14.5 %all_to_all.10 = f32[16,2,384]{2,1,0:T(2,128)S(1)} all-to-all(f32[16,2,384]{2,1,0:T(2,128)S(1)} %get-tuple-element.33), channel_id=1, replica_groups={{0,1,2,3,4,5,6,7,128,129,130,131,132,133,134,135},{8,9,10,11,12,13,14,1..., dimensions={0} | all-to-all | bytes 98304 | tf_op jit(solution)/shard_map/all_to_all | solution.py:304
  32.7 13.1 %all_to_all.11 = bf16[16,4,384]{2,1,0:T(4,128)(2,1)S(1)} all-to-all(bf16[16,4,384]{2,1,0:T(4,128)(2,1)S(1)} %broadcast_in_dim.3), channel_id=1, replica_groups={{0,8,16,24,32,40,48,56,64,72,80,88,96,104,112,120},{1,9,17,25,33,41,49,..., dimensions={0} | all-to-all | bytes 98304 | tf_op jit(solution)/shard_map/all_to_all | solution.py:307
  45.8 3.0 %contrastive_head.1 = (f32[1]{0:T(128)}, f32[256,1024]{1,0:T(8,128)}, f32[256,1024]{1,0:T(8,128)}, f32[2,1,16,64,256]{4,3,2,1,0:T(8,128)}) custom-call(f32[16,128]{1,0:T(8,128)S(1)} %get-tuple-element.23.marks, f32[2,32,384]{2,1,0:T(8,128)S(1)} %bitcast.9, bf16[256,1024]{1,0:T(8,128)(2,1)S(1)} %get-tuple-element.34.sproj, ...), custom_call_target="tpu_custom_call", output_to_operand_aliasing={{3}: (5, {})} | custom-call | tf_op jit(solution)/shard_map/contrastive_head/pallas_call | solution.py:271
  (6 shorter events, 0.1 us)
Async XLA Ops:
  2.0 14.0 %collective-permute-start = (bf16[2,2,64,256]{3,2,1,0:T(8,128)(2,1)S(1)}, bf16[2,2,64,256]{3,2,1,0:T(8,128)(2,1)S(1)}, u32[]{:S(2)}, u32[]{:S(2)}) collective-permute-start(bf16[2,2,64,256]{3,2,1,0:T(8,128)(2,1)S(1)} %get-tuple-element.24), channel_id=1, source_target_pairs={{1,2},{2,1},{3,4},{4,3},{5,6},{6,5},{9,10},{10,9},{11,12},{12,11},... | collective-permute-start | bytes 393224 | tf_op jit(solution)/shard_map/ppermute | solution.py:298
  8.3 7.7 %collective-permute-start.1 = (bf16[2,2,64,256]{3,2,1,0:T(8,128)(2,1)S(1)}, bf16[2,2,64,256]{3,2,1,0:T(8,128)(2,1)S(1)}, u32[]{:S(2)}, u32[]{:S(2)}) collective-permute-start(bf16[2,2,64,256]{3,2,1,0:T(8,128)(2,1)S(1)} %get-tuple-element.25), channel_id=1, source_target_pairs={{0,1},{1,0},{2,3},{3,2},{4,5},{5,4},{6,7},{7,6},{8,9},{9,8},{10,11... | collective-permute-start | bytes 393224 | tf_op jit(solution)/shard_map/ppermute | solution.py:299

commit v8 on v6

--- a/solution.py
+++ b/solution.py
@@ -145,7 +145,11 @@
     )(x0, w1, *in_hbm(g, w2, sp, gp))
 
 
-def edge_kernel(label, cross, chip, x0, x1, xw, hw, sums, w1, w2, o, copies, halo, hh):
+def edge_kernel(label, sharp, cross, chip, x0, x1, xw, hw, sums, w1, w2, inner, o, copies, temp, out_hbm, halo, hh, sems):
+    outs = [pltpu.make_async_copy(inner.at[f], out_hbm.at[f, 0, pl.ds(2, ROWS - 4)], sems.at[f]) for f in range(2)]
+    for cp in outs:
+        cp.start()
+    temp[...] = jnp.full((8, 128), sharp[0], F32)
     here, strips = lax.axis_index("strip"), lax.axis_size("strip")
     odd = lax.rem(here, 2)
     for f in range(2):
@@ -183,55 +187,38 @@
         row = jnp.concatenate([jnp.sum(tot[f], axis=0, keepdims=True) * scale, mark], axis=1)
         for n in range(copies.shape[0]):
             copies[n, f:f + 1] = row
-
-
-def edges(label, chip, cross, x0, x1, xw, hw, sums, w1, w2, members):
+    for cp in outs:
+        cp.wait()
+
+
+def edges(label, sharp, cross, chip, x0, x1, xw, hw, sums, w1, w2, inner, members):
     return pl.pallas_call(
         edge_kernel,
         name="edge_rows",
-        out_shape=(jax.ShapeDtypeStruct((4, 2, COLS, C), F32), jax.ShapeDtypeStruct((members, 2, C + 128), F32)),
-        in_specs=[SM] + [VM] * 9,
-        out_specs=(VM,) * 2,
+        out_shape=(jax.ShapeDtypeStruct((4, 2, COLS, C), F32), jax.ShapeDtypeStruct((members, 2, C + 128), F32),
+                   jax.ShapeDtypeStruct((8, 128), F32), jax.ShapeDtypeStruct((2, 1, ROWS, COLS, C), F32)),
+        in_specs=[SM] * 2 + [VM] * 10,
+        out_specs=(VM, VM, VM, HBM),
         scratch_shapes=[
             pltpu.VMEM((4, 2, COLS, 3 * C), BF),
             pltpu.VMEM((4, 2, COLS, 3 * C), BF),
+            pltpu.SemaphoreType.DMA((2,)),
         ],
         compiler_params=pltpu.CompilerParams(vmem_limit_bytes=24 * MIB),
         cost_estimate=pl.CostEstimate(flops=1_200_000_000, transcendentals=0, bytes_accessed=4_000_000),
-    )(label, cross, chip, x0, x1, xw, hw, sums, w1, w2)
-
-
-def write_kernel(o, oe, out_hbm, sems):
+    )(label, sharp, cross, chip, x0, x1, xw, hw, sums, w1, w2, inner)
+
+
+def head_kernel(sharp, tot, sproj, gproj, oe, partial_hbm, loss_ref, gs_hbm, gg_hbm, out_hbm, buf, sem, osem):
     outs = []
-    for f in range(2):
-        outs.append(pltpu.make_async_copy(o.at[f], out_hbm.at[f, 0, pl.ds(2, 12)], sems.at[3 * f]))
-        for k in range(2):
-            outs.append(pltpu.make_async_copy(oe.at[2 * f + k], out_hbm.at[f, 0, pl.ds(14 * k, 2)], sems.at[3 * f + 1 + k]))
-    for cp in outs:
-        cp.start()
-    for cp in outs:
-        cp.wait()
-
-
-def write(o, oe):
-    return pl.pallas_call(
-        write_kernel,
-        name="write_maps",
-        out_shape=jax.ShapeDtypeStruct((2, 1, ROWS, COLS, C), F32),
-        in_specs=[VM] * 2,
-        out_specs=HBM,
-        scratch_shapes=[pltpu.SemaphoreType.DMA((6,))],
-        compiler_params=pltpu.CompilerParams(vmem_limit_bytes=2 * MIB),
-        cost_estimate=pl.CostEstimate(flops=0, transcendentals=0, bytes_accessed=4_000_000),
-    )(o, oe)
-
-
-def head_kernel(sharp, tot, sproj, gproj, loss_ref, gs_hbm, gg_hbm, buf, sem):
+    for k in range(4):
+        outs.append(pltpu.make_async_copy(oe.at[k], out_hbm.at[k // 2, 0, pl.ds((ROWS - 2) * (k % 2), 2)], osem.at[k]))
+        outs[-1].start()
     pairs = tot.shape[1]
     s_pool = tot[0, :, :C].astype(BF)
     g_pool = tot[1, :, :C].astype(BF)
     label = tot[0, :, C:C + 1]
-    temp = sharp[0]
+    temp = sharp[0:1, 0:1]
     s_emb = jnp.dot(s_pool, sproj[...], preferred_element_type=F32)
     g_emb = jnp.dot(g_pool, gproj[...], preferred_element_type=F32)
     s_inv = lax.rsqrt(jnp.sum(s_emb * s_emb, axis=-1, keepdims=True) + 1e-06)
@@ -247,8 +234,6 @@
     matched = column == label
     lgrad = (ex / row_total - jnp.where(matched, 1.0, 0.0)).astype(BF)
 
-    outs = []
-
     def finish(k, unit_grad, unit, inverse, pool, dest):
         grad = ((unit_grad - unit * jnp.sum(unit * unit_grad, axis=-1, keepdims=True)) * inverse).astype(BF)
         for p in range(2):
@@ -271,17 +256,18 @@
         cp.wait()
 
 
-def head(sharp, tot, sproj, gproj):
+def head(sharp, tot, sproj, gproj, oe, out):
     return pl.pallas_call(
         head_kernel,
         name="contrastive_head",
         out_shape=(jax.ShapeDtypeStruct((1,), F32), jax.ShapeDtypeStruct((C, E), F32),
-                   jax.ShapeDtypeStruct((C, E), F32)),
-        in_specs=[SM] + [VM] * 3,
-        out_specs=(SM, HBM, HBM),
-        scratch_shapes=[pltpu.VMEM((2, C, E), F32), pltpu.SemaphoreType.DMA((4,))],
+                   jax.ShapeDtypeStruct((C, E), F32), jax.ShapeDtypeStruct(out.shape, F32)),
+        in_specs=[VM] * 5 + [HBM],
+        out_specs=(SM, HBM, HBM, HBM),
+        input_output_aliases={5: 3},
+        scratch_shapes=[pltpu.VMEM((2, C, E), F32), pltpu.SemaphoreType.DMA((4,)), pltpu.SemaphoreType.DMA((4,))],
         compiler_params=pltpu.CompilerParams(vmem_limit_bytes=16 * MIB),
-    )(sharp, tot, sproj, gproj)
+    )(sharp, tot, sproj, gproj, oe, out)
 
 
 def gather_groups(batch, strips, inner):
@@ -300,17 +286,16 @@
     cross, chip, x0, w1 = load(state_maps, goal_maps, w1)
     cross = lax.ppermute(cross, "strip", [(i, i + 2 * (i % 2) - 1) for i in range(1, strips - 1)])
     chip = lax.ppermute(chip, "strip", [(i, i ^ 1) for i in range(strips)])
-    xw, hw, o, sums, x1, w2, sp, gp = interior(x0, w1, goal_maps, w2, state_proj, goal_proj)
-    oe, copies = edges(pair_index, chip, cross, x0, x1, xw, hw, sums, w1, w2, 2 * strips)
+    xw, hw, inner, sums, x1, w2, sp, gp = interior(x0, w1, goal_maps, w2, state_proj, goal_proj)
+    oe, copies, temp, out = edges(
+        pair_index, inv_temp, cross, chip, x0, x1, xw, hw, sums, w1, w2, inner, 2 * strips)
     both = ("batch", "strip")
     line = lax.all_to_all(copies, both, 0, 0, tiled=True, axis_index_groups=gather_groups(batch, strips, True))
     means = jnp.sum(line.reshape(2, strips, 2, C + 128), axis=1).astype(BF).reshape(4, C + 128)
     copies = jnp.broadcast_to(means, (batch // 2, 4, C + 128))
     got = lax.all_to_all(copies, both, 0, 0, tiled=True, axis_index_groups=gather_groups(batch, strips, False))
     tot = jnp.transpose(got.reshape(batch // 2, 2, 2, C + 128).astype(F32), (2, 1, 0, 3)).reshape(2, batch, C + 128)
-    out = write(o, oe)
-    loss, gs, gg = head(inv_temp, tot, sp, gp)
-    return loss, gs, gg, out
+    return head(temp, tot, sp, gp, oe, out)
 
 
 def solution(mesh):

time: 47.6 us -> 47.4 us (level)
  blocking collectives: 14.9 us -> 27.5 us
  starting transfers between devices: 13.1 us -> 6.38 us
  waiting for transfers between devices: 4.49 us -> 0.01 us
  Pallas kernels: 12.1 us -> 11.1 us
  local copies, waits for them, and re-layouts: 0.68 us -> 0.06 us
    all_to_all x1 -> x2, blocking collectives: 14.9 us -> 27.5 us  [shards(): lax.all_to_all(copies, both, 0, 0, tiled=True, axis_index_groups=gather_g...]
    all_to_all x1 -> x0, starting transfers between devices: 6.76 us -> none  [shards(): lax.all_to_all(copies, both, 0, 0, tiled=True, axis_index_groups=gather_g...]
    all_to_all x1 -> x0, waiting for transfers between devices: 4.48 us -> none  [shards(): lax.all_to_all(copies, both, 0, 0, tiled=True, axis_index_groups=gather_g...]
    pallas_call x1 -> x0, Pallas kernels: 1.36 us -> none  [write(): pl.pallas_call(write_kernel, name='write_maps', out_shape=jax.ShapeDtypeS...]
    broadcast_in_dim x1, local copies, waits for them, and re-layouts: 0.64 us -> 0.02 us  [shards(): copies = jnp.broadcast_to(means, (batch // 2, 4, C + 128))]
  transfers between devices with their start and end apart: 3 -> 2, of which waited for: 1 -> 0; matrix products, arithmetic and copies ran while one was open for 0% -> 0% of each run, Pallas kernels for 13% -> 10%
where the time goes in v8:
time: 47.4 us; the launch traced here: 47.1 us
  blocking collectives  27.5 us (58%)
  Pallas kernels  11.1 us (23%)
  starting transfers between devices  6.38 us (13%)
  between operations  2.01 us (4%)
    all_to_all x2, blocking collectives, shards(): lax.all_to_all(copies, both, 0, 0, tiled=True, axis_index_groups=gather_g...  27.5 us
    ppermute x1, starting transfers between devices, shards(): lax.ppermute(cross, 'strip', [(i, i + 2 * (i % 2) - 1) for i in range(1,...  6.29 us
    pallas_call x1, Pallas kernels, interior(): pl.pallas_call(functools.partial(interior_kernel, step1, step2), name='in...  4.6 us
    pallas_call x1, Pallas kernels, head(): pl.pallas_call(head_kernel, name='contrastive_head', out_shape=(jax.Shape...  3.05 us
    pallas_call x1, Pallas kernels, edges(): pl.pallas_call(edge_kernel, name='edge_rows', out_shape=(jax.ShapeDtypeSt...  1.87 us
    pallas_call x1, Pallas kernels, load(): pl.pallas_call(load_kernel, name='load_rows', out_shape=(side, side, jax....  1.61 us
  transfers between devices with their start and end apart: 2, of which 0 were waited for; matrix products, arithmetic and copies ran while one was open for 0% of the time, Pallas kernels for 10%

profile of v8, /device:TPU:1, one launch (start us, length us, event | category | flops | bytes accessed | tf_op | source)
XLA Modules:
  0.0 47.1 jit_solution(5558992089909151121)
XLA Ops:
  0.6 1.6 %load_rows.1 = (bf16[2,2,64,256]{3,2,1,0:T(8,128)(2,1)S(1)}, bf16[2,2,64,256]{3,2,1,0:T(8,128)(2,1)S(1)}, bf16[1,16,64,256]{3,2,1,0:T(8,128)(2,1)S(1)}, bf16[3,768,256]{2,1,0:T(8,128)(2,1)S(1)}) custom-call(bf16[1,16,64,256]{3,2,1,0:T(8,128)(2,1)} %s_hbm.1, bf16[1,16,64,256]{3,2,1,0:T(8,128)(2,1)} %g_hbm.3, bf16[3,768,256]{2,1,0:T(8,128)(2,1)} %bitcast.10), custom_call_target="tpu_custom_call" | custom-call | tf_op jit(solution)/shard_map/load_rows/pallas_call | solution.py:41
  2.3 6.3 %collective-permute-start = (bf16[2,2,64,256]{3,2,1,0:T(8,128)(2,1)S(1)}, bf16[2,2,64,256]{3,2,1,0:T(8,128)(2,1)S(1)}, u32[]{:S(2)}, u32[]{:S(2)}) collective-permute-start(bf16[2,2,64,256]{3,2,1,0:T(8,128)(2,1)S(1)} %get-tuple-element.20), channel_id=1, source_target_pairs={{1,2},{2,1},{3,4},{4,3},{5,6},{6,5},{9,10},{10,9},{11,12},{12,11},... | collective-permute-start | bytes 393224 | tf_op jit(solution)/shard_map/ppermute | solution.py:287
  8.6 0.1 collective-permute-start.1
  8.7 4.6 %interior_rows.1 = (bf16[2,16,64,768]{3,2,1,0:T(8,128)(2,1)S(1)}, bf16[2,14,64,768]{3,2,1,0:T(8,128)(2,1)S(1)}, f32[2,12,64,256]{3,2,1,0:T(8,128)S(1)}, f32[2,8,...) custom-call(bf16[1,16,64,256]{3,2,1,0:T(8,128)(2,1)S(1)} %get-tuple-, ...), custom_call_target="tpu_custom_call" | custom-call | flops 4200000000 | bytes 6000000 | tf_op jit(solution)/shard_map/interior_rows/pallas_call | solution.py:132
  14.6 0.0 collective-permute-done.cross
  14.6 0.0 collective-permute-done.1.chip
  14.6 1.9 %edge_rows.1 = (f32[4,2,64,256]{3,2,1,0:T(8,128)S(1)}, f32[16,2,384]{2,1,0:T(2,128)S(1)}, f32[8,128]{1,0:T(8,128)S(1)}, f32[2,1,16,64,256]{4,3,2,1,0:T(8,128)}) custom-call(s32[1]{0:T(128)S(6)} %copy.18.label, f32[1]{0:T(128)S(6)} %copy.17.sharp, bf16[2,2,64,256]{3,2,1,0:T(8,128)(2,1)S(1)} %collective-permute-done.cross, ...), custom_call_target="tpu_custom_call" | custom-call | flops 1200000000 | bytes 4000000 | tf_op jit(solution)/shard_map/edge_rows/pallas_call | solution.py:195
  16.5 14.4 %all_to_all.10 = f32[16,2,384]{2,1,0:T(2,128)S(1)} all-to-all(f32[16,2,384]{2,1,0:T(2,128)S(1)} %get-tuple-element.31), channel_id=1, replica_groups={{0,1,2,3,4,5,6,7,128,129,130,131,132,133,134,135},{8,9,10,11,12,13,14,1..., dimensions={0} | all-to-all | bytes 98304 | tf_op jit(solution)/shard_map/all_to_all | solution.py:293
  31.0 13.1 %all_to_all.11 = bf16[16,4,384]{2,1,0:T(4,128)(2,1)S(1)} all-to-all(bf16[16,4,384]{2,1,0:T(4,128)(2,1)S(1)} %broadcast_in_dim.3), channel_id=1, replica_groups={{0,8,16,24,32,40,48,56,64,72,80,88,96,104,112,120},{1,9,17,25,33,41,49,..., dimensions={0} | all-to-all | bytes 98304 | tf_op jit(solution)/shard_map/all_to_all | solution.py:296
  44.1 3.1 %contrastive_head.1 = (f32[1]{0:T(128)}, f32[256,1024]{1,0:T(8,128)}, f32[256,1024]{1,0:T(8,128)}, f32[2,1,16,64,256]{4,3,2,1,0:T(8,128)}) custom-call(f32[8,128]{1,0:T(8,128)S(1)} %get-tuple-element.30.sharp, f32[2,32,384]{2,1,0:T(8,128)S(1)} %bitcast.9, bf16[256,1024]{1,0:T(8,128)(2,1)S(1)} %get-tuple-element.32.sproj, ...), custom_call_target="tpu_custom_call", output_to_operand_aliasing={{3}: (5, {})} | custom-call | tf_op jit(solution)/shard_map/contrastive_head/pallas_call | solution.py:260
  (6 shorter events, 0.1 us)
Async XLA Ops:
  2.3 12.3 %collective-permute-start = (bf16[2,2,64,256]{3,2,1,0:T(8,128)(2,1)S(1)}, bf16[2,2,64,256]{3,2,1,0:T(8,128)(2,1)S(1)}, u32[]{:S(2)}, u32[]{:S(2)}) collective-permute-start(bf16[2,2,64,256]{3,2,1,0:T(8,128)(2,1)S(1)} %get-tuple-element.20), channel_id=1, source_target_pairs={{1,2},{2,1},{3,4},{4,3},{5,6},{6,5},{9,10},{10,9},{11,12},{12,11},... | collective-permute-start | bytes 393224 | tf_op jit(solution)/shard_map/ppermute | solution.py:287
  8.6 6.0 %collective-permute-start.1 = (bf16[2,2,64,256]{3,2,1,0:T(8,128)(2,1)S(1)}, bf16[2,2,64,256]{3,2,1,0:T(8,128)(2,1)S(1)}, u32[]{:S(2)}, u32[]{:S(2)}) collective-permute-start(bf16[2,2,64,256]{3,2,1,0:T(8,128)(2,1)S(1)} %get-tuple-element.21), channel_id=1, source_target_pairs={{0,1},{1,0},{2,3},{3,2},{4,5},{5,4},{6,7},{7,6},{8,9},{9,8},{10,11... | collective-permute-start | bytes 393224 | tf_op jit(solution)/shard_map/ppermute | solution.py:288

commit v9 on v8

--- a/solution.py
+++ b/solution.py
@@ -78,7 +78,7 @@
     return [(r, min(step, total - r)) for r in range(0, total, step)]
 
 
-def interior_kernel(step1, step2, x0, w1, g_hbm, w2_hbm, sp_hbm, gp_hbm, xw, hw, o, sum_ref, x1, w2, sp, gp, sems):
+def interior_kernel(step1, step2, x0, w1, g_hbm, w2_hbm, sp_hbm, gp_hbm, xw, hw, o, sum_ref, x1, w2, sp, gp, out_hbm, sems):
     cw2 = pltpu.make_async_copy(w2_hbm, w2, sems.at[0])
     csp = pltpu.make_async_copy(sp_hbm, sp, sems.at[1])
     cgp = pltpu.make_async_copy(gp_hbm, gp, sems.at[2])
@@ -118,13 +118,15 @@
         spread(1, range(i * 16 // len(plan), (i + 1) * 16 // len(plan)))
         acc = second(0, r, n, acc)
     sum_ref[0] = acc
+    cout = pltpu.make_async_copy(o.at[0], out_hbm.at[0, 0, pl.ds(2, ROWS - 4)], sems.at[4])
+    cout.start()
     for r, n in spans(14, step1):
         first(1, r, n)
     acc = None
     for r, n in spans(12, step2):
         acc = second(1, r, n, acc)
     sum_ref[1] = acc
-    csp.wait(); cgp.wait()
+    csp.wait(); cgp.wait(); cout.wait()
 
 
 def interior(x0, w1, g, w2, sp, gp, step1=7, step2=4):
@@ -136,19 +138,20 @@
                    jax.ShapeDtypeStruct((2, 14, COLS, 3 * C), BF),
                    jax.ShapeDtypeStruct((2, 12, COLS, C), F32),
                    jax.ShapeDtypeStruct((2, 8, C), F32), jax.ShapeDtypeStruct(x0.shape, BF),
-                   jax.ShapeDtypeStruct(w2.shape, BF), proj, proj),
+                   jax.ShapeDtypeStruct(w2.shape, BF), proj, proj,
+                   jax.ShapeDtypeStruct((2, 1, ROWS, COLS, C), F32)),
         in_specs=[VM] * 2 + [HBM] * 4,
-        out_specs=(VM,) * 8,
-        scratch_shapes=[pltpu.SemaphoreType.DMA((4,))],
+        out_specs=(VM,) * 8 + (HBM,),
+        scratch_shapes=[pltpu.SemaphoreType.DMA((5,))],
         compiler_params=pltpu.CompilerParams(vmem_limit_bytes=24 * MIB),
         cost_estimate=pl.CostEstimate(flops=4_200_000_000, transcendentals=0, bytes_accessed=6_000_000),
     )(x0, w1, *in_hbm(g, w2, sp, gp))
 
 
-def edge_kernel(label, sharp, cross, chip, x0, x1, xw, hw, sums, w1, w2, inner, o, copies, temp, out_hbm, halo, hh, sems):
-    outs = [pltpu.make_async_copy(inner.at[f], out_hbm.at[f, 0, pl.ds(2, ROWS - 4)], sems.at[f]) for f in range(2)]
-    for cp in outs:
-        cp.start()
+def edge_kernel(label, sharp, cross, chip, x0, x1, xw, hw, sums, w1, w2, inner, partial_hbm,
+                o, copies, temp, out_hbm, halo, hh, sem):
+    cout = pltpu.make_async_copy(inner.at[1], out_hbm.at[1, 0, pl.ds(2, ROWS - 4)], sem)
+    cout.start()
     temp[...] = jnp.full((8, 128), sharp[0], F32)
     here, strips = lax.axis_index("strip"), lax.axis_size("strip")
     odd = lax.rem(here, 2)
@@ -187,26 +190,26 @@
         row = jnp.concatenate([jnp.sum(tot[f], axis=0, keepdims=True) * scale, mark], axis=1)
         for n in range(copies.shape[0]):
             copies[n, f:f + 1] = row
-    for cp in outs:
-        cp.wait()
-
-
-def edges(label, sharp, cross, chip, x0, x1, xw, hw, sums, w1, w2, inner, members):
+    cout.wait()
+
+
+def edges(label, sharp, cross, chip, x0, x1, xw, hw, sums, w1, w2, inner, out, members):
     return pl.pallas_call(
         edge_kernel,
         name="edge_rows",
         out_shape=(jax.ShapeDtypeStruct((4, 2, COLS, C), F32), jax.ShapeDtypeStruct((members, 2, C + 128), F32),
-                   jax.ShapeDtypeStruct((8, 128), F32), jax.ShapeDtypeStruct((2, 1, ROWS, COLS, C), F32)),
-        in_specs=[SM] * 2 + [VM] * 10,
+                   jax.ShapeDtypeStruct((8, 128), F32), jax.ShapeDtypeStruct(out.shape, F32)),
+        in_specs=[SM] * 2 + [VM] * 10 + [HBM],
         out_specs=(VM, VM, VM, HBM),
+        input_output_aliases={12: 3},
         scratch_shapes=[
             pltpu.VMEM((4, 2, COLS, 3 * C), BF),
             pltpu.VMEM((4, 2, COLS, 3 * C), BF),
-            pltpu.SemaphoreType.DMA((2,)),
+            pltpu.SemaphoreType.DMA,
         ],
         compiler_params=pltpu.CompilerParams(vmem_limit_bytes=24 * MIB),
         cost_estimate=pl.CostEstimate(flops=1_200_000_000, transcendentals=0, bytes_accessed=4_000_000),
-    )(label, sharp, cross, chip, x0, x1, xw, hw, sums, w1, w2, inner)
+    )(label, sharp, cross, chip, x0, x1, xw, hw, sums, w1, w2, inner, out)
 
 
 def head_kernel(sharp, tot, sproj, gproj, oe, partial_hbm, loss_ref, gs_hbm, gg_hbm, out_hbm, buf, sem, osem):
@@ -286,9 +289,9 @@
     cross, chip, x0, w1 = load(state_maps, goal_maps, w1)
     cross = lax.ppermute(cross, "strip", [(i, i + 2 * (i % 2) - 1) for i in range(1, strips - 1)])
     chip = lax.ppermute(chip, "strip", [(i, i ^ 1) for i in range(strips)])
-    xw, hw, inner, sums, x1, w2, sp, gp = interior(x0, w1, goal_maps, w2, state_proj, goal_proj)
+    xw, hw, inner, sums, x1, w2, sp, gp, out = interior(x0, w1, goal_maps, w2, state_proj, goal_proj)
     oe, copies, temp, out = edges(
-        pair_index, inv_temp, cross, chip, x0, x1, xw, hw, sums, w1, w2, inner, 2 * strips)
+        pair_index, inv_temp, cross, chip, x0, x1, xw, hw, sums, w1, w2, inner, out, 2 * strips)
     both = ("batch", "strip")
     line = lax.all_to_all(copies, both, 0, 0, tiled=True, axis_index_groups=gather_groups(batch, strips, True))
     means = jnp.sum(line.reshape(2, strips, 2, C + 128), axis=1).astype(BF).reshape(4, C + 128)

time: 47.4 us -> 47.1 us (level)
  no operation moved by 1% of the time
where the time goes in v9:
time: 47.1 us; the launch traced here: 46.8 us
  blocking collectives  27.5 us (58%)
  Pallas kernels  10.8 us (23%)
  starting transfers between devices  6.38 us (14%)
  between operations  2.01 us (4%)
    all_to_all x2, blocking collectives, shards(): lax.all_to_all(copies, both, 0, 0, tiled=True, axis_index_groups=gather_g...  27.5 us
    ppermute x1, starting transfers between devices, shards(): lax.ppermute(cross, 'strip', [(i, i + 2 * (i % 2) - 1) for i in range(1,...  6.29 us
    pallas_call x1, Pallas kernels, interior(): pl.pallas_call(functools.partial(interior_kernel, step1, step2), name='in...  4.61 us
    pallas_call x1, Pallas kernels, head(): pl.pallas_call(head_kernel, name='contrastive_head', out_shape=(jax.Shape...  3.05 us
    pallas_call x1, Pallas kernels, load(): pl.pallas_call(load_kernel, name='load_rows', out_shape=(side, side, jax....  1.61 us
    pallas_call x1, Pallas kernels, edges(): pl.pallas_call(edge_kernel, name='edge_rows', out_shape=(jax.ShapeDtypeSt...  1.56 us
  transfers between devices with their start and end apart: 2, of which 0 were waited for; matrix products, arithmetic and copies ran while one was open for 0% of the time, Pallas kernels for 10%

profile of v9, /device:TPU:1, one launch (start us, length us, event | category | flops | bytes accessed | tf_op | source)
XLA Modules:
  0.0 46.8 jit_solution(11540420878284373471)
XLA Ops:
  0.6 1.6 %load_rows.1 = (bf16[2,2,64,256]{3,2,1,0:T(8,128)(2,1)S(1)}, bf16[2,2,64,256]{3,2,1,0:T(8,128)(2,1)S(1)}, bf16[1,16,64,256]{3,2,1,0:T(8,128)(2,1)S(1)}, bf16[3,768,256]{2,1,0:T(8,128)(2,1)S(1)}) custom-call(bf16[1,16,64,256]{3,2,1,0:T(8,128)(2,1)} %s_hbm.1, bf16[1,16,64,256]{3,2,1,0:T(8,128)(2,1)} %g_hbm.3, bf16[3,768,256]{2,1,0:T(8,128)(2,1)} %bitcast.10), custom_call_target="tpu_custom_call" | custom-call | tf_op jit(solution)/shard_map/load_rows/pallas_call | solution.py:41
  2.3 6.3 %collective-permute-start = (bf16[2,2,64,256]{3,2,1,0:T(8,128)(2,1)S(1)}, bf16[2,2,64,256]{3,2,1,0:T(8,128)(2,1)S(1)}, u32[]{:S(2)}, u32[]{:S(2)}) collective-permute-start(bf16[2,2,64,256]{3,2,1,0:T(8,128)(2,1)S(1)} %get-tuple-element.21), channel_id=1, source_target_pairs={{1,2},{2,1},{3,4},{4,3},{5,6},{6,5},{9,10},{10,9},{11,12},{12,11},... | collective-permute-start | bytes 393224 | tf_op jit(solution)/shard_map/ppermute | solution.py:290
  8.6 0.1 collective-permute-start.1
  8.7 4.6 %interior_rows.1 = (bf16[2,16,64,768]{3,2,1,0:T(8,128)(2,1)S(1)}, bf16[2,14,64,768]{3,2,1,0:T(8,128)(2,1)S(1)}, f32[2,12,64,256]{3,2,1,0:T(8,128)S(1)}, f32[2,8,...) custom-call(bf16[1,16,64,256]{3,2,1,0:T(8,128)(2,1)S(1)} %get-tuple-, ...), custom_call_target="tpu_custom_call" | custom-call | flops 4200000000 | bytes 6000000 | tf_op jit(solution)/shard_map/interior_rows/pallas_call | solution.py:134
  14.6 0.0 collective-permute-done.cross
  14.6 0.0 collective-permute-done.1.chip
  14.6 1.6 %edge_rows.1 = (f32[4,2,64,256]{3,2,1,0:T(8,128)S(1)}, f32[16,2,384]{2,1,0:T(2,128)S(1)}, f32[8,128]{1,0:T(8,128)S(1)}, f32[2,1,16,64,256]{4,3,2,1,0:T(8,128)}) custom-call(s32[1]{0:T(128)S(6)} %copy.20.label, f32[1]{0:T(128)S(6)} %copy.19.sharp, bf16[2,2,64,256]{3,2,1,0:T(8,128)(2,1)S(1)} %collective-permute-done.cross, ...), custom_call_target="tpu_custom_call", output_to_operand_aliasing={{3}: (12, {})} | custom-call | flops 1200000000 | bytes 4000000 | tf_op jit(solution)/shard_map/edge_rows/pallas_call | solution.py:197
  16.1 14.4 %all_to_all.10 = f32[16,2,384]{2,1,0:T(2,128)S(1)} all-to-all(f32[16,2,384]{2,1,0:T(2,128)S(1)} %get-tuple-element.33), channel_id=1, replica_groups={{0,1,2,3,4,5,6,7,128,129,130,131,132,133,134,135},{8,9,10,11,12,13,14,1..., dimensions={0} | all-to-all | bytes 98304 | tf_op jit(solution)/shard_map/all_to_all | solution.py:296
  30.7 13.0 %all_to_all.11 = bf16[16,4,384]{2,1,0:T(4,128)(2,1)S(1)} all-to-all(bf16[16,4,384]{2,1,0:T(4,128)(2,1)S(1)} %broadcast_in_dim.3), channel_id=1, replica_groups={{0,8,16,24,32,40,48,56,64,72,80,88,96,104,112,120},{1,9,17,25,33,41,49,..., dimensions={0} | all-to-all | bytes 98304 | tf_op jit(solution)/shard_map/all_to_all | solution.py:299
  43.8 3.0 %contrastive_head.1 = (f32[1]{0:T(128)}, f32[256,1024]{1,0:T(8,128)}, f32[256,1024]{1,0:T(8,128)}, f32[2,1,16,64,256]{4,3,2,1,0:T(8,128)}) custom-call(f32[8,128]{1,0:T(8,128)S(1)} %get-tuple-element.32.sharp, f32[2,32,384]{2,1,0:T(8,128)S(1)} %bitcast.9, bf16[256,1024]{1,0:T(8,128)(2,1)S(1)} %get-tuple-element.34.sproj, ...), custom_call_target="tpu_custom_call", output_to_operand_aliasing={{3}: (5, {})} | custom-call | tf_op jit(solution)/shard_map/contrastive_head/pallas_call | solution.py:263
  (6 shorter events, 0.1 us)
Async XLA Ops:
  2.3 12.3 %collective-permute-start = (bf16[2,2,64,256]{3,2,1,0:T(8,128)(2,1)S(1)}, bf16[2,2,64,256]{3,2,1,0:T(8,128)(2,1)S(1)}, u32[]{:S(2)}, u32[]{:S(2)}) collective-permute-start(bf16[2,2,64,256]{3,2,1,0:T(8,128)(2,1)S(1)} %get-tuple-element.21), channel_id=1, source_target_pairs={{1,2},{2,1},{3,4},{4,3},{5,6},{6,5},{9,10},{10,9},{11,12},{12,11},... | collective-permute-start | bytes 393224 | tf_op jit(solution)/shard_map/ppermute | solution.py:290
  8.6 6.0 %collective-permute-start.1 = (bf16[2,2,64,256]{3,2,1,0:T(8,128)(2,1)S(1)}, bf16[2,2,64,256]{3,2,1,0:T(8,128)(2,1)S(1)}, u32[]{:S(2)}, u32[]{:S(2)}) collective-permute-start(bf16[2,2,64,256]{3,2,1,0:T(8,128)(2,1)S(1)} %get-tuple-element.22), channel_id=1, source_target_pairs={{0,1},{1,0},{2,3},{3,2},{4,5},{5,4},{6,7},{7,6},{8,9},{9,8},{10,11... | collective-permute-start | bytes 393224 | tf_op jit(solution)/shard_map/ppermute | solution.py:291

commit v10 on v9

--- a/solution.py
+++ b/solution.py
@@ -148,7 +148,7 @@
     )(x0, w1, *in_hbm(g, w2, sp, gp))
 
 
-def edge_kernel(label, sharp, cross, chip, x0, x1, xw, hw, sums, w1, w2, inner, partial_hbm,
+def edge_kernel(label, sharp, chip, cross, x0, x1, xw, hw, sums, w1, w2, inner, partial_hbm,
                 o, copies, temp, out_hbm, halo, hh, sem):
     cout = pltpu.make_async_copy(inner.at[1], out_hbm.at[1, 0, pl.ds(2, ROWS - 4)], sem)
     cout.start()
@@ -209,7 +209,7 @@
         ],
         compiler_params=pltpu.CompilerParams(vmem_limit_bytes=24 * MIB),
         cost_estimate=pl.CostEstimate(flops=1_200_000_000, transcendentals=0, bytes_accessed=4_000_000),
-    )(label, sharp, cross, chip, x0, x1, xw, hw, sums, w1, w2, inner, out)
+    )(label, sharp, chip, cross, x0, x1, xw, hw, sums, w1, w2, inner, out)
 
 
 def head_kernel(sharp, tot, sproj, gproj, oe, partial_hbm, loss_ref, gs_hbm, gg_hbm, out_hbm, buf, sem, osem):

time: 47.1 us -> 47 us (level)
    ppermute x1, starting transfers between devices: 0.09 us -> 3.33 us  [shards(): chip = lax.ppermute(chip, 'strip', [(i, i ^ 1) for i in range(strips)])]
    ppermute x1, starting transfers between devices: 6.29 us -> 3.06 us  [shards(): lax.ppermute(cross, 'strip', [(i, i + 2 * (i % 2) - 1) for i in range(1,...]
where the time goes in v10:
time: 47 us; the launch traced here: 46.7 us
  blocking collectives  27.4 us (58%)
  Pallas kernels  10.8 us (23%)
  starting transfers between devices  6.39 us (14%)
  between operations  2 us (4%)
    all_to_all x2, blocking collectives, shards(): lax.all_to_all(copies, both, 0, 0, tiled=True, axis_index_groups=gather_g...  27.4 us
    pallas_call x1, Pallas kernels, interior(): pl.pallas_call(functools.partial(interior_kernel, step1, step2), name='in...  4.61 us
    ppermute x1, starting transfers between devices, shards(): chip = lax.ppermute(chip, 'strip', [(i, i ^ 1) for i in range(strips)])  3.33 us
    ppermute x1, starting transfers between devices, shards(): lax.ppermute(cross, 'strip', [(i, i + 2 * (i % 2) - 1) for i in range(1,...  3.06 us
    pallas_call x1, Pallas kernels, head(): pl.pallas_call(head_kernel, name='contrastive_head', out_shape=(jax.Shape...  3.05 us
    pallas_call x1, Pallas kernels, load(): pl.pallas_call(load_kernel, name='load_rows', out_shape=(side, side, jax....  1.61 us
    pallas_call x1, Pallas kernels, edges(): pl.pallas_call(edge_kernel, name='edge_rows', out_shape=(jax.ShapeDtypeSt...  1.56 us
  transfers between devices with their start and end apart: 2, of which 0 were waited for; matrix products, arithmetic and copies ran while one was open for 0% of the time, Pallas kernels for 10%

profile of v10, /device:TPU:1, one launch (start us, length us, event | category | flops | bytes accessed | tf_op | source)
XLA Modules:
  0.0 46.7 jit_solution(9133797780617253400)
XLA Ops:
  0.6 1.6 %load_rows.1 = (bf16[2,2,64,256]{3,2,1,0:T(8,128)(2,1)S(1)}, bf16[2,2,64,256]{3,2,1,0:T(8,128)(2,1)S(1)}, bf16[1,16,64,256]{3,2,1,0:T(8,128)(2,1)S(1)}, bf16[3,768,256]{2,1,0:T(8,128)(2,1)S(1)}) custom-call(bf16[1,16,64,256]{3,2,1,0:T(8,128)(2,1)} %s_hbm.1, bf16[1,16,64,256]{3,2,1,0:T(8,128)(2,1)} %g_hbm.3, bf16[3,768,256]{2,1,0:T(8,128)(2,1)} %bitcast.10), custom_call_target="tpu_custom_call" | custom-call | tf_op jit(solution)/shard_map/load_rows/pallas_call | solution.py:41
  2.3 3.3 %collective-permute-start = (bf16[2,2,64,256]{3,2,1,0:T(8,128)(2,1)S(1)}, bf16[2,2,64,256]{3,2,1,0:T(8,128)(2,1)S(1)}, u32[]{:S(2)}, u32[]{:S(2)}) collective-permute-start(bf16[2,2,64,256]{3,2,1,0:T(8,128)(2,1)S(1)} %get-tuple-element.21), channel_id=1, source_target_pairs={{0,1},{1,0},{2,3},{3,2},{4,5},{5,4},{6,7},{7,6},{8,9},{9,8},{10,11... | collective-permute-start | bytes 393224 | tf_op jit(solution)/shard_map/ppermute | solution.py:291
  5.6 3.1 %collective-permute-start.1 = (bf16[2,2,64,256]{3,2,1,0:T(8,128)(2,1)S(1)}, bf16[2,2,64,256]{3,2,1,0:T(8,128)(2,1)S(1)}, u32[]{:S(2)}, u32[]{:S(2)}) collective-permute-start(bf16[2,2,64,256]{3,2,1,0:T(8,128)(2,1)S(1)} %get-tuple-element.22), channel_id=1, source_target_pairs={{1,2},{2,1},{3,4},{4,3},{5,6},{6,5},{9,10},{10,9},{11,12},{12,11},... | collective-permute-start | bytes 393224 | tf_op jit(solution)/shard_map/ppermute | solution.py:290
  8.7 4.6 %interior_rows.1 = (bf16[2,16,64,768]{3,2,1,0:T(8,128)(2,1)S(1)}, bf16[2,14,64,768]{3,2,1,0:T(8,128)(2,1)S(1)}, f32[2,12,64,256]{3,2,1,0:T(8,128)S(1)}, f32[2,8,...) custom-call(bf16[1,16,64,256]{3,2,1,0:T(8,128)(2,1)S(1)} %get-tuple-, ...), custom_call_target="tpu_custom_call" | custom-call | flops 4200000000 | bytes 6000000 | tf_op jit(solution)/shard_map/interior_rows/pallas_call | solution.py:134
  14.6 0.0 collective-permute-done.chip
  14.6 0.0 collective-permute-done.1.cross
  14.6 1.6 %edge_rows.1 = (f32[4,2,64,256]{3,2,1,0:T(8,128)S(1)}, f32[16,2,384]{2,1,0:T(2,128)S(1)}, f32[8,128]{1,0:T(8,128)S(1)}, f32[2,1,16,64,256]{4,3,2,1,0:T(8,128)}) custom-call(s32[1]{0:T(128)S(6)} %copy.20.label, f32[1]{0:T(128)S(6)} %copy.19.sharp, bf16[2,2,64,256]{3,2,1,0:T(8,128)(2,1)S(1)} %collective-permute-done.chip, ...), custom_call_target="tpu_custom_call", output_to_operand_aliasing={{3}: (12, {})} | custom-call | flops 1200000000 | bytes 4000000 | tf_op jit(solution)/shard_map/edge_rows/pallas_call | solution.py:197
  16.1 14.4 %all_to_all.10 = f32[16,2,384]{2,1,0:T(2,128)S(1)} all-to-all(f32[16,2,384]{2,1,0:T(2,128)S(1)} %get-tuple-element.33), channel_id=1, replica_groups={{0,1,2,3,4,5,6,7,128,129,130,131,132,133,134,135},{8,9,10,11,12,13,14,1..., dimensions={0} | all-to-all | bytes 98304 | tf_op jit(solution)/shard_map/all_to_all | solution.py:296
  30.6 13.1 %all_to_all.11 = bf16[16,4,384]{2,1,0:T(4,128)(2,1)S(1)} all-to-all(bf16[16,4,384]{2,1,0:T(4,128)(2,1)S(1)} %broadcast_in_dim.3), channel_id=1, replica_groups={{0,8,16,24,32,40,48,56,64,72,80,88,96,104,112,120},{1,9,17,25,33,41,49,..., dimensions={0} | all-to-all | bytes 98304 | tf_op jit(solution)/shard_map/all_to_all | solution.py:299
  43.7 3.0 %contrastive_head.1 = (f32[1]{0:T(128)}, f32[256,1024]{1,0:T(8,128)}, f32[256,1024]{1,0:T(8,128)}, f32[2,1,16,64,256]{4,3,2,1,0:T(8,128)}) custom-call(f32[8,128]{1,0:T(8,128)S(1)} %get-tuple-element.32.sharp, f32[2,32,384]{2,1,0:T(8,128)S(1)} %bitcast.9, bf16[256,1024]{1,0:T(8,128)(2,1)S(1)} %get-tuple-element.34.sproj, ...), custom_call_target="tpu_custom_call", output_to_operand_aliasing={{3}: (5, {})} | custom-call | tf_op jit(solution)/shard_map/contrastive_head/pallas_call | solution.py:263
  (6 shorter events, 0.1 us)
Async XLA Ops:
  2.3 12.3 %collective-permute-start = (bf16[2,2,64,256]{3,2,1,0:T(8,128)(2,1)S(1)}, bf16[2,2,64,256]{3,2,1,0:T(8,128)(2,1)S(1)}, u32[]{:S(2)}, u32[]{:S(2)}) collective-permute-start(bf16[2,2,64,256]{3,2,1,0:T(8,128)(2,1)S(1)} %get-tuple-element.21), channel_id=1, source_target_pairs={{0,1},{1,0},{2,3},{3,2},{4,5},{5,4},{6,7},{7,6},{8,9},{9,8},{10,11... | collective-permute-start | bytes 393224 | tf_op jit(solution)/shard_map/ppermute | solution.py:291
  5.6 9.0 %collective-permute-start.1 = (bf16[2,2,64,256]{3,2,1,0:T(8,128)(2,1)S(1)}, bf16[2,2,64,256]{3,2,1,0:T(8,128)(2,1)S(1)}, u32[]{:S(2)}, u32[]{:S(2)}) collective-permute-start(bf16[2,2,64,256]{3,2,1,0:T(8,128)(2,1)S(1)} %get-tuple-element.22), channel_id=1, source_target_pairs={{1,2},{2,1},{3,4},{4,3},{5,6},{6,5},{9,10},{10,9},{11,12},{12,11},... | collective-permute-start | bytes 393224 | tf_op jit(solution)/shard_map/ppermute | solution.py:290

commit v11 on v9

--- a/solution.py
+++ b/solution.py
@@ -186,10 +186,10 @@
         tot[f] = tot[f] + jnp.sum(y.reshape(16, 8, C), axis=0)
     scale = 1.0 / (strips * ROWS * COLS)
     mark = jnp.full((1, 128), label[0], jnp.int32).astype(F32) * (1.0 / strips)
-    for f in range(2):
-        row = jnp.concatenate([jnp.sum(tot[f], axis=0, keepdims=True) * scale, mark], axis=1)
-        for n in range(copies.shape[0]):
-            copies[n, f:f + 1] = row
+    both = jnp.concatenate(
+        [jnp.concatenate([jnp.sum(tot[f], axis=0, keepdims=True) * scale, mark], axis=1) for f in range(2)], axis=0).astype(BF)
+    for n in range(copies.shape[0]):
+        copies[n] = both
     cout.wait()
 
 
@@ -197,7 +197,7 @@
     return pl.pallas_call(
         edge_kernel,
         name="edge_rows",
-        out_shape=(jax.ShapeDtypeStruct((4, 2, COLS, C), F32), jax.ShapeDtypeStruct((members, 2, C + 128), F32),
+        out_shape=(jax.ShapeDtypeStruct((4, 2, COLS, C), F32), jax.ShapeDtypeStruct((members, 2, C + 128), BF),
                    jax.ShapeDtypeStruct((8, 128), F32), jax.ShapeDtypeStruct(out.shape, F32)),
         in_specs=[SM] * 2 + [VM] * 10 + [HBM],
         out_specs=(VM, VM, VM, HBM),
@@ -294,7 +294,7 @@
         pair_index, inv_temp, cross, chip, x0, x1, xw, hw, sums, w1, w2, inner, out, 2 * strips)
     both = ("batch", "strip")
     line = lax.all_to_all(copies, both, 0, 0, tiled=True, axis_index_groups=gather_groups(batch, strips, True))
-    means = jnp.sum(line.reshape(2, strips, 2, C + 128), axis=1).astype(BF).reshape(4, C + 128)
+    means = jnp.sum(line.reshape(2, strips, 2, C + 128).astype(F32), axis=1).astype(BF).reshape(4, C + 128)
     copies = jnp.broadcast_to(means, (batch // 2, 4, C + 128))
     got = lax.all_to_all(copies, both, 0, 0, tiled=True, axis_index_groups=gather_groups(batch, strips, False))
     tot = jnp.transpose(got.reshape(batch // 2, 2, 2, C + 128).astype(F32), (2, 1, 0, 3)).reshape(2, batch, C + 128)

time: 47.1 us -> 46.9 us (level)
  no operation moved by 1% of the time
where the time goes in v11:
time: 46.9 us; the launch traced here: 46.7 us
  blocking collectives  27.4 us (58%)
  Pallas kernels  10.8 us (23%)
  starting transfers between devices  6.38 us (14%)
  between operations  2 us (4%)
    all_to_all x2, blocking collectives, shards(): lax.all_to_all(copies, both, 0, 0, tiled=True, axis_index_groups=gather_g...  27.4 us
    ppermute x1, starting transfers between devices, shards(): lax.ppermute(cross, 'strip', [(i, i + 2 * (i % 2) - 1) for i in range(1,...  6.29 us
    pallas_call x1, Pallas kernels, interior(): pl.pallas_call(functools.partial(interior_kernel, step1, step2), name='in...  4.61 us
    pallas_call x1, Pallas kernels, head(): pl.pallas_call(head_kernel, name='contrastive_head', out_shape=(jax.Shape...  3.05 us
    pallas_call x1, Pallas kernels, load(): pl.pallas_call(load_kernel, name='load_rows', out_shape=(side, side, jax....  1.61 us
    pallas_call x1, Pallas kernels, edges(): pl.pallas_call(edge_kernel, name='edge_rows', out_shape=(jax.ShapeDtypeSt...  1.56 us
  transfers between devices with their start and end apart: 2, of which 0 were waited for; matrix products, arithmetic and copies ran while one was open for 0% of the time, Pallas kernels for 10%

profile of v11, /device:TPU:1, one launch (start us, length us, event | category | flops | bytes accessed | tf_op | source)
XLA Modules:
  0.0 46.7 jit_solution(17229129771273490041)
XLA Ops:
  0.6 1.6 %load_rows.1 = (bf16[2,2,64,256]{3,2,1,0:T(8,128)(2,1)S(1)}, bf16[2,2,64,256]{3,2,1,0:T(8,128)(2,1)S(1)}, bf16[1,16,64,256]{3,2,1,0:T(8,128)(2,1)S(1)}, bf16[3,768,256]{2,1,0:T(8,128)(2,1)S(1)}) custom-call(bf16[1,16,64,256]{3,2,1,0:T(8,128)(2,1)} %s_hbm.1, bf16[1,16,64,256]{3,2,1,0:T(8,128)(2,1)} %g_hbm.3, bf16[3,768,256]{2,1,0:T(8,128)(2,1)} %bitcast.10), custom_call_target="tpu_custom_call" | custom-call | tf_op jit(solution)/shard_map/load_rows/pallas_call | solution.py:41
  2.3 6.3 %collective-permute-start = (bf16[2,2,64,256]{3,2,1,0:T(8,128)(2,1)S(1)}, bf16[2,2,64,256]{3,2,1,0:T(8,128)(2,1)S(1)}, u32[]{:S(2)}, u32[]{:S(2)}) collective-permute-start(bf16[2,2,64,256]{3,2,1,0:T(8,128)(2,1)S(1)} %get-tuple-element.21), channel_id=1, source_target_pairs={{1,2},{2,1},{3,4},{4,3},{5,6},{6,5},{9,10},{10,9},{11,12},{12,11},... | collective-permute-start | bytes 393224 | tf_op jit(solution)/shard_map/ppermute | solution.py:290
  8.6 0.1 collective-permute-start.1
  8.7 4.6 %interior_rows.1 = (bf16[2,16,64,768]{3,2,1,0:T(8,128)(2,1)S(1)}, bf16[2,14,64,768]{3,2,1,0:T(8,128)(2,1)S(1)}, f32[2,12,64,256]{3,2,1,0:T(8,128)S(1)}, f32[2,8,...) custom-call(bf16[1,16,64,256]{3,2,1,0:T(8,128)(2,1)S(1)} %get-tuple-, ...), custom_call_target="tpu_custom_call" | custom-call | flops 4200000000 | bytes 6000000 | tf_op jit(solution)/shard_map/interior_rows/pallas_call | solution.py:134
  14.6 0.0 collective-permute-done.cross
  14.6 0.0 collective-permute-done.1.chip
  14.6 1.6 %edge_rows.1 = (f32[4,2,64,256]{3,2,1,0:T(8,128)S(1)}, bf16[16,2,384]{2,1,0:T(2,128)(2,1)S(1)}, f32[8,128]{1,0:T(8,128)S(1)}, f32[2,1,16,64,256]{4,3,2,1,0:T(8,128)}) custom-call(s32[1]{0:T(128)S(6)} %copy.20.label, f32[1]{0:T(128)S(6)} %copy.19.sharp, bf16[2,2,64,256]{3,2,1,0:T(8,128)(2,1)S(1)} %collective-permute-done.cross, ...), custom_call_target="tpu_custom_call", output_to_operand_aliasing={{3}: (12, {})} | custom-call | flops 1200000000 | bytes 4000000 | tf_op jit(solution)/shard_map/edge_rows/pallas_call | solution.py:197
  16.1 14.3 %all_to_all.10 = bf16[16,2,384]{2,1,0:T(2,128)(2,1)S(1)} all-to-all(bf16[16,2,384]{2,1,0:T(2,128)(2,1)S(1)} %get-tuple-element.33), channel_id=1, replica_groups={{0,1,2,3,4,5,6,7,128,129,130,131,132,133,134,135},{8,9,10,11,12,13,14,1..., dimensions={0} | all-to-all | bytes 49152 | tf_op jit(solution)/shard_map/all_to_all | solution.py:296
  30.6 13.0 %all_to_all.11 = bf16[16,4,384]{2,1,0:T(4,128)(2,1)S(1)} all-to-all(bf16[16,4,384]{2,1,0:T(4,128)(2,1)S(1)} %broadcast_in_dim.3), channel_id=1, replica_groups={{0,8,16,24,32,40,48,56,64,72,80,88,96,104,112,120},{1,9,17,25,33,41,49,..., dimensions={0} | all-to-all | bytes 98304 | tf_op jit(solution)/shard_map/all_to_all | solution.py:299
  43.7 3.0 %contrastive_head.1 = (f32[1]{0:T(128)}, f32[256,1024]{1,0:T(8,128)}, f32[256,1024]{1,0:T(8,128)}, f32[2,1,16,64,256]{4,3,2,1,0:T(8,128)}) custom-call(f32[8,128]{1,0:T(8,128)S(1)} %get-tuple-element.32.sharp, f32[2,32,384]{2,1,0:T(8,128)S(1)} %bitcast.9, bf16[256,1024]{1,0:T(8,128)(2,1)S(1)} %get-tuple-element.34.sproj, ...), custom_call_target="tpu_custom_call", output_to_operand_aliasing={{3}: (5, {})} | custom-call | tf_op jit(solution)/shard_map/contrastive_head/pallas_call | solution.py:263
  (6 shorter events, 0.1 us)
Async XLA Ops:
  2.3 12.3 %collective-permute-start = (bf16[2,2,64,256]{3,2,1,0:T(8,128)(2,1)S(1)}, bf16[2,2,64,256]{3,2,1,0:T(8,128)(2,1)S(1)}, u32[]{:S(2)}, u32[]{:S(2)}) collective-permute-start(bf16[2,2,64,256]{3,2,1,0:T(8,128)(2,1)S(1)} %get-tuple-element.21), channel_id=1, source_target_pairs={{1,2},{2,1},{3,4},{4,3},{5,6},{6,5},{9,10},{10,9},{11,12},{12,11},... | collective-permute-start | bytes 393224 | tf_op jit(solution)/shard_map/ppermute | solution.py:290
  8.6 6.0 %collective-permute-start.1 = (bf16[2,2,64,256]{3,2,1,0:T(8,128)(2,1)S(1)}, bf16[2,2,64,256]{3,2,1,0:T(8,128)(2,1)S(1)}, u32[]{:S(2)}, u32[]{:S(2)}) collective-permute-start(bf16[2,2,64,256]{3,2,1,0:T(8,128)(2,1)S(1)} %get-tuple-element.22), channel_id=1, source_target_pairs={{0,1},{1,0},{2,3},{3,2},{4,5},{5,4},{6,7},{7,6},{8,9},{9,8},{10,11... | collective-permute-start | bytes 393224 | tf_op jit(solution)/shard_map/ppermute | solution.py:291
